TPU v7x, 32 devices: a whole 2x2x4 slice. The times are simulated.
32 devices in a mesh: expert: 8 (over y, x, core), tensor: 4 (over z).
Axes of the slice: x: 2, y: 2, z: 4, core: 2. Of those that a mesh axis runs over, the one named last changes fastest.
Arguments:
- tokens: bfloat16 [8192, 1024], P('expert'), may hold values from -6 to 6
- cotangent: bfloat16 [8192, 1024], P('expert'), may hold values from -6 to 6
- routes: int32 [8192], P('expert'), may hold values from 0 to 15, as said below
- slot_index: int32 [8192], P('expert'), may hold values from 0 to 128, as said below
- first_gain: float32 [1024], replicated, may hold values from 0.1 to 1.9
- first_shift: float32 [1024], replicated, may hold values from -1.25 to 1.25
- project_in: bfloat16 [1024, 3, 1024], P(None, None, 'tensor'), may hold values from -0.25 to 0.25
- project_out: bfloat16 [1024, 1024], P('tensor'), may hold values from -1.5 to 1.5
- second_gain: float32 [1024], replicated, may hold values from 0.1 to 1.9
- second_shift: float32 [1024], replicated, may hold values from -1.25 to 1.25
- router_weight: bfloat16 [1024, 16], replicated, may hold values from -0.09375 to 0.09375
- mixing_weight: bfloat16 [1024, 2], replicated, may hold values from -0.1875 to 0.1875
- dense_up: bfloat16 [1024, 4096], P(None, 'tensor'), may hold values from -0.1875 to 0.1875
- dense_down: bfloat16 [4096, 1024], P('tensor'), may hold values from -0.1875 to 0.1875
- expert_up: bfloat16 [16, 1024, 4096], P('expert', None, 'tensor'), may hold values from -0.375 to 0.375
- expert_down: bfloat16 [16, 4096, 1024], P('expert', 'tensor'), may hold values from -3 to 3
Outputs:
- layer_out: bfloat16 [8192, 1024], P('expert')
- input_grad: bfloat16 [8192, 1024], P('expert')
- first_gain_grad: float32 [1024], replicated
- first_shift_grad: float32 [1024], replicated
- project_in_grad: float32 [1024, 3, 1024], P(None, None, 'tensor')
- project_out_grad: float32 [1024, 1024], P('tensor')
- second_gain_grad: float32 [1024], replicated
- second_shift_grad: float32 [1024], replicated
- router_grad: float32 [1024, 16], replicated
- mixing_grad: float32 [1024, 2], replicated
- dense_up_grad: float32 [1024, 4096], P(None, 'tensor')
- dense_down_grad: float32 [4096, 1024], P('tensor')
- expert_up_grad: float32 [16, 1024, 4096], P('expert', None, 'tensor')
- expert_down_grad: float32 [16, 4096, 1024], P('expert', 'tensor')
Inputs may be any that keep to these rules, and one draw needn't show every extreme that they name: `routes`: in every block of 1024 tokens (tokens b * 1024 to (b + 1) * 1024 - 1) some expert is named by more than 128 tokens. slot_index[t] is the number of earlier tokens of t's block with the same route, or 128 where that number is 128 or more (the token is dropped); so at most 128 kept tokens of a block name one expert, and every block fills all 128 slots of some expert.
All inputs are finite; a program needn't handle non-finite values.
Results may differ from a plain program's by a relative error of at most 0.023.
Values may be sent and summed in bfloat16 or wider, within the bound.
No kernel may reach another device: no remote copies, remote signals or barrier semaphores. Data moves between devices by JAX's collectives and lax.ppermute only.
A program may use at most 192 MiB of HBM per device.

v0:
```python
import jax
import jax.numpy as jnp
from jax import lax
from jax.sharding import PartitionSpec as P

HEAD_DIM = 64
SEQ = 1024


EPS = 1e-05
NEGATIVE = -1e30


def layer_norm(row_values, norm_gain, norm_shift):
    row_mean = jnp.mean(row_values, axis=-1, keepdims=True)
    centred = row_values - row_mean
    spread = jnp.mean(centred * centred, axis=-1, keepdims=True)
    return centred * lax.rsqrt(spread + EPS) * norm_gain + norm_shift


def gelu_tanh(values):
    return jax.nn.gelu(values, approximate=True)


def gelu_back(pre_act, incoming):
    return jax.vjp(gelu_tanh, pre_act)[1](incoming)[0]


def causal_scores(query_block, key_seq, offset):
    score_scale = HEAD_DIM ** (-0.5)
    scores = (
        jnp.einsum("qhd,khd->hqk", query_block, key_seq, preferred_element_type=jnp.float32)
        * score_scale
    )
    query_pos = offset + lax.iota(jnp.int32, query_block.shape[0])
    key_pos = lax.iota(jnp.int32, key_seq.shape[0])
    allowed = key_pos[None, :] <= query_pos[:, None]
    return jnp.where(allowed[None], scores, NEGATIVE)


def attend_forward(queries, key_rows, values, block_rows):
    row_count, head_count, head_width = queries.shape
    per_seq = SEQ // block_rows

    def one_block(block_index):
        seq_start = block_index // per_seq * SEQ
        offset = block_index % per_seq * block_rows
        query_block = lax.dynamic_slice_in_dim(queries, seq_start + offset, block_rows, 0)
        scores = causal_scores(query_block, key_rows, offset)
        row_max = jnp.max(scores, axis=-1, keepdims=True)
        powers = jnp.exp(scores - row_max)
        row_total = jnp.sum(powers, axis=-1, keepdims=True)
        weights = (powers / row_total).astype(jnp.bfloat16)
        blended = jnp.einsum("hqk,khd->qhd", weights, values, preferred_element_type=jnp.float32)
        return (blended.astype(jnp.bfloat16), (row_max + jnp.log(row_total))[..., 0])

    blended, log_total = lax.map(one_block, jnp.arange(row_count // block_rows, dtype=jnp.int32))
    return (blended.reshape(row_count, head_count * head_width), log_total)


def attend_backward(queries, key_rows, values, log_total, grad_blended, block_rows):
    row_count, head_count, head_width = queries.shape
    per_seq = SEQ // block_rows
    score_scale = HEAD_DIM ** (-0.5)

    def one_seq(sequence):
        seq_start = sequence * SEQ

        def step(totals, inner_index):
            key_acc, value_acc = totals
            offset = inner_index * block_rows
            query_block = lax.dynamic_slice_in_dim(queries, seq_start + offset, block_rows, 0)
            grad_block = lax.dynamic_slice_in_dim(grad_blended, seq_start + offset, block_rows, 0)
            row_log = lax.dynamic_index_in_dim(
                log_total, sequence * per_seq + inner_index, 0, keepdims=False
            )
            scores = causal_scores(query_block, key_rows, offset)
            weights = jnp.exp(scores - row_log[..., None])
            weight_grad = jnp.einsum(
                "qhd,khd->hqk", grad_block, values, preferred_element_type=jnp.float32
            )
            row_inner = jnp.sum(weights * weight_grad, axis=-1, keepdims=True)
            score_grad = (weights * (weight_grad - row_inner)).astype(jnp.bfloat16)
            query_grad = (
                jnp.einsum("hqk,khd->qhd", score_grad, key_rows, preferred_element_type=jnp.float32)
                * score_scale
            )
            key_acc = (
                key_acc
                + jnp.einsum(
                    "hqk,qhd->khd", score_grad, query_block, preferred_element_type=jnp.float32
                )
                * score_scale
            )
            value_acc = value_acc + jnp.einsum(
                "hqk,qhd->khd",
                weights.astype(jnp.bfloat16),
                grad_block,
                preferred_element_type=jnp.float32,
            )
            return ((key_acc, value_acc), query_grad)

        empty_acc = jnp.zeros((SEQ, head_count, head_width), jnp.float32)
        (key_grad, value_grad), query_grad = lax.scan(
            step, (empty_acc, empty_acc), jnp.arange(per_seq, dtype=jnp.int32)
        )
        return (query_grad.reshape(SEQ, head_count, head_width), key_grad, value_grad)

    query_grad, key_grad, value_grad = lax.map(
        one_seq, jnp.arange(row_count // SEQ, dtype=jnp.int32)
    )
    flat_width = head_count * head_width
    return jnp.stack(
        [
            query_grad.reshape(row_count, flat_width),
            key_grad.reshape(row_count, flat_width),
            value_grad.reshape(row_count, flat_width),
        ],
        axis=1,
    )


def send_home(buffer):
    return lax.all_to_all(
        buffer.astype(jnp.bfloat16), "expert", split_axis=1, concat_axis=0, tiled=True
    ).astype(buffer.dtype)


def send_grads_home(buffer):
    return lax.all_to_all(
        buffer.astype(jnp.bfloat16), "expert", split_axis=1, concat_axis=0, tiled=True
    ).astype(buffer.dtype)


def local(
    tokens,
    cotangent,
    routes,
    slot_index,
    first_gain,
    first_shift,
    project_in,
    project_out,
    second_gain,
    second_shift,
    router_weight,
    mixing_weight,
    dense_up,
    dense_down,
    expert_up,
    expert_down,
):
    inputs = tokens.astype(jnp.float32)
    cotan_rows = cotangent.astype(jnp.float32)
    row_count, model_width = inputs.shape
    expert_count = router_weight.shape[1]
    capacity = 2 * row_count // expert_count
    head_count = project_in.shape[2] // HEAD_DIM
    block_rows = min(512, SEQ)
    normed_in, first_back = jax.vjp(layer_norm, inputs, first_gain, first_shift)
    normed_low = normed_in.astype(jnp.bfloat16)
    projected = jnp.einsum(
        "td,dcn->tcn", normed_low, project_in, preferred_element_type=jnp.float32
    ).astype(jnp.bfloat16)
    queries = projected[:, 0].reshape(row_count, head_count, HEAD_DIM)
    key_rows = projected[:, 1].reshape(row_count, head_count, HEAD_DIM)
    values = projected[:, 2].reshape(row_count, head_count, HEAD_DIM)
    attended, log_total = attend_forward(queries, key_rows, values, block_rows)
    attn_part = jnp.dot(attended, project_out, preferred_element_type=jnp.float32)
    attn_full = lax.psum(attn_part, "tensor")
    residual = inputs + attn_full
    normed_mid, second_back = jax.vjp(layer_norm, residual, second_gain, second_shift)
    mid_low = normed_mid.astype(jnp.bfloat16)
    router_logits = jnp.dot(mid_low, router_weight, preferred_element_type=jnp.float32)
    mixing_logits = jnp.dot(mid_low, mixing_weight, preferred_element_type=jnp.float32)
    chosen = routes[:, None] == lax.iota(jnp.int32, expert_count)[None, :]

    def gating(route_logits, mix_logits):
        router_probs = jax.nn.softmax(route_logits, axis=-1)
        return (
            jnp.sum(jnp.where(chosen, router_probs, 0.0), axis=-1),
            jax.nn.softmax(mix_logits, axis=-1),
        )

    (gate_value, mixing), gating_back = jax.vjp(gating, router_logits, mixing_logits)
    slot_total = expert_count * capacity
    slot_place = jnp.where(slot_index < capacity, routes * capacity + slot_index, slot_total)
    holder = (
        jnp.full((slot_total,), row_count, jnp.int32)
        .at[slot_place]
        .set(lax.iota(jnp.int32, row_count), mode="drop")
    )

    def to_slots(row_values):
        taken = jnp.take(row_values, holder, axis=0, mode="fill", fill_value=0)
        return taken.reshape(expert_count, capacity, row_values.shape[1])

    def from_slots(buffer):
        return jnp.take(
            buffer.reshape(slot_total, buffer.shape[-1]),
            slot_place,
            axis=0,
            mode="fill",
            fill_value=0,
        )

    arrived = lax.all_to_all(to_slots(mid_low), "expert", split_axis=0, concat_axis=1, tiled=True)
    expert_pre = jnp.einsum("erd,edf->erf", arrived, expert_up, preferred_element_type=jnp.float32)
    expert_hidden = gelu_tanh(expert_pre).astype(jnp.bfloat16)
    expert_part = jnp.einsum(
        "erf,efd->erd", expert_hidden, expert_down, preferred_element_type=jnp.float32
    )
    dense_pre = jnp.dot(mid_low, dense_up, preferred_element_type=jnp.float32)
    dense_hidden = gelu_tanh(dense_pre).astype(jnp.bfloat16)
    dense_part = jnp.dot(dense_hidden, dense_down, preferred_element_type=jnp.float32)
    dense_weight = mixing[:, 0:1]
    expert_weight = (mixing[:, 1] * gate_value)[:, None]
    dense_full, expert_full = (
        lax.psum(dense_part.astype(jnp.bfloat16), "tensor").astype(jnp.float32),
        lax.psum(expert_part.astype(jnp.bfloat16), "tensor").astype(jnp.float32),
    )
    expert_tok = from_slots(send_home(expert_full))
    layer_out = residual + dense_weight * dense_full + expert_weight * expert_tok
    dense_dot = jnp.sum(cotan_rows * dense_full, axis=-1)
    expert_dot = jnp.sum(cotan_rows * expert_tok, axis=-1)
    dense_out_grad = (cotan_rows * dense_weight).astype(jnp.bfloat16)
    expert_tok_grad = (cotan_rows * expert_weight).astype(jnp.bfloat16)
    mixing_dots = jnp.stack([dense_dot, gate_value * expert_dot], axis=-1)
    gate_grad = mixing[:, 1] * expert_dot
    router_logit_grad, mixing_logit_grad = gating_back((gate_grad, mixing_dots))
    router_low = router_logit_grad.astype(jnp.bfloat16)
    mixing_low = mixing_logit_grad.astype(jnp.bfloat16)
    router_grad = jnp.einsum("td,te->de", mid_low, router_low, preferred_element_type=jnp.float32)
    mixing_grad = jnp.einsum("td,te->de", mid_low, mixing_low, preferred_element_type=jnp.float32)
    mid_from_gates = jnp.einsum(
        "te,de->td", router_low, router_weight, preferred_element_type=jnp.float32
    ) + jnp.einsum("te,de->td", mixing_low, mixing_weight, preferred_element_type=jnp.float32)
    dense_down_grad = jnp.einsum(
        "tf,td->fd", dense_hidden, dense_out_grad, preferred_element_type=jnp.float32
    )
    dense_hidden_grad = jnp.einsum(
        "td,fd->tf", dense_out_grad, dense_down, preferred_element_type=jnp.float32
    )
    dense_pre_grad = gelu_back(dense_pre, dense_hidden_grad).astype(jnp.bfloat16)
    dense_up_grad = jnp.einsum(
        "td,tf->df", mid_low, dense_pre_grad, preferred_element_type=jnp.float32
    )
    mid_dense_part = jnp.einsum(
        "tf,df->td", dense_pre_grad, dense_up, preferred_element_type=jnp.float32
    )
    grad_arrived = lax.all_to_all(
        to_slots(expert_tok_grad), "expert", split_axis=0, concat_axis=1, tiled=True
    )
    expert_down_grad = jnp.einsum(
        "erf,erd->efd", expert_hidden, grad_arrived, preferred_element_type=jnp.float32
    )
    expert_hidden_grad = jnp.einsum(
        "erd,efd->erf", grad_arrived, expert_down, preferred_element_type=jnp.float32
    )
    expert_pre_grad = gelu_back(expert_pre, expert_hidden_grad).astype(jnp.bfloat16)
    expert_up_grad = jnp.einsum(
        "erd,erf->edf", arrived, expert_pre_grad, preferred_element_type=jnp.float32
    )
    arrived_grad = jnp.einsum(
        "erf,edf->erd", expert_pre_grad, expert_up, preferred_element_type=jnp.float32
    )
    mid_dense, arrived_full = (
        lax.psum(mid_dense_part.astype(jnp.bfloat16), "tensor").astype(jnp.float32),
        lax.psum(arrived_grad.astype(jnp.bfloat16), "tensor").astype(jnp.float32),
    )
    mid_grad = mid_dense + from_slots(send_grads_home(arrived_full)) + mid_from_gates
    resid_from_mid, second_gain_grad, second_shift_grad = second_back(mid_grad)
    residual_grad = cotan_rows + resid_from_mid
    attn_grad_low = residual_grad.astype(jnp.bfloat16)
    project_out_grad = jnp.einsum(
        "tn,td->nd", attended, attn_grad_low, preferred_element_type=jnp.float32
    )
    attended_grad = jnp.einsum(
        "td,nd->tn", attn_grad_low, project_out, preferred_element_type=jnp.float32
    ).astype(jnp.bfloat16)
    qkv_grad = attend_backward(
        queries,
        key_rows,
        values,
        log_total,
        attended_grad.reshape(row_count, head_count, HEAD_DIM),
        block_rows,
    ).astype(jnp.bfloat16)
    project_in_grad = jnp.einsum(
        "td,tcn->dcn", normed_low, qkv_grad, preferred_element_type=jnp.float32
    )
    normed_part = jnp.einsum(
        "tcn,dcn->td", qkv_grad, project_in, preferred_element_type=jnp.float32
    )
    normed_grad = lax.psum(normed_part.astype(jnp.bfloat16), "tensor").astype(jnp.float32)
    input_from_norm, first_gain_grad, first_shift_grad = first_back(normed_grad)
    input_grad = (residual_grad + input_from_norm).astype(jnp.bfloat16)
    (
        router_grad,
        mixing_grad,
        dense_up_grad,
        dense_down_grad,
        second_gain_grad,
        second_shift_grad,
        project_out_grad,
        project_in_grad,
        first_gain_grad,
        first_shift_grad,
    ) = (
        lax.psum(router_grad.astype(jnp.bfloat16), "expert").astype(jnp.float32),
        lax.psum(mixing_grad.astype(jnp.bfloat16), "expert").astype(jnp.float32),
        lax.psum(dense_up_grad.astype(jnp.bfloat16), "expert").astype(jnp.float32),
        lax.psum(dense_down_grad.astype(jnp.bfloat16), "expert").astype(jnp.float32),
        lax.psum(second_gain_grad.astype(jnp.bfloat16), "expert").astype(jnp.float32),
        lax.psum(second_shift_grad.astype(jnp.bfloat16), "expert").astype(jnp.float32),
        lax.psum(project_out_grad.astype(jnp.bfloat16), "expert").astype(jnp.float32),
        lax.psum(project_in_grad.astype(jnp.bfloat16), "expert").astype(jnp.float32),
        lax.psum(first_gain_grad.astype(jnp.bfloat16), "expert").astype(jnp.float32),
        lax.psum(first_shift_grad.astype(jnp.bfloat16), "expert").astype(jnp.float32),
    )
    return (
        layer_out.astype(jnp.bfloat16),
        input_grad,
        first_gain_grad,
        first_shift_grad,
        project_in_grad,
        project_out_grad,
        second_gain_grad,
        second_shift_grad,
        router_grad,
        mixing_grad,
        dense_up_grad,
        dense_down_grad,
        expert_up_grad,
        expert_down_grad,
    )


def solution(mesh):
    placed = (
        P("expert", None),
        P("expert", None),
        P("expert"),
        P("expert"),
        P(),
        P(),
        P(None, None, "tensor"),
        P("tensor", None),
        P(),
        P(),
        P(),
        P(),
        P(None, "tensor"),
        P("tensor", None),
        P("expert", None, "tensor"),
        P("expert", "tensor", None),
    )
    return jax.shard_map(
        local,
        mesh=mesh,
        in_specs=placed,
        out_specs=(
            P("expert", None),
            P("expert", None),
            P(),
            P(),
            P(None, None, "tensor"),
            P("tensor", None),
            P(),
            P(),
            P(),
            P(),
            P(None, "tensor"),
            P("tensor", None),
            P("expert", None, "tensor"),
            P("expert", "tensor", None),
        ),
        check_vma=False,
    )
```

profile of v0, /device:TPU:0, one launch (start us, length us, event | category | flops | bytes accessed | tf_op | source)
XLA Modules:
  0.0 1272.5 jit_solution(15387023293925295045)
XLA Ops:
  16.1 23.0 %while.43 = (s32[]{:T(128)}, bf16[2,512,4,64]{1,3,2,0:T(8,128)(2,1)}, f32[2,4,512]{2,1,0:T(4,128)S(1)}, s32[2]{0:T(128)S(1)}, bf16[1024,4,64]{0,2,1:T(8,128)(2,1...) while((s32[]{:T(128)}, ...), condition=%wide.region_5.6_spmd, body=%wide.region_2.5_spmd.sunk | while | flops 562690560 | bytes 35197428 | solution.py:57
  46.4 4.8 scatter_custom_fusion
  51.2 152.4 %all-reduce.10.cloned.1.call-done = f32[1024,1024]{1,0:T(8,128)} async-done(((f32[1024,1024]{1,0:T(8,128)}), f32[1024,1024]{1,0:T(8,128)}) %all-reduce.10.cloned.1.call-update) | async-done | bytes 4194320 | tf_op jit(solution)/shard_map/psum | solution.py:170
  211.6 12.8 %gather_fusion = bf16[2048,1024]{1,0:T(8,128)(2,1)} fusion(bf16[1024,1024]{1,0:T(8,128)(2,1)} %add_convert_fusion.1, s32[2048]{0:T(1024)S(1)} %fusion.86), kind=kCustom, calls=%fused_computation.clone | custom fusion | bytes 8396800 | tf_op jit(solution)/shard_map/jit(_take)/gather | solution.py:195
  243.4 38.5 %all-to-all-done = bf16[16,128,1024]{2,1,0:T(8,128)(2,1)} async-done(((bf16[16,128,1024]{2,1,0:T(8,128)(2,1)}), bf16[16,128,1024]{2,1,0:T(8,128)(2,1)}, u32[]{:S(2)}, u32[]{:S(2)}) %all-to-all-start) | async-done | bytes 4194336 | tf_op jit(solution)/shard_map/all_to_all | solution.py:207
  294.6 6.8 convolution_convert_fusion.1
  301.4 220.2 %all-reduce.18.cloned.1.call-done = (bf16[1024,1024]{1,0:T(8,128)(2,1)}, bf16[2,1024,1024]{2,1,0:T(8,128)(2,1)}) async-done(((bf16[1024,1024]{1,0:T(8,128)(2,1)}, bf16[2,1024,1024]{2,1,0:T(8,128)(2,1)}), (bf16[1024,1024]{1,0:T(8,128)(2,1)}, bf16[2,1024,1024]{2,1,0:T(8,128)(2,1)})) %all-reduce.18.cloned.1.call-update) | async-done | bytes 6291472 | tf_op jit(solution)/shard_map/psum | solution.py:219
  521.6 8.5 copy.55
  530.1 4.7 all-to-all-start.1
  539.5 44.4 %all-to-all-done.1 = bf16[2,1024,1024]{2,0,1:T(2,128)(2,1)} async-done(((bf16[2,1024,1024]{2,0,1:T(2,128)(2,1)}), bf16[2,1024,1024]{2,0,1:T(2,128)(2,1)}, u32[]{:S(2)}, u32[]{:S(2)}) %all-to-all-start.1) | async-done | bytes 4194336 | tf_op jit(solution)/shard_map/all_to_all | solution.py:124
  583.9 7.1 copy.56
  591.1 9.7 gather_fusion.1
  607.2 12.8 %gather_fusion.2 = bf16[2048,1024]{1,0:T(8,128)(2,1)} fusion(bf16[1024,1024]{1,0:T(8,128)(2,1)} %fusion.66, s32[2048]{0:T(1024)S(1)} %fusion.86), kind=kCustom, calls=%fused_computation.2.clone | custom fusion | bytes 8396800 | tf_op jit(solution)/shard_map/jit(_take)/gather | solution.py:195
  628.4 7.4 fusion.62
  640.9 36.5 %all-to-all-done.2 = bf16[16,128,1024]{2,1,0:T(8,128)(2,1)} async-done(((bf16[16,128,1024]{2,1,0:T(8,128)(2,1)}), bf16[16,128,1024]{2,1,0:T(8,128)(2,1)}, u32[]{:S(2)}, u32[]{:S(2)}) %all-to-all-start.2) | async-done | bytes 4194336 | tf_op jit(solution)/shard_map/all_to_all | solution.py:251
  680.9 12.1 fusion.43
  695.0 6.5 convolution_convert_fusion
  701.5 220.2 %all-reduce.16.cloned.1.call-done = (bf16[2,1024,1024]{2,1,0:T(8,128)(2,1)}, bf16[1024,1024]{1,0:T(8,128)(2,1)}) async-done(((bf16[2,1024,1024]{2,1,0:T(8,128)(2,1)}, bf16[1024,1024]{1,0:T(8,128)(2,1)}), (bf16[2,1024,1024]{2,1,0:T(8,128)(2,1)}, bf16[1024,1024]{1,0:T(8,128)(2,1)})) %all-reduce.16.cloned.1.call-update) | async-done | bytes 6291472 | tf_op jit(solution)/shard_map/psum | solution.py:269
  921.7 8.5 copy.58
  939.8 44.2 %all-to-all-done.3 = bf16[2,1024,1024]{2,0,1:T(2,128)(2,1)} async-done(((bf16[2,1024,1024]{2,0,1:T(2,128)(2,1)}), bf16[2,1024,1024]{2,0,1:T(2,128)(2,1)}, u32[]{:S(2)}, u32[]{:S(2)}) %all-to-all-start.3) | async-done | bytes 4194336 | tf_op jit(solution)/shard_map/all_to_all | solution.py:130
  984.0 7.1 copy.59
  991.1 9.8 gather_fusion.3
  1000.9 7.5 multiply_reduce_fusion.1
  1016.9 33.1 %while.44 = (s32[]{:T(128)}, f32[1024,4,64]{0,2,1:T(8,128)}, f32[1024,4,64]{0,2,1:T(8,128)}, bf16[2,512,4,64]{1,3,2,0:T(8,128)(2,1)}, s32[2]{0:T(128)S(1)}, /*in...) while((s32[]{:T(128)}, f32[1024,4,64]{0,2,1:T(8,128)}, ...), condition=%wide.region_27.30_spmd.clone, body=%wide.region_25.29_spmd.clone.sunk | while | flops 1375599104 | bytes 97579512 | solution.py:104
  1057.7 4.9 bitcast_convert_fusion
  1062.9 5.5 convolution_convert_fusion.3
  1077.8 13.7 %fusion.97 = f32[2,1024,1024]{2,1,0:T(8,128)} fusion(bf16[2,1024,1024]{2,1,0:T(8,128)(2,1)} %bitcast.152, f32[2,1024,1024]{2,1,0:T(8,128)} %copy-done.81), kind=kOutput, calls=%fused_computation.170 | convolution fusion | flops 4313841664 | bytes 20971520 | tf_op jit(solution)/shard_map/erf,erd->efd/dot_general | solution.py:254
  1091.6 6.9 fusion.107
  1098.5 47.6 %all-reduce.12.cloned.1.call-done = bf16[1024,1024]{1,0:T(8,128)(2,1)} async-done(((bf16[1024,1024]{1,0:T(8,128)(2,1)}), bf16[1024,1024]{1,0:T(8,128)(2,1)}) %all-reduce.12.cloned.1.call-update) | async-done | bytes 2097168 | tf_op jit(solution)/shard_map/psum | solution.py:295
  1153.6 26.6 %all-reduce = (bf16[1024]{0:T(1024)(128)(2,1)S(1)}, bf16[1024]{0:T(1024)(128)(2,1)S(1)}, bf16[1024]{0:T(1024)(128)(2,1)S(1)}, bf16[1024]{0:T(1024)(128)(2,1)S(1)...) all-reduce(bf16[1024]{0:T(1024)(128)(2,1)S(1)} %get-tuple-element.3, ...), channel_id=1, replica_groups=mesh['expert'=8,'tensor'=4] {'expert'}, use_global_device_ids=true, to_apply=%region_32.35 | all-reduce | flops 22528 | bytes 90112 | tf_op jit(solution)/shard_map/psum | solution.py:318
  1183.8 5.5 add_convert_fusion
  1189.3 65.5 %all-reduce.14.cloned.1.call-done = (bf16[1024,3,256]{2,0,1:T(8,128)(2,1)}, bf16[256,1024]{1,0:T(8,128)(2,1)}, bf16[1024,1024]{1,0:T(8,128)(2,1)}, bf16[1024,1024]{1,0:T(8,128)(2,1)}) async-done(((bf16[1024,3,256]{2,0,1:T(8,128)(2,1)}, bf16[256,1024]{1,0:T(8,128)(2,1)}, bf16[1024,1024]{1,0:T(8,128)(2,1)}, bf16[1024,1024]{1,0:T(8,128)(2,1)}), (bf16[1024,3,256]{2,0,1:T(8,128)(2,1)}, ...) | async-done | bytes 6291472 | tf_op jit(solution)/shard_map/psum | solution.py:317
  (321 shorter events, 187.7 us)
Async XLA Ops:
  7.2 232.2 %copy-start = (bf16[1024,1024]{1,0:T(8,128)(2,1)S(1)}, bf16[1024,1024]{1,0:T(8,128)(2,1)}, u32[]{:S(2)}) copy-start(bf16[1024,1024]{1,0:T(8,128)(2,1)} %param.37) | copy-start | bytes 6291460
  7.2 196.4 %all-reduce.10.cloned.1.call-start = ((), (), s32[]{:S(2)}) async-start(), calls=%async_computation.4 | async-start | bytes 8388608 | tf_op jit(solution)/shard_map/psum | solution.py:170
  39.0 6.6 copy-start.3
  39.1 6.6 copy-start.11
  39.1 6.6 copy-start.46
  207.6 16.8 %copy-start.63 = (f32[1024]{0:T(1024)}, f32[1024]{0:T(1024)S(1)}, u32[]{:S(2)}) copy-start(f32[1024]{0:T(1024)S(1)} %multiply_reduce_fusion.3) | copy-start | bytes 12292
  228.2 53.7 %all-to-all-start = ((bf16[16,128,1024]{2,1,0:T(8,128)(2,1)}), bf16[16,128,1024]{2,1,0:T(8,128)(2,1)}, u32[]{:S(2)}, u32[]{:S(2)}) async-start(bf16[16,128,1024]{2,1,0:T(8,128)(2,1)} %bitcast.148), calls=%async_computation | async-start | bytes 8388608 | tf_op jit(solution)/shard_map/all_to_all | solution.py:207
  232.8 288.8 %all-reduce.18.cloned.1.call-start = ((), (), s32[]{:S(2)}) async-start(), calls=%async_computation.8 | async-start | bytes 12582912 | tf_op jit(solution)/shard_map/psum | solution.py:219
  286.7 7.9 copy-start.71
  530.1 7.1 copy-start.42
  530.1 53.8 %all-to-all-start.1 = ((bf16[2,1024,1024]{2,0,1:T(2,128)(2,1)}), bf16[2,1024,1024]{2,0,1:T(2,128)(2,1)}, u32[]{:S(2)}, u32[]{:S(2)}) async-start(bf16[2,1024,1024]{2,0,1:T(2,128)(2,1)} %copy.55), calls=%async_computation.1 | async-start | bytes 8388608 | tf_op jit(solution)/shard_map/all_to_all | solution.py:124
  623.8 53.7 %all-to-all-start.2 = ((bf16[16,128,1024]{2,1,0:T(8,128)(2,1)}), bf16[16,128,1024]{2,1,0:T(8,128)(2,1)}, u32[]{:S(2)}, u32[]{:S(2)}) async-start(bf16[16,128,1024]{2,1,0:T(8,128)(2,1)} %bitcast.147), calls=%async_computation.2 | async-start | bytes 8388608 | tf_op jit(solution)/shard_map/all_to_all | solution.py:251
  628.4 293.3 %all-reduce.16.cloned.1.call-start = ((), (), s32[]{:S(2)}) async-start(), calls=%async_computation.7 | async-start | bytes 12582912 | tf_op jit(solution)/shard_map/psum | solution.py:269
  628.4 8.8 copy-start.75
  680.3 12.7 copy-start.24
  680.9 14.1 %copy-start.74 = (bf16[2,1024,1024]{2,1,0:T(8,128)(2,1)S(1)}, bf16[2,1024,1024]{2,1,0:T(8,128)(2,1)}, u32[]{:S(2)}) copy-start(bf16[2,1024,1024]{2,1,0:T(8,128)(2,1)} %param.38) | copy-start | bytes 12582916
  930.2 53.8 %all-to-all-start.3 = ((bf16[2,1024,1024]{2,0,1:T(2,128)(2,1)}), bf16[2,1024,1024]{2,0,1:T(2,128)(2,1)}, u32[]{:S(2)}, u32[]{:S(2)}) async-start(bf16[2,1024,1024]{2,0,1:T(2,128)(2,1)} %copy.58), calls=%async_computation.3 | async-start | bytes 8388608 | tf_op jit(solution)/shard_map/all_to_all | solution.py:130
  934.9 211.2 %all-reduce.12.cloned.1.call-start = ((), (), s32[]{:S(2)}) async-start(), calls=%async_computation.5 | async-start | bytes 4194304 | tf_op jit(solution)/shard_map/psum | solution.py:295
  991.1 9.8 copy-start.49
  991.1 9.8 copy-start.51
  991.1 9.8 copy-start.54
  1000.9 7.6 copy-start.64
  1000.9 7.6 copy-start.6
  1000.9 7.7 copy-start.13
  1000.9 8.3 copy-start.21
  1062.6 192.2 %all-reduce.14.cloned.1.call-start = ((), (), s32[]{:S(2)}) async-start(), calls=%async_computation.6 | async-start | bytes 12582912 | tf_op jit(solution)/shard_map/psum | solution.py:317
  1068.4 6.0 copy-start.10
  1068.4 6.0 copy-start.38
  1077.8 13.7 %copy-start.23 = (bf16[2,8,128,1024]{3,2,1,0:T(8,128)(2,1)S(1)}, bf16[2,8,128,1024]{3,2,1,0:T(8,128)(2,1)}, u32[]{:S(2)}) copy-start(bf16[2,8,128,1024]{3,2,1,0:T(8,128)(2,1)} %copy-done.22) | copy-start | bytes 12582916
  1077.8 13.7 %copy-start.83 = (bf16[2,1024,1024]{2,1,0:T(8,128)(2,1)S(1)}, bf16[2,1024,1024]{2,1,0:T(8,128)(2,1)}, u32[]{:S(2)}) copy-start(bf16[2,1024,1024]{2,1,0:T(8,128)(2,1)} %copy-done.82) | copy-start | bytes 12582916
  1098.5 52.3 %copy-start.62 = (f32[1024]{0:T(1024)S(1)}, f32[1024]{0:T(1024)}, u32[]{:S(2)}) copy-start(f32[1024]{0:T(1024)} %copy-done.61) | copy-start | bytes 12292
  1148.1 35.8 %copy-start.60 = (f32[1024]{0:T(1024)S(1)}, f32[1024]{0:T(1024)}, u32[]{:S(2)}) copy-start(f32[1024]{0:T(1024)} %copy-done.59) | copy-start | bytes 12292
  (73 other events, 224.1 us)
Sparse Core Ops, SparseCore 0:
  45.9 157.6 all-reduce.9
  301.5 220.0 all-reduce.17
  701.6 219.9 all-reduce.15
  1062.7 83.2 all-reduce.11
  1150.6 104.1 all-reduce.13
where the time goes:
time: 1280 us; the launch traced here: 1270 us
  waiting for transfers between devices  869 us (68%)
  matrix products  142 us (11%)
  local copies, waits for them, and re-layouts  120 us (9%)
  other arithmetic  69.5 us (5%)
  blocking collectives  26.6 us (2%)
  starting transfers between devices  19 us (1%)
  between operations  15.2 us (1%)
    psum x1, waiting for transfers between devices, local(): lax.psum(dense_part.astype(jnp.bfloat16), 'tensor').astype(jnp.float32)  220 us
    psum x1, waiting for transfers between devices, local(): lax.psum(arrived_grad.astype(jnp.bfloat16), 'tensor').astype(jnp.float32)  220 us
    psum x1, waiting for transfers between devices, local(): attn_full = lax.psum(attn_part, 'tensor')  152 us
    psum x1, waiting for transfers between devices, local(): lax.psum(project_in_grad.astype(jnp.bfloat16), 'expert').astype(jnp.float32)  65.5 us
    psum x1, waiting for transfers between devices, local(): lax.psum(normed_part.astype(jnp.bfloat16), 'tensor').astype(jnp.float32)  47.6 us
    all_to_all x1, waiting for transfers between devices, send_home(): lax.all_to_all(buffer.astype(jnp.bfloat16), 'expert', split_axis=1, conca...  44.4 us
    all_to_all x1, waiting for transfers between devices, send_grads_home(): lax.all_to_all(buffer.astype(jnp.bfloat16), 'expert', split_axis=1, conca...  44.2 us
    all_to_all x1, waiting for transfers between devices, local(): lax.all_to_all(to_slots(mid_low), 'expert', split_axis=0, concat_axis=1,...  38.5 us
  transfers between devices with their start and end apart: 9, of which 9 were waited for; matrix products, arithmetic and copies ran while one was open for 7% of the time, Pallas kernels for 0%

commit v1 on v0

v1 whole, which is shorter than its diff:
```python
import functools

import jax
import jax.numpy as jnp
from jax import lax
from jax.experimental import pallas as pl
from jax.experimental.pallas import tpu as pltpu
from jax.sharding import PartitionSpec as P

HEAD_DIM = 64
EPS = 1e-05
NEGATIVE = -1e30
BF = jnp.bfloat16
F32 = jnp.float32


def norm_stats(rows):
    row_mean = jnp.mean(rows, axis=-1, keepdims=True)
    centred = rows - row_mean
    spread = jnp.mean(centred * centred, axis=-1, keepdims=True)
    inverse = lax.rsqrt(spread + EPS)
    return centred * inverse, inverse


def norm_back(unit, inverse, gain, grad):
    weighted = grad * gain
    first = jnp.mean(weighted, axis=-1, keepdims=True)
    second = jnp.mean(weighted * unit, axis=-1, keepdims=True)
    return inverse * (weighted - first - unit * second)


def gelu_both(v):
    inner = 0.7978845608 * (v + 0.044715 * v * v * v)
    bent = jnp.tanh(inner)
    value = 0.5 * v * (1.0 + bent)
    slope = 0.5 * (1.0 + bent) + 0.5 * v * (1.0 - bent * bent) * 0.7978845608 * (
        1.0 + 3.0 * 0.044715 * v * v
    )
    return value, slope


def t_dot(a, b):
    return lax.dot_general(a, b, (((0,), (0,)), ((), ())), preferred_element_type=F32)


def after(value, *others):
    return lax.optimization_barrier((value,) + others)[0]


def dot(a, b):
    return jnp.dot(a, b, preferred_element_type=F32)

def dot_t(a, b):
    return lax.dot_general(a, b, (((1,), (1,)), ((), ())), preferred_element_type=F32)

def head_lanes(head, rows):
    lanes = lax.broadcasted_iota(jnp.int32, (rows, 2 * HEAD_DIM), 1)
    return (lanes < HEAD_DIM) if head == 0 else (lanes >= HEAD_DIM)

def keep_causal(scores, tile):
    keys = scores.shape[0]
    key_pos = lax.broadcasted_iota(jnp.int32, (tile, tile), 0)
    query_pos = lax.broadcasted_iota(jnp.int32, (tile, tile), 1)
    last = jnp.where(key_pos <= query_pos, scores[keys - tile :], NEGATIVE)
    if keys == tile:
        return last
    return jnp.concatenate([scores[: keys - tile], last], axis=0)

def attend_forward_kernel(tile, qkv_ref, out_ref, log_ref):
    rows = qkv_ref.shape[1]
    values_t = jnp.transpose(qkv_ref[2])
    for block in range(rows // tile):
        keys = (block + 1) * tile
        here = pl.ds(block * tile, tile)
        query_block = qkv_ref[0, here, :]
        pieces, logs = [], []
        for head in range(2):
            q = jnp.where(head_lanes(head, tile), query_block, jnp.zeros_like(query_block))
            scores = dot_t(qkv_ref[1, :keys, :], q) * (HEAD_DIM ** (-0.5))
            scores = keep_causal(scores, tile)
            top = jnp.max(scores, axis=0, keepdims=True)
            powers = jnp.exp(scores - top)
            total = jnp.sum(powers, axis=0, keepdims=True)
            blended = dot(values_t[head * HEAD_DIM : (head + 1) * HEAD_DIM, :keys], powers.astype(BF))
            pieces.append(blended / total)
            logs.append(top + jnp.log(total))
        out_ref[here, :] = jnp.transpose(jnp.concatenate(pieces, axis=0)).astype(BF)
        for head in range(2):
            log_ref[0, head : head + 1, here] = logs[head]

def attend_backward_kernel(tile, qkv_ref, log_ref, grad_ref, out_ref, key_acc, value_acc):
    rows = qkv_ref.shape[1]
    scale = HEAD_DIM ** (-0.5)
    keys_t = jnp.transpose(qkv_ref[1])
    count = rows // tile
    for block in reversed(range(count)):
        keys = (block + 1) * tile
        here = pl.ds(block * tile, tile)
        query_block = qkv_ref[0, here, :]
        grad_block = grad_ref[here, :]
        pieces = []
        for head in range(2):
            lanes = head_lanes(head, tile)
            q = jnp.where(lanes, query_block, jnp.zeros_like(query_block))
            g = jnp.where(lanes, grad_block, jnp.zeros_like(grad_block))
            scores = dot_t(qkv_ref[1, :keys, :], q) * scale
            scores = keep_causal(scores, tile)
            weights = jnp.exp(scores - log_ref[0, head : head + 1, here])
            weight_grad = dot_t(qkv_ref[2, :keys, :], g)
            inner = jnp.sum(weights * weight_grad, axis=0, keepdims=True)
            score_grad = (weights * (weight_grad - inner)).astype(BF)
            key_step = dot(score_grad, q)
            value_step = dot(weights.astype(BF), g)
            if block == count - 1 and head == 0:
                key_acc[...] = key_step
                value_acc[...] = value_step
            else:
                key_acc[:keys, :] += key_step
                value_acc[:keys, :] += value_step
            pieces.append(dot(keys_t[head * HEAD_DIM : (head + 1) * HEAD_DIM, :keys], score_grad))
        out_ref[0, here, :] = (jnp.transpose(jnp.concatenate(pieces, axis=0)) * scale).astype(BF)
    out_ref[1] = (key_acc[...] * scale).astype(BF)
    out_ref[2] = value_acc[...].astype(BF)

def attend_forward(qkv, tile=256):
    _, rows, columns = qkv.shape
    pairs = columns // (2 * HEAD_DIM)
    return pl.pallas_call(
        functools.partial(attend_forward_kernel, tile),
        grid=(pairs,),
        out_shape=(
            jax.ShapeDtypeStruct((rows, columns), BF),
            jax.ShapeDtypeStruct((pairs, 8, rows), F32),
        ),
        in_specs=[pl.BlockSpec((3, rows, 2 * HEAD_DIM), lambda p: (0, 0, p))],
        out_specs=(
            pl.BlockSpec((rows, 2 * HEAD_DIM), lambda p: (0, p)),
            pl.BlockSpec((1, 8, rows), lambda p: (p, 0, 0)),
        ),
        cost_estimate=pl.CostEstimate(
            flops=8 * rows * rows * columns // 2, bytes_accessed=8 * rows * columns,
            transcendentals=rows * rows * columns // 128),
        name="attend_forward",
    )(qkv)

def attend_backward(qkv, logs, grads, tile=256):
    _, rows, columns = qkv.shape
    pairs = columns // (2 * HEAD_DIM)
    return pl.pallas_call(
        functools.partial(attend_backward_kernel, tile),
        grid=(pairs,),
        out_shape=jax.ShapeDtypeStruct((3, rows, columns), BF),
        in_specs=[
            pl.BlockSpec((3, rows, 2 * HEAD_DIM), lambda p: (0, 0, p)),
            pl.BlockSpec((1, 8, rows), lambda p: (p, 0, 0)),
            pl.BlockSpec((rows, 2 * HEAD_DIM), lambda p: (0, p)),
        ],
        out_specs=pl.BlockSpec((3, rows, 2 * HEAD_DIM), lambda p: (0, 0, p)),
        scratch_shapes=[pltpu.VMEM((rows, 2 * HEAD_DIM), F32)] * 2,
        cost_estimate=pl.CostEstimate(
            flops=20 * rows * rows * columns // 2, bytes_accessed=16 * rows * columns,
            transcendentals=rows * rows * columns // 128),
        name="attend_backward",
    )(qkv, logs, grads)


def project_kernel(heads_ref, weight_ref, token_ref, gain_ref, shift_ref, rest_ref, low_ref):
    total = token_ref[...].astype(F32)
    for z in range(heads_ref.shape[0]):
        total = total + dot(heads_ref[z], weight_ref[z])
    rest_ref[...] = total
    unit, _ = norm_stats(total)
    low_ref[...] = (unit * gain_ref[...] + shift_ref[...]).astype(BF)


def project_norm(heads, weight, tokens, gain, shift, tile=256):
    parts, rows, columns = heads.shape
    width = weight.shape[2]
    block = lambda i: (i, 0)
    return pl.pallas_call(
        project_kernel,
        grid=(rows // tile,),
        out_shape=(
            jax.ShapeDtypeStruct((rows, width), F32),
            jax.ShapeDtypeStruct((rows, width), BF),
        ),
        in_specs=[
            pl.BlockSpec((parts, tile, columns), lambda i: (0, i, 0)),
            pl.BlockSpec((parts, columns, width), lambda i: (0, 0, 0)),
            pl.BlockSpec((tile, width), block),
            pl.BlockSpec((1, width), lambda i: (0, 0)),
            pl.BlockSpec((1, width), lambda i: (0, 0)),
        ],
        out_specs=(pl.BlockSpec((tile, width), block), pl.BlockSpec((tile, width), block)),
        cost_estimate=pl.CostEstimate(
            flops=2 * rows * parts * columns * width,
            bytes_accessed=12 * rows * width,
            transcendentals=rows,
        ),
        name="project_norm",
    )(heads, weight, tokens, gain[None], shift[None])


def gelu_back_kernel(rows_ref, up_ref, hidden_grad_ref, hidden_ref, pre_grad_ref, in_ref, dot_ref):
    shape = rows_ref.shape
    count = shape[0] * shape[2]
    hidden, slope = gelu_both(dot(rows_ref[...].reshape(count, shape[3]), up_ref[0]))
    hidden = hidden.astype(BF)
    hidden_ref[0] = hidden
    hidden_grad = hidden_grad_ref[0].astype(F32)
    pre_grad = (hidden_grad * slope).astype(BF)
    pre_grad_ref[0] = pre_grad
    in_ref[...] = dot_t(pre_grad, up_ref[0]).astype(BF).reshape(shape)
    dots = jnp.sum(hidden.astype(F32) * hidden_grad, axis=1, keepdims=True)
    dot_ref[0] = jnp.broadcast_to(dots, (count, 128))


def expert_back(arrived, expert_up, hidden_grads, tile=512):
    blocks, held, capacity, width = arrived.shape
    rows = blocks * capacity
    units = expert_up.shape[2]
    slots = pl.BlockSpec((tile // capacity, 1, capacity, width), lambda e, i: (i, e, 0, 0))
    flat = pl.BlockSpec((1, tile, units), lambda e, i: (e, i, 0))
    return pl.pallas_call(
        gelu_back_kernel,
        grid=(held, rows // tile),
        out_shape=(
            jax.ShapeDtypeStruct((held, rows, units), BF),
            jax.ShapeDtypeStruct((held, rows, units), BF),
            jax.ShapeDtypeStruct(arrived.shape, BF),
            jax.ShapeDtypeStruct((held, rows, 128), F32),
        ),
        in_specs=[slots, pl.BlockSpec((1, width, units), lambda e, i: (e, 0, 0)), flat],
        out_specs=(flat, flat, slots, pl.BlockSpec((1, tile, 128), lambda e, i: (e, i, 0))),
        cost_estimate=pl.CostEstimate(
            flops=4 * held * rows * units * width,
            bytes_accessed=14 * held * rows * width,
            transcendentals=held * rows * units,
        ),
        name="expert_back",
    )(arrived, expert_up, hidden_grads)


def down_kernel(hidden_ref, down_ref, out_ref):
    out_ref[...] = dot(hidden_ref[0], down_ref[0]).astype(BF).reshape(out_ref.shape)


def expert_down_rows(hidden, expert_down, blocks, tile=512):
    held, rows, units = hidden.shape
    capacity = rows // blocks
    width = expert_down.shape[2]
    return pl.pallas_call(
        down_kernel,
        grid=(held, rows // tile),
        out_shape=jax.ShapeDtypeStruct((blocks, held, capacity, width), BF),
        in_specs=[
            pl.BlockSpec((1, tile, units), lambda e, i: (e, i, 0)),
            pl.BlockSpec((1, units, width), lambda e, i: (e, 0, 0)),
        ],
        out_specs=pl.BlockSpec(
            (tile // capacity, 1, capacity, width), lambda e, i: (i, e, 0, 0)
        ),
        cost_estimate=pl.CostEstimate(
            flops=2 * held * rows * units * width,
            bytes_accessed=6 * held * rows * width,
            transcendentals=0,
        ),
        name="expert_down_rows",
    )(hidden, expert_down)


def hidden_grad_kernel(grads_ref, down_ref, out_ref):
    shape = grads_ref.shape
    rows = grads_ref[...].reshape(shape[0] * shape[2], shape[3])
    out_ref[0] = dot_t(rows, down_ref[0]).astype(BF)


def expert_hidden_grad(cotan_slots, expert_down, tile=512):
    blocks, held, capacity, width = cotan_slots.shape
    rows = blocks * capacity
    units = expert_down.shape[1]
    return pl.pallas_call(
        hidden_grad_kernel,
        grid=(held, rows // tile),
        out_shape=jax.ShapeDtypeStruct((held, rows, units), BF),
        in_specs=[
            pl.BlockSpec((tile // capacity, 1, capacity, width), lambda e, i: (i, e, 0, 0)),
            pl.BlockSpec((1, units, width), lambda e, i: (e, 0, 0)),
        ],
        out_specs=pl.BlockSpec((1, tile, units), lambda e, i: (e, i, 0)),
        cost_estimate=pl.CostEstimate(
            flops=2 * held * rows * units * width,
            bytes_accessed=6 * held * rows * width,
            transcendentals=0,
        ),
        name="expert_hidden_grad",
    )(cotan_slots, expert_down)


def normed_kernel(grad_ref, weight_ref, token_ref, out_ref, sums_ref):
    total = dot_t(grad_ref[0], weight_ref[0])
    for c in range(1, grad_ref.shape[0]):
        total = total + dot_t(grad_ref[c], weight_ref[c])
    out_ref[...] = total.astype(BF)
    unit, _ = norm_stats(token_ref[...].astype(F32))

    @pl.when(pl.program_id(0) == 0)
    def _():
        sums_ref[...] = jnp.zeros_like(sums_ref)

    sums_ref[0:1, :] += jnp.sum(total * unit, axis=0, keepdims=True)
    sums_ref[1:2, :] += jnp.sum(total, axis=0, keepdims=True)


def normed_back(qkv_grad, project_in, tokens, tile=256):
    count, rows, columns = qkv_grad.shape
    width = project_in.shape[1]
    return pl.pallas_call(
        normed_kernel,
        grid=(rows // tile,),
        out_shape=(
            jax.ShapeDtypeStruct((rows, width), BF),
            jax.ShapeDtypeStruct((8, width), F32),
        ),
        in_specs=[
            pl.BlockSpec((count, tile, columns), lambda i: (0, i, 0)),
            pl.BlockSpec((count, width, columns), lambda i: (0, 0, 0)),
            pl.BlockSpec((tile, width), lambda i: (i, 0)),
        ],
        out_specs=(
            pl.BlockSpec((tile, width), lambda i: (i, 0)),
            pl.BlockSpec((8, width), lambda i: (0, 0)),
        ),
        cost_estimate=pl.CostEstimate(
            flops=2 * count * rows * columns * width,
            bytes_accessed=6 * rows * width,
            transcendentals=rows,
        ),
        name="normed_back",
    )(qkv_grad, project_in, tokens)


def local(
    tokens,
    cotangent,
    routes,
    slot_index,
    first_gain,
    first_shift,
    project_in,
    project_out,
    second_gain,
    second_shift,
    router_weight,
    mixing_weight,
    dense_up,
    dense_down,
    expert_up,
    expert_down,
):
    row_count, width = tokens.shape
    expert_count = router_weight.shape[1]
    capacity = 2 * row_count // expert_count
    held = expert_up.shape[0]
    blocks = expert_count // held
    slot_total = expert_count * capacity
    head_columns = project_in.shape[2]
    parts = lax.axis_size("tensor")
    part_rows = row_count // parts
    my_start = lax.axis_index("tensor") * part_rows

    def mine(rows, axis=0):
        return lax.dynamic_slice_in_dim(rows, my_start, part_rows, axis)

    half = head_columns // 2
    odd = lax.axis_index("expert") % 2
    own_half = lax.all_gather(
        lax.dynamic_slice_in_dim(project_out, odd * half, half, 0), "tensor", axis=0
    )
    project_in = jnp.swapaxes(project_in, 0, 1)
    unit_in, _ = norm_stats(tokens.astype(F32))
    normed_low = (unit_in * first_gain + first_shift).astype(BF)
    qkv = jnp.einsum("td,cdn->ctn", normed_low, project_in, preferred_element_type=F32).astype(BF)
    attended, log_total = attend_forward(qkv)
    attended, own_half = lax.optimization_barrier((attended, own_half))
    attended_all = lax.all_gather(attended, "tensor", axis=0, tiled=True).reshape(
        parts, row_count, head_columns
    )

    swap = [(i, i ^ 1) for i in range(lax.axis_size("expert"))]
    other_half = lax.ppermute(own_half, "expert", swap)
    project_out_all = jnp.concatenate(
        [
            jnp.where(odd == 0, own_half, other_half),
            jnp.where(odd == 0, other_half, own_half),
        ],
        axis=1,
    )

    slot_place = jnp.where(slot_index < capacity, routes * capacity + slot_index, slot_total)
    slot_place = after(slot_place, attended)
    hit = lax.iota(jnp.int32, slot_total)[:, None] == slot_place[None, :]
    pick = hit.astype(BF)

    def to_slots(rows):
        return dot(pick, rows).astype(BF).reshape(blocks, held * capacity, width)

    def exchange(buffer):
        return lax.all_to_all(buffer, "expert", 0, 0, tiled=True)

    def from_slots(buffer):
        return t_dot(pick, buffer.reshape(slot_total, width))

    cotan_slots = exchange(to_slots(cotangent)).reshape(blocks, held, capacity, width)

    residual, mid_low = project_norm(
        attended_all, project_out_all, tokens, second_gain, second_shift
    )
    mid_slots = after(to_slots(mid_low), cotan_slots)
    arrived = exchange(mid_slots).reshape(blocks, held, capacity, width)
    mid_low = after(mid_low, mid_slots)
    router_logits = dot(mid_low, router_weight)
    mixing_logits = dot(mid_low, mixing_weight)
    router_probs = jax.nn.softmax(router_logits, axis=-1)
    mixing = jax.nn.softmax(mixing_logits, axis=-1)
    chosen = (routes[:, None] == lax.iota(jnp.int32, expert_count)[None, :]).astype(F32)
    gate = jnp.sum(chosen * router_probs, axis=-1, keepdims=True)
    dense_weight = mixing[:, 0:1]
    expert_weight = mixing[:, 1:2] * gate
    cotan = cotangent.astype(F32)

    dense_hidden, dense_slope = gelu_both(dot(mid_low, dense_up))
    dense_hidden = dense_hidden.astype(BF)
    dense_part = dot(dense_hidden, dense_down)
    dense_out_grad = (cotan * dense_weight).astype(BF)
    dense_pre_grad = (dot_t(dense_out_grad, dense_down) * dense_slope).astype(BF)
    mid_dense_part = dot_t(dense_pre_grad, dense_up)
    dense_down_grad = t_dot(dense_hidden, dense_out_grad)
    dense_up_grad = t_dot(mid_low, dense_pre_grad)
    dense_dot = jnp.sum(cotan * dense_part, axis=-1, keepdims=True)

    hidden_grads = expert_hidden_grad(after(cotan_slots, mid_slots), expert_down)
    hiddens, pre_grads, in_slots, slot_dots = expert_back(arrived, expert_up, hidden_grads)
    in_slots = in_slots.reshape(blocks, held * capacity, width)
    in_home = exchange(in_slots)

    slot_dot = jnp.swapaxes(slot_dots[:, :, 0].reshape(held, blocks, capacity), 0, 1)
    slot_dot = exchange(after(slot_dot.reshape(blocks, held * capacity), in_slots))
    slot_dot = slot_dot.reshape(slot_total)
    slot_weight = jnp.sum(jnp.where(hit, expert_weight[:, 0][None, :], 0.0), axis=1)
    slot_weight = exchange(after(slot_weight, slot_dot).reshape(blocks, held * capacity))
    slot_weight = slot_weight.reshape(blocks, held, capacity)
    out_slots = expert_down_rows(after(hiddens, in_slots), expert_down, blocks).reshape(
        blocks, held * capacity, width
    )
    out_home = exchange(after(out_slots, in_home))

    expert_dot = jnp.sum(jnp.where(hit, slot_dot[:, None], 0.0), axis=0)[:, None]
    gated_dot = gate * expert_dot
    mean_dot = dense_weight * dense_dot + mixing[:, 1:2] * gated_dot
    mixing_low = (mixing * (jnp.concatenate([dense_dot, gated_dot], axis=1) - mean_dot)).astype(BF)
    router_low = (expert_weight * expert_dot * (chosen - router_probs)).astype(BF)
    mid_part = (
        mid_dense_part
        + dot_t(router_low, router_weight)
        + dot_t(mixing_low, mixing_weight)
        + expert_weight * from_slots(in_home)
    )
    mid_low_part = mid_part.astype(BF)
    mid_grad = lax.psum_scatter(mid_low_part, "tensor", scatter_dimension=0, tiled=True)

    up_grads, down_grads = [], []
    for e in range(held):
        row_weight = after(slot_weight, in_home)[:, e].reshape(blocks * capacity, 1)
        grads = cotan_slots[:, e].reshape(blocks * capacity, width)
        rows = arrived[:, e].reshape(blocks * capacity, width)
        down_grads.append(t_dot(hiddens[e], (grads.astype(F32) * row_weight).astype(BF)))
        up_grads.append(t_dot(rows, (pre_grads[e].astype(F32) * row_weight).astype(BF)))
    expert_up_grad = jnp.stack(up_grads)
    expert_down_grad = jnp.stack(down_grads)
    out_part = dense_weight * dense_part + expert_weight * from_slots(after(out_home, mid_low_part))
    out_low = out_part.astype(BF)
    out_sum = lax.psum_scatter(
        after(out_low, mid_grad), "tensor", scatter_dimension=0, tiled=True
    )

    def pack(pieces):
        return jnp.concatenate([piece.reshape(blocks, -1, width) for piece in pieces], axis=1)

    def unpack(rows, sizes):
        starts = [sum(sizes[:i]) for i in range(len(sizes))]
        return [rows[..., s : s + n, :] for s, n in zip(starts, sizes)]

    mid_grad = mid_grad.astype(F32)
    residual_mine = mine(residual)
    unit_mine, inverse_mine = norm_stats(residual_mine)
    second_gain_grad = jnp.sum(mid_grad * unit_mine, axis=0)
    second_shift_grad = jnp.sum(mid_grad, axis=0)
    residual_grad = mine(cotangent).astype(F32) + norm_back(
        unit_mine, inverse_mine, second_gain, mid_grad
    )
    attn_grad_low = residual_grad.astype(BF)
    attended_grad = jnp.einsum(
        "td,znd->ztn", attn_grad_low, project_out_all, preferred_element_type=F32
    ).astype(BF)
    dense_sent = after(
        pack([dense_up_grad.astype(BF), dense_down_grad.astype(BF)]), out_home, attended_grad
    )
    attended_grad = lax.all_to_all(attended_grad, "tensor", 0, 0, tiled=True).reshape(
        row_count, head_columns
    )
    dense_got = exchange(dense_sent)
    qkv_grad = attend_backward(qkv, log_total, attended_grad)
    normed_low_part, first_sums = normed_back(qkv_grad, project_in, tokens)
    normed_grad = lax.psum_scatter(
        after(normed_low_part, out_sum), "tensor", scatter_dimension=0, tiled=True
    )
    late_residual, late_sum = lax.optimization_barrier(
        (residual, out_sum, normed_low_part)
    )[:2]
    layer_mine = (mine(late_residual) + late_sum.astype(F32)).astype(BF)
    normed_grad_f32 = normed_grad.astype(F32)
    unit_first, inverse_first = norm_stats(mine(tokens).astype(F32))
    input_mine = residual_grad + norm_back(unit_first, inverse_first, first_gain, normed_grad_f32)
    both_mine = jnp.stack([layer_mine, input_mine.astype(BF)])

    project_out_grad = jnp.einsum(
        "ztn,td->znd", mine(attended_all, 1), attn_grad_low, preferred_element_type=F32
    ).astype(BF)
    project_out_grad = jnp.swapaxes(
        project_out_grad.reshape(parts, blocks, head_columns // blocks, width), 0, 1
    ).reshape(parts * head_columns, width)
    project_in_grad = (
        jnp.einsum(
            "ctn,td->cnd", after(qkv_grad, normed_low_part), normed_low,
            preferred_element_type=F32,
        )
        .astype(BF)
        .reshape(3 * head_columns, width)
    )
    router_grad = t_dot(router_low, mid_low)
    mixing_grad = t_dot(mixing_low, mid_low)
    small = jnp.concatenate(
        [
            first_sums[:2],
            jnp.stack([second_gain_grad, second_shift_grad]),
            router_grad,
            mixing_grad,
        ],
        axis=0,
    )
    small_rows = small.shape[0]
    each = -(-small_rows // blocks)
    small = jnp.pad(small, ((0, each * blocks - small_rows), (0, 0))).reshape(blocks, each, width)
    small = jnp.pad(small, ((0, 0), (0, 16 - each), (0, 0))).astype(BF)
    rest_sent = pack([project_in_grad, project_out_grad, small.reshape(blocks * 16, width)])
    rest_got = exchange(after(rest_sent, dense_got))
    dense_got, rest_got, both_mine = lax.optimization_barrier((dense_got, rest_got, both_mine))
    both = lax.all_gather(both_mine, "tensor", axis=0)
    layer_out = both[:, 0].reshape(row_count, width)
    input_grad = both[:, 1].reshape(row_count, width)
    dense_piece = jnp.sum(dense_got.astype(F32), axis=0)
    project_in_piece, project_out_piece, small_piece = unpack(
        jnp.sum(rest_got.astype(F32), axis=0),
        [3 * head_columns // blocks, parts * head_columns // blocks, 16],
    )
    across = jnp.concatenate(
        [
            project_out_piece.reshape(parts, head_columns // blocks, width),
            jnp.broadcast_to(small_piece[None], (parts, 16, width)),
        ],
        axis=1,
    ).astype(BF)
    across = jnp.sum(
        lax.all_to_all(across, "tensor", 0, 0, tiled=True).astype(F32), axis=0
    )
    project_out_piece = across[: head_columns // blocks]
    small_piece = across[head_columns // blocks :]
    pieces = jnp.concatenate(
        [project_in_piece, project_out_piece, small_piece, dense_piece], axis=0
    ).astype(BF)
    sizes = [
        piece.shape[0] for piece in (project_in_piece, project_out_piece, small_piece)
    ] + [dense_piece.shape[0] // 2] * 2
    spread = exchange(jnp.broadcast_to(pieces[None], (blocks,) + pieces.shape))
    project_in_grad, project_out_grad, small, dense_up_grad, dense_down_grad = [
        piece.reshape(-1, width).astype(F32) for piece in unpack(spread, sizes)
    ]
    project_in_grad = jnp.transpose(project_in_grad.reshape(3, head_columns, width), (2, 0, 1))
    small = small.reshape(blocks, 16, width)[:, :each].reshape(blocks * each, width)

    return (
        layer_out,
        input_grad,
        small[0],
        small[1],
        project_in_grad,
        project_out_grad,
        small[2],
        small[3],
        small[4 : 4 + expert_count].T,
        small[4 + expert_count : 6 + expert_count].T,
        dense_up_grad,
        dense_down_grad,
        expert_up_grad,
        expert_down_grad,
    )


def solution(mesh):
    placed = (
        P("expert", None),
        P("expert", None),
        P("expert"),
        P("expert"),
        P(),
        P(),
        P(None, None, "tensor"),
        P("tensor", None),
        P(),
        P(),
        P(),
        P(),
        P(None, "tensor"),
        P("tensor", None),
        P("expert", None, "tensor"),
        P("expert", "tensor", None),
    )
    return jax.shard_map(
        local,
        mesh=mesh,
        in_specs=placed,
        out_specs=(
            P("expert", None),
            P("expert", None),
            P(),
            P(),
            P(None, None, "tensor"),
            P("tensor", None),
            P(),
            P(),
            P(),
            P(),
            P(None, "tensor"),
            P("tensor", None),
            P("expert", None, "tensor"),
            P("expert", "tensor", None),
        ),
        check_vma=False,
    )
```

time: 1280 us -> 603 us (0.47)
  waiting for transfers between devices: 869 us -> 272 us
  local copies, waits for them, and re-layouts: 120 us -> 33.8 us
  Pallas kernels: 0 us -> 71 us
  matrix products: 142 us -> 97.5 us
  starting transfers between devices: 19 us -> 50.5 us
  blocking collectives: 26.6 us -> 0 us
  other arithmetic: 69.5 us -> 54.8 us
    psum x5 -> x0, waiting for transfers between devices: 706 us -> none  [the longest x1 220 us: local(): lax.psum(dense_part.astype(jnp.bfloat16), 'tensor').astype(jnp.float32)]
    pallas_call x0 -> x7, Pallas kernels: none -> 71 us  [the longest x1 17.6 us: expert_back(): pl.pallas_call(gelu_back_kernel, grid=(held, rows // tile), out_shape=(ja...]
    all_gather x0 -> x3, waiting for transfers between devices: none -> 57.6 us  [the longest x1 26.5 us: local(): lax.all_gather(attended, 'tensor', axis=0, tiled=True)]
    gather x4 -> x0, local copies, waits for them, and re-layouts: 45.1 us -> none  [the longest x2 25.6 us: to_slots(): taken = jnp.take(row_values, holder, axis=0, mode='fill', fill_value=0)]
    dot_general x38 -> x24, matrix products: 142 us -> 97.5 us  [the longest x10 37.1 us: t_dot(): lax.dot_general(a, b, (((0,), (0,)), ((), ())), preferred_element_type=F32)]
    all_to_all x4 -> x11, waiting for transfers between devices: 164 us -> 203 us  [the longest x9 165 us: exchange(): return lax.all_to_all(buffer, 'expert', 0, 0, tiled=True)]
    all_to_all x4 -> x11, starting transfers between devices: 18.5 us -> 49 us  [the longest x9 41.2 us: exchange(): return lax.all_to_all(buffer, 'expert', 0, 0, tiled=True)]
    psum x1 -> x0, blocking collectives: 26.6 us -> none  [local(): lax.psum(first_gain_grad.astype(jnp.bfloat16), 'expert').astype(jnp.float32)]
  transfers between devices with their start and end apart: 9 -> 18, of which waited for: 9 -> 15; matrix products, arithmetic and copies ran while one was open for 7% -> 27% of each run, Pallas kernels for 0% -> 9%
where the time goes in v1:
time: 603 us; the launch traced here: 595 us
  waiting for transfers between devices  272 us (45%)
  matrix products  97.5 us (16%)
  Pallas kernels  71 us (12%)
  other arithmetic  54.8 us (9%)
  starting transfers between devices  50.5 us (8%)
  local copies, waits for them, and re-layouts  33.8 us (6%)
  between operations  15.1 us (3%)
    all_to_all x9, waiting for transfers between devices, exchange(): return lax.all_to_all(buffer, 'expert', 0, 0, tiled=True)  165 us
    all_to_all x9, starting transfers between devices, exchange(): return lax.all_to_all(buffer, 'expert', 0, 0, tiled=True)  41.2 us
    dot_general x10, matrix products, t_dot(): lax.dot_general(a, b, (((0,), (0,)), ((), ())), preferred_element_type=F32)  37.1 us
    dot_general x6, matrix products, dot(): return jnp.dot(a, b, preferred_element_type=F32)  33.7 us
    all_gather x1, waiting for transfers between devices, local(): lax.all_gather(attended, 'tensor', axis=0, tiled=True)  26.5 us
    all_to_all x1, waiting for transfers between devices, local(): lax.all_to_all(attended_grad, 'tensor', 0, 0, tiled=True)  21.8 us
    pallas_call x1, Pallas kernels, expert_back(): pl.pallas_call(gelu_back_kernel, grid=(held, rows // tile), out_shape=(ja...  17.6 us
    all_gather x1, waiting for transfers between devices, local(): both = lax.all_gather(both_mine, 'tensor', axis=0)  16.8 us
  transfers between devices with their start and end apart: 18, of which 15 were waited for; matrix products, arithmetic and copies ran while one was open for 27% of the time, Pallas kernels for 9%

profile of v1, /device:TPU:0, one launch (start us, length us, event | category | flops | bytes accessed | tf_op | source)
XLA Modules:
  0.0 594.8 jit_solution(7966780887492537763)
XLA Ops:
  16.9 9.7 %attend_forward.1 = (bf16[1024,256]{1,0:T(8,128)(2,1)}, f32[2,8,1024]{2,1,0:T(8,128)}) custom-call(bf16[3,1024,256]{2,1,0:T(8,128)(2,1)} %fusion.40.qkv_ref), custom_call_target="tpu_custom_call" | custom-call | flops 1073741824 | bytes 2097152 | tf_op jit(solution)/shard_map/attend_forward/pallas_call | solution.py:128
  26.7 14.2 %all-gather.8.cloned.1.call-done = bf16[512,1024]{1,0:T(8,128)(2,1)} async-done(((bf16[128,1024]{1,0:T(8,128)(2,1)}), bf16[512,1024]{1,0:T(8,128)(2,1)}) %all-gather.8.cloned.1.call-update) | async-done | bytes 1048592 | tf_op jit(solution)/shard_map/all_gather | solution.py:377
  40.9 7.6 %fusion.26 = bf16[2048,1024]{1,0:T(8,128)(2,1)} fusion(bf16[1024,1024]{1,0:T(8,128)(2,1)} %param.17, s32[1024]{0:T(1024)S(1)} %add_select_fusion), kind=kOutput, calls=%fused_computation.47 | convolution fusion | flops 4299161600 | bytes 6295552 | tf_op jit(solution)/shard_map/dot_general | solution.py:51
  48.5 5.2 all-to-all-start
  61.6 26.5 %all-gather.6.cloned.1.call-done = bf16[4096,256]{1,0:T(8,128)(2,1)} async-done(((bf16[1024,256]{1,0:T(8,128)(2,1)}), bf16[4096,256]{1,0:T(8,128)(2,1)}) %all-gather.6.cloned.1.call-update) | async-done | bytes 2097168 | tf_op jit(solution)/shard_map/all_gather | solution.py:386
  88.1 7.4 %project_norm.1 = (f32[1024,1024]{1,0:T(8,128)}, bf16[1024,1024]{1,0:T(8,128)(2,1)}) custom-call(bf16[4,1024,256]{2,1,0:T(8,128)(2,1)} %bitcast.164, bf16[4,256,1024]{2,1,0:T(8,128)(2,1)} %pad_maximum_fusion.3.weight_ref, bf16[1024,1024]{1,0:T(8,128)(2,1)} %token_ref.3, f32[1,1024]{1,0:T(1,128)} %bitcast.181, f32[1,1024]{1,0:T(1,128)} %bitcast.192), custom_call_target="tpu_custom_call" | custom-call | flops 2147483648 | bytes 12582912 | tf_op jit(solution)/shard_map/project_norm/pallas_call | solution.py:180
  95.5 7.6 %fusion.25 = bf16[2048,1024]{1,0:T(8,128)(2,1)} fusion(bf16[1024,1024]{1,0:T(8,128)(2,1)} %get-tuple-element.51, s32[1024]{0:T(1024)S(1)} %add_select_fusion), kind=kOutput, calls=%fused_computation.46 | convolution fusion | flops 4299161600 | bytes 6295552 | tf_op jit(solution)/shard_map/dot_general | solution.py:51
  112.5 9.1 %expert_hidden_grad.1.hidden_grad_ref = bf16[2,1024,1024]{2,1,0:T(8,128)(2,1)} custom-call(bf16[8,2,128,1024]{3,2,1,0:T(8,128)(2,1)} %bitcast.9.grads_ref, bf16[2,1024,1024]{2,1,0:T(8,128)(2,1)} %down_ref.3), custom_call_target="tpu_custom_call" | custom-call | flops 4294967296 | bytes 12582912 | tf_op jit(solution)/shard_map/expert_hidden_grad/pallas_call | solution.py:282
  121.6 6.5 %fusion.90 = f32[1024,1024]{1,0:T(8,128)} fusion(bf16[1024,1024]{1,0:T(8,128)(2,1)} %get-tuple-element.51, bf16[1024,1024]{1,0:T(8,128)(2,1)} %param.28), kind=kOutput, calls=%fused_computation.166 | convolution fusion | flops 2147483648 | bytes 8388608 | tf_op jit(solution)/shard_map/dot_general | solution.py:51
  128.1 28.8 %all-to-all-done.1 = bf16[8,256,1024]{2,1,0:T(8,128)(2,1)} async-done(((bf16[8,256,1024]{2,1,0:T(8,128)(2,1)}), bf16[8,256,1024]{2,1,0:T(8,128)(2,1)}, u32[]{:S(2)}, u32[]{:S(2)}) %all-to-all-start.1) | async-done | bytes 4194336 | tf_op jit(solution)/shard_map/all_to_all | solution.py:409
  156.9 17.6 %expert_back.1 = (bf16[2,1024,1024]{2,1,0:T(8,128)(2,1)}, bf16[2,1024,1024]{2,1,0:T(8,128)(2,1)}, bf16[8,2,128,1024]{3,2,1,0:T(8,128)(2,1)}, f32[2,1024,128]{2,1,0:T(8,128)}) custom-call(bf16[8,2,128,1024]{3,2,1,0:T(8,128)(2,1)} %bitcast.13.rows_ref, bf16[2,1024,1024]{2,1,0:T(8,128)(2,1)} %up_ref.1, bf16[2,1024,1024]{2,1,0:T(8,128)(2,1)} %expert_hidden_grad.1.hidden_grad_ref), custom_call_target="tpu_custom_call" | custom-call | flops 8589934592 | bytes 29360128 | tf_op jit(solution)/shard_map/expert_back/pallas_call | solution.py:224
  184.6 4.8 all-to-all-start.2
  189.4 7.5 %fusion.12 = (f32[1024]{0:T(1024)S(1)}, f32[1024,1024]{1,0:T(8,128)}) fusion(bf16[1024,1024]{1,0:T(8,128)(2,1)} %param.17, bf16[1024,1024]{1,0:T(8,128)(2,1)S(1)} %copy-done, f32[1024,1024]{1,0:T(8,128)} %fusion.90), kind=kOutput, calls=%fused_computation.25 | convolution fusion | flops 2160065536 | bytes 12587008 | tf_op jit(solution)/shard_map/dot_general | solution.py:51
  196.9 9.1 %expert_down_rows.1 = bf16[8,2,128,1024]{3,2,1,0:T(8,128)(2,1)} custom-call(bf16[2,1024,1024]{2,1,0:T(8,128)(2,1)} %get-tuple-element.55.hidden_ref, bf16[2,1024,1024]{2,1,0:T(8,128)(2,1)} %down_ref.3), custom_call_target="tpu_custom_call" | custom-call | flops 4294967296 | bytes 12582912 | tf_op jit(solution)/shard_map/expert_down_rows/pallas_call | solution.py:252
  211.8 6.4 %fusion.19 = bf16[1024,1024]{1,0:T(8,128)(2,1)S(1)} fusion(f32[1024,1024]{1,0:T(8,128)} %fusion.90, bf16[1024,1024]{1,0:T(8,128)(2,1)S(1)} %copy-done, bf16[1024,1024]{1,0:T(8,128)(2,1)S(1)} %copy-done.17, f32[1024]{0:T(1024)S(1)} %bitcast.183), kind=kOutput, calls=%fused_computation.32 | convolution fusion | flops 2170552320 | bytes 10489856 | tf_op jit(solution)/shard_map/dot_general | solution.py:54
  223.9 14.6 %all-to-all-done.2 = bf16[8,256,1024]{2,1,0:T(8,128)(2,1)} async-done(((bf16[8,256,1024]{2,1,0:T(8,128)(2,1)}), bf16[8,256,1024]{2,1,0:T(8,128)(2,1)}, u32[]{:S(2)}, u32[]{:S(2)}) %all-to-all-start.2) | async-done | bytes 4194336 | tf_op jit(solution)/shard_map/all_to_all | solution.py:409
  243.4 6.5 %fusion.1 = f32[1024,1024]{1,0:T(8,128)S(1)} fusion(bf16[2048,1024]{1,0:T(8,128)(2,1)} %bitcast.25, s32[1024]{0:T(1024)S(1)} %add_select_fusion), kind=kOutput, calls=%fused_computation.6 | convolution fusion | flops 4297064448 | bytes 8392704 | tf_op jit(solution)/shard_map/dot_general | solution.py:43
  255.6 36.6 %all-to-all-done.3 = bf16[8,256,1024]{2,1,0:T(8,128)(2,1)} async-done(((bf16[8,256,1024]{2,1,0:T(8,128)(2,1)}), bf16[8,256,1024]{2,1,0:T(8,128)(2,1)}, u32[]{:S(2)}, u32[]{:S(2)}) %all-to-all-start.3) | async-done | bytes 4194336 | tf_op jit(solution)/shard_map/all_to_all | solution.py:409
  292.2 8.8 %add_convert_fusion = bf16[1024,1024]{1,0:T(8,128)(2,1)} fusion(f32[1024,1024]{1,0:T(8,128)} %get-tuple-element.152, f32[1024]{0:T(1024)S(1)} %bitcast.173, f32[1024]{0:T(1024)S(1)} %bitcast.184, bf16[2048,1024]{1,0:T(8,128)(2,1)} %bitcast.33, s32[1024]{0:T(1024)S(1)} %add_select_fusion), kind=kOutput, calls=%fused_computation.38 | convolution fusion | flops 4301258752 | bytes 10498048 | tf_op jit(solution)/shard_map/dot_general | solution.py:43
  301.1 6.8 %convolution_convert_fusion.1 = bf16[1024,1024]{1,0:T(8,128)(2,1)} fusion(bf16[1024,1024]{1,0:T(8,128)(2,1)S(1)} %copy-done.18, f32[1024]{0:T(1024)S(1)} %bitcast.185, f32[1024,1024]{1,0:T(8,128)} %fusion.90), kind=kOutput, calls=%fused_computation.68 | convolution fusion | flops 2161115136 | bytes 8392704 | tf_op jit(solution)/shard_map/dot_general | solution.py:43
  322.4 21.8 %all-to-all-done.6 = bf16[4,256,256]{1,2,0:T(8,128)(2,1)} async-done(((bf16[4,256,256]{1,2,0:T(8,128)(2,1)}), bf16[4,256,256]{1,2,0:T(8,128)(2,1)}, u32[]{:S(2)}, u32[]{:S(2)}) %all-to-all-start.6) | async-done | bytes 524320 | tf_op jit(solution)/shard_map/all_to_all | solution.py:509
  351.3 11.9 %attend_backward.1.grad_ref = bf16[3,1024,256]{2,1,0:T(8,128)(2,1)} custom-call(bf16[3,1024,256]{2,1,0:T(8,128)(2,1)} %fusion.40.qkv_ref, f32[2,8,1024]{2,1,0:T(8,128)} %get-tuple-element.61.log_ref, bf16[1024,256]{1,0:T(8,128)(2,1)} %bitcast.163), custom_call_target="tpu_custom_call" | custom-call | flops 2684354560 | bytes 4194304 | tf_op jit(solution)/shard_map/attend_backward/pallas_call | solution.py:149
  363.2 6.2 %normed_back.1 = (bf16[1024,1024]{1,0:T(8,128)(2,1)}, f32[8,1024]{1,0:T(8,128)}) custom-call(bf16[3,1024,256]{2,1,0:T(8,128)(2,1)} %attend_backward.1.grad_ref, bf16[3,1024,256]{2,1,0:T(8,128)(2,1)} %bitcast.191, bf16[1024,1024]{1,0:T(8,128)(2,1)} %token_ref.3), custom_call_target="tpu_custom_call" | custom-call | flops 1610612736 | bytes 6291456 | tf_op jit(solution)/shard_map/normed_back/pallas_call | solution.py:318
  381.7 16.2 %all-to-all-done.5 = bf16[8,256,1024]{2,1,0:T(8,128)(2,1)} async-done(((bf16[8,256,1024]{2,1,0:T(8,128)(2,1)}), bf16[8,256,1024]{2,1,0:T(8,128)(2,1)}, u32[]{:S(2)}, u32[]{:S(2)}) %all-to-all-start.5) | async-done | bytes 4194336 | tf_op jit(solution)/shard_map/all_to_all | solution.py:409
  405.3 8.1 %reduce-scatter.8.cloned.1.call-done = bf16[256,1024]{1,0:T(8,128)(2,1)} async-done(((bf16[1024,1024]{1,0:T(8,128)(2,1)}), bf16[256,1024]{1,0:T(8,128)(2,1)}) %reduce-scatter.8.cloned.1.call-update) | async-done | bytes 524304 | tf_op jit(solution)/shard_map/reduce_scatter | solution.py:515
  418.3 30.4 %all-to-all-done.7 = bf16[8,240,1024]{2,1,0:T(8,128)(2,1)} async-done(((bf16[8,240,1024]{2,1,0:T(8,128)(2,1)}), bf16[8,240,1024]{2,1,0:T(8,128)(2,1)}, u32[]{:S(2)}, u32[]{:S(2)}) %all-to-all-start.7) | async-done | bytes 3932192 | tf_op jit(solution)/shard_map/all_to_all | solution.py:409
  459.4 15.9 %all-to-all-done.8 = bf16[4,48,1024]{2,1,0:T(8,128)(2,1)S(1)} async-done(((bf16[4,48,1024]{2,1,0:T(8,128)(2,1)}), bf16[4,48,1024]{2,1,0:T(8,128)(2,1)S(1)}, u32[]{:S(2)}, u32[]{:S(2)}) %all-to-all-start.8) | async-done | bytes 393248 | tf_op jit(solution)/shard_map/all_to_all | solution.py:575
  475.4 4.8 all-to-all-start.10
  488.5 4.8 all-to-all-start.9
  509.6 6.8 %pad_maximum_fusion = (f32[2,1024,1024]{2,1,0:T(8,128)}, f32[2,1024,1024]{2,1,0:T(8,128)}) fusion(f32[1,1024,1024]{2,1,0:T(8,128)S(1)} %convolution_bitcast_fusion.2, f32[1,1024,1024]{2,1,0:T(8,128)S(1)} %convolution_bitcast_fusion.3, f32[1,1024,1024]{2,1,0:T(8,128)S(1)} %convolution_bitcast_fusion, f32[1,1024,1024]{2,1,0:T(8,128)S(1)} %convolution_bitcast_fusion.1), kind=kLoop, calls=%fused_computation | loop fusion | flops 4194304 | bytes 33554432 | tf_op jit(solution)/shard_map/stack | solution.py:479
  516.4 16.8 %all-gather.10.cloned.1.call-done = bf16[8,256,1024]{2,1,0:T(8,128)(2,1)} async-done(((bf16[2,256,1024]{2,1,0:T(8,128)(2,1)}), bf16[8,256,1024]{2,1,0:T(8,128)(2,1)}) %all-gather.10.cloned.1.call-update) | async-done | bytes 4194320 | tf_op jit(solution)/shard_map/all_gather | solution.py:559
  537.9 29.7 %all-to-all-done.9 = bf16[8,400,1024]{2,1,0:T(8,128)(2,1)} async-done(((bf16[8,400,1024]{2,1,0:T(8,128)(2,1)}), bf16[8,400,1024]{2,1,0:T(8,128)(2,1)}, u32[]{:S(2)}, u32[]{:S(2)}) %all-to-all-start.9) | async-done | bytes 6553632 | tf_op jit(solution)/shard_map/all_to_all | solution.py:409
  (176 shorter events, 164.9 us)
Async XLA Ops:
  7.2 182.2 %copy-start = (bf16[1024,1024]{1,0:T(8,128)(2,1)S(1)}, bf16[1024,1024]{1,0:T(8,128)(2,1)}, u32[]{:S(2)}) copy-start(bf16[1024,1024]{1,0:T(8,128)(2,1)} %param.29) | copy-start | bytes 6291460
  7.2 6.4 %copy-start.26 = (f32[1024]{0:T(1024)S(1)}, f32[1024]{0:T(1024)}, u32[]{:S(2)}) copy-start(f32[1024]{0:T(1024)} %param.21) | copy-start | bytes 12292
  7.2 6.4 %copy-start.22 = (f32[1024]{0:T(1024)S(1)}, f32[1024]{0:T(1024)}, u32[]{:S(2)}) copy-start(f32[1024]{0:T(1024)} %param.20) | copy-start | bytes 12292
  7.2 33.7 %all-gather.8.cloned.1.call-start = ((), (), s32[]{:S(2)}) async-start(), calls=%async_computation.18 | async-start | bytes 1310720 | tf_op jit(solution)/shard_map/all_gather | solution.py:377
  9.1 79.0 %all-gather.6.cloned.1.call-start = ((), (), s32[]{:S(2)}) async-start(), calls=%async_computation.14 | async-start | bytes 2621440 | tf_op jit(solution)/shard_map/all_gather | solution.py:386
  13.6 13.0 %copy-start.19 = (s32[1024]{0:T(1024)S(1)}, s32[1024]{0:T(1024)}, u32[]{:S(2)}) copy-start(s32[1024]{0:T(1024)} %param.18) | copy-start | bytes 12292
  13.6 13.0 %copy-start.23 = (s32[1024]{0:T(1024)S(1)}, s32[1024]{0:T(1024)}, u32[]{:S(2)}) copy-start(s32[1024]{0:T(1024)} %param.19) | copy-start | bytes 12292
  48.5 54.5 %all-to-all-start = ((bf16[8,256,1024]{2,1,0:T(8,128)(2,1)}), bf16[8,256,1024]{2,1,0:T(8,128)(2,1)}, u32[]{:S(2)}, u32[]{:S(2)}) async-start(bf16[8,256,1024]{2,1,0:T(8,128)(2,1)} %bitcast.149), calls=%async_computation | async-start | bytes 8388608 | tf_op jit(solution)/shard_map/all_to_all | solution.py:409
  53.8 3.6 collective-permute-start
  103.1 7.0 %copy-start.16 = (bf16[1024,16]{0,1:T(8,128)(2,1)S(1)}, bf16[1024,16]{0,1:T(8,128)(2,1)}, u32[]{:S(2)}) copy-start(bf16[1024,16]{0,1:T(8,128)(2,1)} %param.26) | copy-start | bytes 98308
  103.1 53.8 %all-to-all-start.1 = ((bf16[8,256,1024]{2,1,0:T(8,128)(2,1)}), bf16[8,256,1024]{2,1,0:T(8,128)(2,1)}, u32[]{:S(2)}, u32[]{:S(2)}) async-start(bf16[8,256,1024]{2,1,0:T(8,128)(2,1)} %bitcast.150), calls=%async_computation.1 | async-start | bytes 8388608 | tf_op jit(solution)/shard_map/all_to_all | solution.py:409
  176.6 8.0 %all-to-all-start.4 = ((f32[8,1,256]{2,1,0:T(1,128)}), f32[8,1,256]{2,1,0:T(1,128)S(1)}, u32[]{:S(2)}, u32[]{:S(2)}) async-start(f32[8,1,256]{2,1,0:T(1,128)} %all_to_all.43), calls=%async_computation.4 | async-start | bytes 16384 | tf_op jit(solution)/shard_map/all_to_all | solution.py:409
  184.6 53.9 %all-to-all-start.2 = ((bf16[8,256,1024]{2,1,0:T(8,128)(2,1)}), bf16[8,256,1024]{2,1,0:T(8,128)(2,1)}, u32[]{:S(2)}, u32[]{:S(2)}) async-start(bf16[8,256,1024]{2,1,0:T(8,128)(2,1)} %bitcast.148), calls=%async_computation.2 | async-start | bytes 8388608 | tf_op jit(solution)/shard_map/all_to_all | solution.py:409
  211.8 7.7 %copy-start.24 = (bf16[1024,1024]{1,0:T(8,128)(2,1)S(1)}, bf16[1024,1024]{1,0:T(8,128)(2,1)}, u32[]{:S(2)}) copy-start(bf16[1024,1024]{1,0:T(8,128)(2,1)} %param.28) | copy-start | bytes 6291460
  238.5 53.7 %all-to-all-start.3 = ((bf16[8,256,1024]{2,1,0:T(8,128)(2,1)}), bf16[8,256,1024]{2,1,0:T(8,128)(2,1)}, u32[]{:S(2)}, u32[]{:S(2)}) async-start(bf16[8,256,1024]{2,1,0:T(8,128)(2,1)} %bitcast.147), calls=%async_computation.3 | async-start | bytes 8388608 | tf_op jit(solution)/shard_map/all_to_all | solution.py:409
  243.1 57.9 %reduce-scatter.4.cloned.1.call-start = ((), (), s32[]{:S(2)}) async-start(), calls=%async_computation.15 | async-start | bytes 2621440 | tf_op jit(solution)/shard_map/reduce_scatter | solution.py:470
  243.3 6.6 %copy-start.5 = (f32[1024,1024]{1,0:T(8,128)S(1)}, f32[1024,1024]{1,0:T(8,128)}, u32[]{:S(2)}) copy-start(f32[1024,1024]{1,0:T(8,128)} %fusion.80) | copy-start | bytes 12582916
  243.3 6.6 %copy-start.9 = (f32[1024,1024]{1,0:T(8,128)S(1)}, f32[1024,1024]{1,0:T(8,128)}, u32[]{:S(2)}) copy-start(f32[1024,1024]{1,0:T(8,128)} %fusion.91) | copy-start | bytes 12582916
  252.7 116.7 %reduce-scatter.6.cloned.1.call-start = ((), (), s32[]{:S(2)}) async-start(), calls=%async_computation.16 | async-start | bytes 2621440 | tf_op jit(solution)/shard_map/reduce_scatter | solution.py:483
  292.2 8.9 %copy-start.18 = (bf16[1024,1024]{1,0:T(8,128)(2,1)S(1)}, bf16[1024,1024]{1,0:T(8,128)(2,1)}, u32[]{:S(2)}) copy-start(bf16[1024,1024]{1,0:T(8,128)(2,1)} %param.17) | copy-start | bytes 6291460
  301.0 6.8 %copy-start.7 = (f32[1024,1024]{1,0:T(8,128)S(1)}, f32[1024,1024]{1,0:T(8,128)}, u32[]{:S(2)}) copy-start(f32[1024,1024]{1,0:T(8,128)} %get-tuple-element.68) | copy-start | bytes 12582916
  301.0 6.8 %copy-start.8 = (bf16[256,1024]{1,0:T(8,128)(2,1)S(1)}, bf16[256,1024]{1,0:T(8,128)(2,1)}, u32[]{:S(2)}) copy-start(bf16[256,1024]{1,0:T(8,128)(2,1)} %reduce-scatter.4.cloned.1.call-done) | copy-start | bytes 1572868
  301.1 6.8 %copy-start.21 = (f32[1024]{0:T(1024)S(1)}, f32[1024]{0:T(1024)}, u32[]{:S(2)}) copy-start(f32[1024]{0:T(1024)} %param.24) | copy-start | bytes 12292
  308.4 7.3 %copy-start.2 = (bf16[1024,1024]{1,0:T(8,128)(2,1)S(1)}, bf16[1024,1024]{1,0:T(8,128)(2,1)}, u32[]{:S(2)}) copy-start(bf16[1024,1024]{1,0:T(8,128)(2,1)} %get-tuple-element.51) | copy-start | bytes 6291460
  311.6 32.6 %all-to-all-start.6 = ((bf16[4,256,256]{1,2,0:T(8,128)(2,1)}), bf16[4,256,256]{1,2,0:T(8,128)(2,1)}, u32[]{:S(2)}, u32[]{:S(2)}) async-start(bf16[4,256,256]{1,2,0:T(8,128)(2,1)} %fusion.46), calls=%async_computation.7 | async-start | bytes 1048576 | tf_op jit(solution)/shard_map/all_to_all | solution.py:509
  344.2 53.7 %all-to-all-start.5 = ((bf16[8,256,1024]{2,1,0:T(8,128)(2,1)}), bf16[8,256,1024]{2,1,0:T(8,128)(2,1)}, u32[]{:S(2)}, u32[]{:S(2)}) async-start(bf16[8,256,1024]{2,1,0:T(8,128)(2,1)} %pad_maximum_fusion.2), calls=%async_computation.6 | async-start | bytes 8388608 | tf_op jit(solution)/shard_map/all_to_all | solution.py:409
  348.8 64.6 %reduce-scatter.8.cloned.1.call-start = ((), (), s32[]{:S(2)}) async-start(), calls=%async_computation.17 | async-start | bytes 2621440 | tf_op jit(solution)/shard_map/reduce_scatter | solution.py:515
  397.9 50.8 %all-to-all-start.7 = ((bf16[8,240,1024]{2,1,0:T(8,128)(2,1)}), bf16[8,240,1024]{2,1,0:T(8,128)(2,1)}, u32[]{:S(2)}, u32[]{:S(2)}) async-start(bf16[8,240,1024]{2,1,0:T(8,128)(2,1)} %fusion.24), calls=%async_computation.8 | async-start | bytes 7864320 | tf_op jit(solution)/shard_map/all_to_all | solution.py:409
  402.4 130.9 %all-gather.10.cloned.1.call-start = ((), (), s32[]{:S(2)}) async-start(), calls=%async_computation.19 | async-start | bytes 5242880 | tf_op jit(solution)/shard_map/all_gather | solution.py:559
  452.5 22.9 %all-to-all-start.8 = ((bf16[4,48,1024]{2,1,0:T(8,128)(2,1)}), bf16[4,48,1024]{2,1,0:T(8,128)(2,1)S(1)}, u32[]{:S(2)}, u32[]{:S(2)}) async-start(bf16[4,48,1024]{2,1,0:T(8,128)(2,1)} %pad_maximum_fusion.6), calls=%async_computation.11 | async-start | bytes 786432 | tf_op jit(solution)/shard_map/all_to_all | solution.py:575
  475.4 9.5 %all-to-all-start.10 = ((f32[8,1,256]{2,1,0:T(1,128)}), f32[8,1,256]{2,1,0:T(1,128)S(1)}, u32[]{:S(2)}, u32[]{:S(2)}) async-start(f32[8,1,256]{2,1,0:T(1,128)} %bitcast.52), calls=%async_computation.13 | async-start | bytes 16384 | tf_op jit(solution)/shard_map/all_to_all | solution.py:409
  488.5 79.2 %all-to-all-start.9 = ((bf16[8,400,1024]{2,1,0:T(8,128)(2,1)}), bf16[8,400,1024]{2,1,0:T(8,128)(2,1)}, u32[]{:S(2)}, u32[]{:S(2)}) async-start(bf16[8,400,1024]{2,1,0:T(8,128)(2,1)} %broadcast_in_dim.52), calls=%async_computation.12 | async-start | bytes 13107200 | tf_op jit(solution)/shard_map/all_to_all | solution.py:409
  (16 other events, 56.2 us)
Sparse Core Ops, SparseCore 0:
  10.2 30.6 all-gather.7
  43.0 45.0 all-gather.5
  252.8 43.1 reduce-scatter.3
  301.1 49.4 reduce-scatter.5
  369.6 43.7 reduce-scatter.7
  448.8 84.3 all-gather.9

commit v2 on v1

--- a/solution.py
+++ b/solution.py
@@ -30,13 +30,10 @@
 
 
 def gelu_both(v):
-    inner = 0.7978845608 * (v + 0.044715 * v * v * v)
-    bent = jnp.tanh(inner)
-    value = 0.5 * v * (1.0 + bent)
-    slope = 0.5 * (1.0 + bent) + 0.5 * v * (1.0 - bent * bent) * 0.7978845608 * (
-        1.0 + 3.0 * 0.044715 * v * v
-    )
-    return value, slope
+    square = v * v
+    half = 0.5 + 0.5 * jnp.tanh(v * (0.7978845608 + 0.7978845608 * 0.044715 * square))
+    steep = v * (1.5957691216 + 1.5957691216 * 0.134145 * square)
+    return v * half, half + half * (steep * (1.0 - half))
 
 
 def t_dot(a, b):
@@ -204,22 +201,35 @@
 def gelu_back_kernel(rows_ref, up_ref, hidden_grad_ref, hidden_ref, pre_grad_ref, in_ref, dot_ref):
     shape = rows_ref.shape
     count = shape[0] * shape[2]
-    hidden, slope = gelu_both(dot(rows_ref[...].reshape(count, shape[3]), up_ref[0]))
-    hidden = hidden.astype(BF)
-    hidden_ref[0] = hidden
-    hidden_grad = hidden_grad_ref[0].astype(F32)
-    pre_grad = (hidden_grad * slope).astype(BF)
-    pre_grad_ref[0] = pre_grad
-    in_ref[...] = dot_t(pre_grad, up_ref[0]).astype(BF).reshape(shape)
-    dots = jnp.sum(hidden.astype(F32) * hidden_grad, axis=1, keepdims=True)
-    dot_ref[0] = jnp.broadcast_to(dots, (count, 128))
+    rows = rows_ref[...].reshape(count, shape[3])
+    units = up_ref.shape[2]
+    step = min(256, units)
+    dots = None
+    for start in range(0, units, step):
+        here = slice(start, start + step)
+        hidden, slope = gelu_both(dot(rows, up_ref[0, :, here]))
+        hidden = hidden.astype(BF)
+        hidden_ref[0, :, here] = hidden
+        hidden_grad = hidden_grad_ref[0, :, here].astype(F32)
+        pre_grad_ref[0, :, here] = (hidden_grad * slope).astype(BF)
+        product = hidden.astype(F32) * hidden_grad
+        for lane in range(0, step, 128):
+            part = product[:, lane : lane + 128]
+            dots = part if dots is None else dots + part
+    columns = in_ref.shape[3]
+    in_ref[...] = dot_t(pre_grad_ref[0], up_ref[0, :columns, :]).astype(BF).reshape(in_ref.shape)
+    capacity = shape[2]
+    for block in range(shape[0]):
+        here = jnp.transpose(dots[block * capacity : (block + 1) * capacity])
+        here = jnp.sum(here, axis=0, keepdims=True)
+        dot_ref[0, block] = jnp.broadcast_to(here, (8, capacity))
 
 
 def expert_back(arrived, expert_up, hidden_grads, tile=512):
     blocks, held, capacity, width = arrived.shape
     rows = blocks * capacity
     units = expert_up.shape[2]
-    slots = pl.BlockSpec((tile // capacity, 1, capacity, width), lambda e, i: (i, e, 0, 0))
+    slots = lambda e, i: (i, e, 0, 0)
     flat = pl.BlockSpec((1, tile, units), lambda e, i: (e, i, 0))
     return pl.pallas_call(
         gelu_back_kernel,
@@ -227,46 +237,128 @@
         out_shape=(
             jax.ShapeDtypeStruct((held, rows, units), BF),
             jax.ShapeDtypeStruct((held, rows, units), BF),
-            jax.ShapeDtypeStruct(arrived.shape, BF),
-            jax.ShapeDtypeStruct((held, rows, 128), F32),
-        ),
-        in_specs=[slots, pl.BlockSpec((1, width, units), lambda e, i: (e, 0, 0)), flat],
-        out_specs=(flat, flat, slots, pl.BlockSpec((1, tile, 128), lambda e, i: (e, i, 0))),
-        cost_estimate=pl.CostEstimate(
-            flops=4 * held * rows * units * width,
-            bytes_accessed=14 * held * rows * width,
+            jax.ShapeDtypeStruct((blocks, held, capacity, width // 2), BF),
+            jax.ShapeDtypeStruct((held, blocks, 8, capacity), F32),
+        ),
+        in_specs=[
+            pl.BlockSpec((tile // capacity, 1, capacity, width), slots),
+            pl.BlockSpec((1, width, units), lambda e, i: (e, 0, 0)),
+            flat,
+        ],
+        out_specs=(
+            flat,
+            flat,
+            pl.BlockSpec((tile // capacity, 1, capacity, width // 2), slots),
+            pl.BlockSpec((1, tile // capacity, 8, capacity), lambda e, i: (e, i, 0, 0)),
+        ),
+        cost_estimate=pl.CostEstimate(
+            flops=3 * held * rows * units * width,
+            bytes_accessed=13 * held * rows * width,
             transcendentals=held * rows * units,
         ),
         name="expert_back",
     )(arrived, expert_up, hidden_grads)
 
 
-def down_kernel(hidden_ref, down_ref, out_ref):
-    out_ref[...] = dot(hidden_ref[0], down_ref[0]).astype(BF).reshape(out_ref.shape)
-
-
-def expert_down_rows(hidden, expert_down, blocks, tile=512):
-    held, rows, units = hidden.shape
+EXTRA = 16
+
+
+def slot_tail_kernel(flat_ref, weight_ref, dot_ref, out_ref):
+    count, _, size, columns = out_ref.shape
+    capacity = size - EXTRA
+    rows = dot_t(flat_ref[0], weight_ref[0]).astype(BF)
+    for block in range(count):
+        out_ref[block, 0, :capacity, :] = rows[block * capacity : (block + 1) * capacity]
+        dots = dot_ref[0, block]
+        low = dots - dots.astype(BF).astype(F32)
+        line = lax.broadcasted_iota(jnp.int32, dots.shape, 0)
+        both = jnp.where(line == 0, dots, jnp.where(line == 1, low, 0.0))
+        out_ref[block, 0, capacity:, :] = jnp.zeros((EXTRA, columns), BF)
+        out_ref[block, 0, capacity:, :capacity] = jnp.concatenate(
+            [both, jnp.zeros_like(both)], axis=0
+        ).astype(BF)
+
+
+def slot_tail_rows(flat, weight, dots, columns, tile=512):
+    held, rows, depth = flat.shape
+    _, blocks, _, capacity = dots.shape
+    return pl.pallas_call(
+        slot_tail_kernel,
+        grid=(held, rows // tile),
+        out_shape=jax.ShapeDtypeStruct((blocks, held, capacity + EXTRA, columns), BF),
+        in_specs=[
+            pl.BlockSpec((1, tile, depth), lambda e, i: (e, i, 0)),
+            pl.BlockSpec((1, columns, depth), lambda e, i: (e, 1, 0)),
+            pl.BlockSpec((1, tile // capacity, 8, capacity), lambda e, i: (e, i, 0, 0)),
+        ],
+        out_specs=pl.BlockSpec(
+            (tile // capacity, 1, capacity + EXTRA, columns), lambda e, i: (i, e, 0, 0)
+        ),
+        cost_estimate=pl.CostEstimate(
+            flops=2 * held * rows * depth * columns,
+            bytes_accessed=4 * held * rows * (depth + columns),
+            transcendentals=0,
+        ),
+        name="slot_tail_rows",
+    )(flat, weight, dots)
+
+
+def slot_rows_kernel(flat_ref, weight_ref, out_ref):
+    out_ref[...] = dot(flat_ref[0], weight_ref[0]).astype(BF).reshape(out_ref.shape)
+
+
+def slot_rows(flat, weight, part, columns, blocks, tile=512):
+    held, rows, depth = flat.shape
     capacity = rows // blocks
-    width = expert_down.shape[2]
-    return pl.pallas_call(
-        down_kernel,
+    return pl.pallas_call(
+        slot_rows_kernel,
         grid=(held, rows // tile),
-        out_shape=jax.ShapeDtypeStruct((blocks, held, capacity, width), BF),
+        out_shape=jax.ShapeDtypeStruct((blocks, held, capacity, columns), BF),
         in_specs=[
-            pl.BlockSpec((1, tile, units), lambda e, i: (e, i, 0)),
-            pl.BlockSpec((1, units, width), lambda e, i: (e, 0, 0)),
+            pl.BlockSpec((1, tile, depth), lambda e, i: (e, i, 0)),
+            pl.BlockSpec((1, depth, columns), lambda e, i: (e, 0, part)),
         ],
         out_specs=pl.BlockSpec(
-            (tile // capacity, 1, capacity, width), lambda e, i: (i, e, 0, 0)
-        ),
-        cost_estimate=pl.CostEstimate(
-            flops=2 * held * rows * units * width,
-            bytes_accessed=6 * held * rows * width,
+            (tile // capacity, 1, capacity, columns), lambda e, i: (i, e, 0, 0)
+        ),
+        cost_estimate=pl.CostEstimate(
+            flops=2 * held * rows * depth * columns,
+            bytes_accessed=4 * held * rows * (depth + columns),
             transcendentals=0,
         ),
-        name="expert_down_rows",
-    )(hidden, expert_down)
+        name="slot_rows",
+    )(flat, weight)
+
+
+def combine_kernel(place_ref, weight_ref, back_ref, base_ref, out_ref):
+    tile, slots = place_ref.shape[0], back_ref.shape[0]
+    pick = lax.broadcasted_iota(jnp.int32, (tile, slots), 1) == place_ref[...]
+    rows = dot(pick.astype(BF), back_ref[...])
+    out_ref[...] = (base_ref[...] + weight_ref[...] * rows).astype(BF)
+
+
+def combine(place, weight, back, base, part, tile=256):
+    slots, columns = back.shape
+    rows = base.shape[0]
+    own = pl.BlockSpec((tile, 1), lambda i: (i, 0))
+    return pl.pallas_call(
+        combine_kernel,
+        grid=(rows // tile,),
+        out_shape=jax.ShapeDtypeStruct((rows, columns), BF),
+        in_specs=[
+            own,
+            own,
+            pl.BlockSpec((slots, columns), lambda i: (0, 0)),
+            pl.BlockSpec((tile, columns), lambda i: (i, part)),
+        ],
+        out_specs=pl.BlockSpec((tile, columns), lambda i: (i, 0)),
+        cost_estimate=pl.CostEstimate(
+            flops=2 * rows * slots * columns,
+            bytes_accessed=2 * slots * columns + 6 * rows * columns,
+            transcendentals=0,
+        ),
+        name="combine",
+    )(place, weight, back, base)
 
 
 def hidden_grad_kernel(grads_ref, down_ref, out_ref):
@@ -338,6 +430,65 @@
         ),
         name="normed_back",
     )(qkv_grad, project_in, tokens)
+
+
+def mid_back_kernel(
+    place_ref, low_half_ref, high_half_ref, gates_ref, rest_ref, cotan_ref, gain_ref, weight_ref,
+    heads_ref, rest_grad_ref, low_ref, sums_ref,
+):
+    grad = jnp.concatenate([low_half_ref[...], high_half_ref[...]], axis=1).astype(F32)
+    grad = grad + gates_ref[...]
+    unit, inverse = norm_stats(rest_ref[...])
+    rest_grad = cotan_ref[...].astype(F32) + norm_back(unit, inverse, gain_ref[...], grad)
+    rest_grad_ref[...] = rest_grad
+    low = rest_grad.astype(BF)
+    low_ref[...] = low
+    for z in range(weight_ref.shape[0]):
+        heads_ref[z] = dot_t(low, weight_ref[z]).astype(BF)
+    sums_ref[0:1, :] = jnp.sum(grad * unit, axis=0, keepdims=True)
+    sums_ref[1:2, :] = jnp.sum(grad, axis=0, keepdims=True)
+
+
+def mid_back(place, mid_grads, gates, residual, cotangent, gain, weight):
+    parts, columns, width = weight.shape
+    rows = mid_grads[0].shape[0]
+    here = lambda i, place: (place[0], 0)
+    whole = lambda i, place: (0, 0)
+    cube = lambda i, place: (0, 0, 0)
+    return pl.pallas_call(
+        mid_back_kernel,
+        grid_spec=pltpu.PrefetchScalarGridSpec(
+            num_scalar_prefetch=1,
+            grid=(1,),
+            in_specs=[
+                pl.BlockSpec((rows, width // 2), whole),
+                pl.BlockSpec((rows, width // 2), whole),
+                pl.BlockSpec((rows, width), whole),
+                pl.BlockSpec((rows, width), here),
+                pl.BlockSpec((rows, width), here),
+                pl.BlockSpec((1, width), whole),
+                pl.BlockSpec((parts, columns, width), cube),
+            ],
+            out_specs=(
+                pl.BlockSpec((parts, rows, columns), cube),
+                pl.BlockSpec((rows, width), whole),
+                pl.BlockSpec((rows, width), whole),
+                pl.BlockSpec((8, width), whole),
+            ),
+        ),
+        out_shape=(
+            jax.ShapeDtypeStruct((parts, rows, columns), BF),
+            jax.ShapeDtypeStruct((rows, width), F32),
+            jax.ShapeDtypeStruct((rows, width), BF),
+            jax.ShapeDtypeStruct((8, width), F32),
+        ),
+        cost_estimate=pl.CostEstimate(
+            flops=2 * rows * parts * columns * width,
+            bytes_accessed=16 * rows * width,
+            transcendentals=rows,
+        ),
+        name="mid_back",
+    )(place[None], *mid_grads, gates, residual, cotangent, gain[None], weight)
 
 
 def local(
@@ -372,30 +523,48 @@
     def mine(rows, axis=0):
         return lax.dynamic_slice_in_dim(rows, my_start, part_rows, axis)
 
-    half = head_columns // 2
-    odd = lax.axis_index("expert") % 2
-    own_half = lax.all_gather(
-        lax.dynamic_slice_in_dim(project_out, odd * half, half, 0), "tensor", axis=0
+    z = lax.axis_index("tensor")
+
+    def shift_tensor(pick):
+        return [
+            lax.ppermute(pick(k), "tensor", [(i, (i + k) % parts) for i in range(parts)])
+            if k
+            else pick(0)
+            for k in range(parts)
+        ]
+
+    def scatter_tensor(rows):
+        return shift_tensor(
+            lambda k: lax.dynamic_index_in_dim(rows, (z + k) % parts, 0, keepdims=False)
+        )
+
+    def in_order(pieces):
+        twice = jnp.stack(pieces[::-1] * 2)
+        return lax.dynamic_slice_in_dim(twice, parts - 1 - z, parts, 0)
+
+    place = lax.axis_index("expert")
+    odd = place % 2
+    far = place // 2 % 2
+    quarter = head_columns // 4
+    own = lax.dynamic_slice_in_dim(project_out, (2 * far + odd) * quarter, quarter, 0)
+    own = lax.all_to_all(
+        jnp.broadcast_to(own[None], (parts,) + own.shape), "tensor", 0, 0, tiled=True
     )
     project_in = jnp.swapaxes(project_in, 0, 1)
     unit_in, _ = norm_stats(tokens.astype(F32))
     normed_low = (unit_in * first_gain + first_shift).astype(BF)
     qkv = jnp.einsum("td,cdn->ctn", normed_low, project_in, preferred_element_type=F32).astype(BF)
     attended, log_total = attend_forward(qkv)
-    attended, own_half = lax.optimization_barrier((attended, own_half))
     attended_all = lax.all_gather(attended, "tensor", axis=0, tiled=True).reshape(
         parts, row_count, head_columns
     )
-
-    swap = [(i, i ^ 1) for i in range(lax.axis_size("expert"))]
-    other_half = lax.ppermute(own_half, "expert", swap)
-    project_out_all = jnp.concatenate(
-        [
-            jnp.where(odd == 0, own_half, other_half),
-            jnp.where(odd == 0, other_half, own_half),
-        ],
-        axis=1,
-    )
+    pairs = [(i, i ^ 1) for i in range(blocks)]
+
+    def from_pair(rows):
+        return lax.ppermute(rows, "expert", pairs)
+
+    def both_sides(side, own, other):
+        return jnp.stack([jnp.where(side == 0, own, other), jnp.where(side == 0, other, own)])
 
     slot_place = jnp.where(slot_index < capacity, routes * capacity + slot_index, slot_total)
     slot_place = after(slot_place, attended)
@@ -408,17 +577,19 @@
     def exchange(buffer):
         return lax.all_to_all(buffer, "expert", 0, 0, tiled=True)
 
-    def from_slots(buffer):
-        return t_dot(pick, buffer.reshape(slot_total, width))
-
-    cotan_slots = exchange(to_slots(cotangent)).reshape(blocks, held, capacity, width)
+    own_far = lax.ppermute(own, "expert", [(i, i ^ 2) for i in range(blocks)])
+    cotan_sent, own_far = lax.optimization_barrier((to_slots(cotangent), own_far))
+    cotan_slots = exchange(cotan_sent).reshape(blocks, held, capacity, width)
+    own_sides = both_sides(far, own, own_far)
+    project_out_all = jnp.transpose(both_sides(odd, own_sides, from_pair(own_sides)), (2, 1, 0, 3, 4))
+    project_out_all = project_out_all.reshape(parts, head_columns, width)
 
     residual, mid_low = project_norm(
         attended_all, project_out_all, tokens, second_gain, second_shift
     )
-    mid_slots = after(to_slots(mid_low), cotan_slots)
+    mid_slots = to_slots(mid_low)
     arrived = exchange(mid_slots).reshape(blocks, held, capacity, width)
-    mid_low = after(mid_low, mid_slots)
+    mid_low = after(mid_low, mid_slots, cotan_slots)
     router_logits = dot(mid_low, router_weight)
     mixing_logits = dot(mid_low, mixing_weight)
     router_probs = jax.nn.softmax(router_logits, axis=-1)
@@ -440,96 +611,126 @@
     dense_dot = jnp.sum(cotan * dense_part, axis=-1, keepdims=True)
 
     hidden_grads = expert_hidden_grad(after(cotan_slots, mid_slots), expert_down)
-    hiddens, pre_grads, in_slots, slot_dots = expert_back(arrived, expert_up, hidden_grads)
-    in_slots = in_slots.reshape(blocks, held * capacity, width)
-    in_home = exchange(in_slots)
-
-    slot_dot = jnp.swapaxes(slot_dots[:, :, 0].reshape(held, blocks, capacity), 0, 1)
-    slot_dot = exchange(after(slot_dot.reshape(blocks, held * capacity), in_slots))
-    slot_dot = slot_dot.reshape(slot_total)
     slot_weight = jnp.sum(jnp.where(hit, expert_weight[:, 0][None, :], 0.0), axis=1)
-    slot_weight = exchange(after(slot_weight, slot_dot).reshape(blocks, held * capacity))
-    slot_weight = slot_weight.reshape(blocks, held, capacity)
-    out_slots = expert_down_rows(after(hiddens, in_slots), expert_down, blocks).reshape(
-        blocks, held * capacity, width
-    )
-    out_home = exchange(after(out_slots, in_home))
-
-    expert_dot = jnp.sum(jnp.where(hit, slot_dot[:, None], 0.0), axis=0)[:, None]
-    gated_dot = gate * expert_dot
-    mean_dot = dense_weight * dense_dot + mixing[:, 1:2] * gated_dot
-    mixing_low = (mixing * (jnp.concatenate([dense_dot, gated_dot], axis=1) - mean_dot)).astype(BF)
-    router_low = (expert_weight * expert_dot * (chosen - router_probs)).astype(BF)
-    mid_part = (
-        mid_dense_part
-        + dot_t(router_low, router_weight)
-        + dot_t(mixing_low, mixing_weight)
-        + expert_weight * from_slots(in_home)
-    )
-    mid_low_part = mid_part.astype(BF)
-    mid_grad = lax.psum_scatter(mid_low_part, "tensor", scatter_dimension=0, tiled=True)
-
-    up_grads, down_grads = [], []
-    for e in range(held):
-        row_weight = after(slot_weight, in_home)[:, e].reshape(blocks * capacity, 1)
-        grads = cotan_slots[:, e].reshape(blocks * capacity, width)
-        rows = arrived[:, e].reshape(blocks * capacity, width)
-        down_grads.append(t_dot(hiddens[e], (grads.astype(F32) * row_weight).astype(BF)))
-        up_grads.append(t_dot(rows, (pre_grads[e].astype(F32) * row_weight).astype(BF)))
-    expert_up_grad = jnp.stack(up_grads)
-    expert_down_grad = jnp.stack(down_grads)
-    out_part = dense_weight * dense_part + expert_weight * from_slots(after(out_home, mid_low_part))
-    out_low = out_part.astype(BF)
-    out_sum = lax.psum_scatter(
-        after(out_low, mid_grad), "tensor", scatter_dimension=0, tiled=True
-    )
-
-    def pack(pieces):
-        return jnp.concatenate([piece.reshape(blocks, -1, width) for piece in pieces], axis=1)
-
-    def unpack(rows, sizes):
-        starts = [sum(sizes[:i]) for i in range(len(sizes))]
-        return [rows[..., s : s + n, :] for s, n in zip(starts, sizes)]
-
-    mid_grad = mid_grad.astype(F32)
-    residual_mine = mine(residual)
-    unit_mine, inverse_mine = norm_stats(residual_mine)
-    second_gain_grad = jnp.sum(mid_grad * unit_mine, axis=0)
-    second_shift_grad = jnp.sum(mid_grad, axis=0)
-    residual_grad = mine(cotangent).astype(F32) + norm_back(
-        unit_mine, inverse_mine, second_gain, mid_grad
-    )
-    attn_grad_low = residual_grad.astype(BF)
-    attended_grad = jnp.einsum(
-        "td,znd->ztn", attn_grad_low, project_out_all, preferred_element_type=F32
+    slot_weight = slot_weight.reshape(blocks, held * capacity)
+    arrived, mid_dense_part, dense_dot, dense_up_grad, dense_down_grad = lax.optimization_barrier(
+        (arrived, mid_dense_part, dense_dot, dense_up_grad, dense_down_grad)
+    )
+    hiddens, pre_grads, low_slots, slot_dots = expert_back(arrived, expert_up, hidden_grads)
+    low_home = exchange(low_slots.reshape(blocks, held * capacity, width // 2))
+    high_slots = slot_tail_rows(after(pre_grads, low_slots), expert_up, slot_dots, width // 2)
+    out_slots = slot_rows(after(hiddens, high_slots), expert_down, 0, width, blocks)
+    high_home = exchange(
+        after(high_slots, out_slots).reshape(blocks, held * (capacity + EXTRA), width // 2)
+    )
+    high_home, out_slots = lax.optimization_barrier((high_home, out_slots))
+    out_home = exchange(out_slots.reshape(blocks, held * capacity, width))
+
+    out_base = dense_weight * dense_part
+    place_column = slot_place[:, None]
+    tail_column = jnp.where(
+        slot_index < capacity, routes * (capacity + EXTRA) + slot_index,
+        expert_count * (capacity + EXTRA),
+    )[:, None]
+
+    def sum_rows(rows):
+        return lax.psum_scatter(rows, "tensor", scatter_dimension=0, tiled=True)
+
+    mid_low_half = combine(
+        place_column, expert_weight, low_home.reshape(slot_total, -1), mid_dense_part, 0
+    )
+    mid_high_half = combine(
+        tail_column,
+        expert_weight,
+        high_home.reshape(expert_count * (capacity + EXTRA), -1),
+        mid_dense_part,
+        1,
+    )
+    mid_grad_low = sum_rows(mid_low_half)
+    mid_grad_high = sum_rows(after(mid_high_half, mid_low_half))
+
+    slot_dot = after(high_home, mid_high_half).reshape(
+        blocks, held, capacity + EXTRA, width // 2
+    )[:, :, capacity : capacity + 2, :capacity]
+    slot_dot = jnp.sum(slot_dot.astype(F32), axis=2).reshape(slot_total)
+    expert_dot = jnp.sum(jnp.where(hit, slot_dot[:, None], 0.0), axis=0)
+    dots = jnp.stack([dense_dot[:, 0], expert_dot]).reshape(2, parts, part_rows)
+    dots = sum(scatter_tensor(jnp.swapaxes(dots, 0, 1)))[:, :, None]
+    dense_dot, expert_dot = dots[0], dots[1]
+    gate_mine, mixing_mine = mine(gate), mine(mixing)
+    gated_dot = gate_mine * expert_dot
+    mean_dot = mixing_mine[:, 0:1] * dense_dot + mixing_mine[:, 1:2] * gated_dot
+    mixing_low = (
+        mixing_mine * (jnp.concatenate([dense_dot, gated_dot], axis=1) - mean_dot)
     ).astype(BF)
-    dense_sent = after(
-        pack([dense_up_grad.astype(BF), dense_down_grad.astype(BF)]), out_home, attended_grad
-    )
-    attended_grad = lax.all_to_all(attended_grad, "tensor", 0, 0, tiled=True).reshape(
-        row_count, head_columns
-    )
-    dense_got = exchange(dense_sent)
+    router_low = (
+        mixing_mine[:, 1:2] * gated_dot * (mine(chosen) - mine(router_probs))
+    ).astype(BF)
+    gates_mine = dot_t(router_low, router_weight) + dot_t(mixing_low, mixing_weight)
+
+    chips = blocks // 2
+    same_core = [[2 * i + core for i in range(chips)] for core in range(2)]
+
+    def exchange_chips(buffer):
+        return lax.all_to_all(
+            buffer, "expert", 0, 0, tiled=True, axis_index_groups=same_core
+        )
+
+    def split(rows):
+        return rows.reshape(2, chips, -1, width)
+
+    def pair_sum(rows):
+        sent = lax.dynamic_index_in_dim(rows, 1 - odd, 0, keepdims=False)
+        kept = lax.dynamic_index_in_dim(rows, odd, 0, keepdims=False)
+        return (kept.astype(F32) + from_pair(sent).astype(F32)).astype(BF)
+
+    def spread(piece):
+        got = exchange_chips(jnp.broadcast_to(piece[None], (chips,) + piece.shape))
+        return got, from_pair(got)
+
+    dense_half = pair_sum(
+        jnp.concatenate([split(dense_up_grad.astype(BF)), split(dense_down_grad.astype(BF))], axis=2)
+    )
+    dense_got = exchange_chips(after(dense_half, out_home))
+
+    attended_grad, residual_grad, attn_grad_low, second_sums = mid_back(
+        lax.axis_index("tensor"),
+        (mid_grad_low, mid_grad_high),
+        gates_mine,
+        residual,
+        cotangent,
+        second_gain,
+        project_out_all,
+    )
+    attended_grad_sent = attended_grad
+    out_sum = sum_rows(
+        combine(
+            place_column,
+            expert_weight,
+            after(out_home, attended_grad_sent).reshape(slot_total, -1),
+            out_base,
+            0,
+        )
+    )
+    attended_grad = in_order(scatter_tensor(attended_grad)).reshape(row_count, head_columns)
+    project_out_grad = jnp.einsum(
+        "ztn,td->znd",
+        mine(attended_all, 1),
+        after(attn_grad_low, attended_grad_sent),
+        preferred_element_type=F32,
+    ).astype(BF)
+    dense_piece = jnp.sum(after(dense_got, attended_grad_sent).astype(F32), axis=0).astype(BF)
     qkv_grad = attend_backward(qkv, log_total, attended_grad)
-    normed_low_part, first_sums = normed_back(qkv_grad, project_in, tokens)
-    normed_grad = lax.psum_scatter(
-        after(normed_low_part, out_sum), "tensor", scatter_dimension=0, tiled=True
-    )
+    normed_low_part, first_sums = normed_back(after(qkv_grad, dense_got), project_in, tokens)
+    slot_weight = exchange(after(slot_weight, normed_low_part)).reshape(blocks, held, capacity)
     late_residual, late_sum = lax.optimization_barrier(
         (residual, out_sum, normed_low_part)
     )[:2]
     layer_mine = (mine(late_residual) + late_sum.astype(F32)).astype(BF)
-    normed_grad_f32 = normed_grad.astype(F32)
-    unit_first, inverse_first = norm_stats(mine(tokens).astype(F32))
-    input_mine = residual_grad + norm_back(unit_first, inverse_first, first_gain, normed_grad_f32)
-    both_mine = jnp.stack([layer_mine, input_mine.astype(BF)])
-
-    project_out_grad = jnp.einsum(
-        "ztn,td->znd", mine(attended_all, 1), attn_grad_low, preferred_element_type=F32
-    ).astype(BF)
-    project_out_grad = jnp.swapaxes(
-        project_out_grad.reshape(parts, blocks, head_columns // blocks, width), 0, 1
-    ).reshape(parts * head_columns, width)
+    layer_out = lax.all_gather(layer_mine, "tensor", axis=0, tiled=True)
+    normed_grad = lax.psum_scatter(
+        after(normed_low_part, layer_mine), "tensor", scatter_dimension=0, tiled=True
+    )
     project_in_grad = (
         jnp.einsum(
             "ctn,td->cnd", after(qkv_grad, normed_low_part), normed_low,
@@ -538,56 +739,74 @@
         .astype(BF)
         .reshape(3 * head_columns, width)
     )
-    router_grad = t_dot(router_low, mid_low)
-    mixing_grad = t_dot(mixing_low, mid_low)
     small = jnp.concatenate(
         [
             first_sums[:2],
-            jnp.stack([second_gain_grad, second_shift_grad]),
-            router_grad,
-            mixing_grad,
+            second_sums[:2],
+            t_dot(after(router_low, attended_grad_sent), mine(mid_low)),
+            t_dot(after(mixing_low, attended_grad_sent), mine(mid_low)),
         ],
         axis=0,
     )
-    small_rows = small.shape[0]
-    each = -(-small_rows // blocks)
-    small = jnp.pad(small, ((0, each * blocks - small_rows), (0, 0))).reshape(blocks, each, width)
-    small = jnp.pad(small, ((0, 0), (0, 16 - each), (0, 0))).astype(BF)
-    rest_sent = pack([project_in_grad, project_out_grad, small.reshape(blocks * 16, width)])
-    rest_got = exchange(after(rest_sent, dense_got))
-    dense_got, rest_got, both_mine = lax.optimization_barrier((dense_got, rest_got, both_mine))
-    both = lax.all_gather(both_mine, "tensor", axis=0)
-    layer_out = both[:, 0].reshape(row_count, width)
-    input_grad = both[:, 1].reshape(row_count, width)
-    dense_piece = jnp.sum(dense_got.astype(F32), axis=0)
-    project_in_piece, project_out_piece, small_piece = unpack(
-        jnp.sum(rest_got.astype(F32), axis=0),
-        [3 * head_columns // blocks, parts * head_columns // blocks, 16],
-    )
+    each = -(-small.shape[0] // blocks)
+    small = jnp.pad(small, ((0, each * blocks - small.shape[0]), (0, 0)))
+    small = jnp.pad(small.reshape(blocks, each, width), ((0, 0), (0, 16 - each), (0, 0)))
+    out_rows = head_columns // blocks
+    rest = jnp.concatenate(
+        [
+            split(project_in_grad),
+            jnp.transpose(
+                project_out_grad.reshape(parts, 2, chips, out_rows, width), (1, 2, 0, 3, 4)
+            ).reshape(2, chips, parts * out_rows, width),
+            split(small.astype(BF)),
+        ],
+        axis=2,
+    )
+    rest_half = pair_sum(rest)
+    rest_got = exchange_chips(after(rest_half, dense_piece, slot_weight))
+    rest_piece = jnp.sum(rest_got.astype(F32), axis=0).astype(BF)
+    dense = exchange_chips(
+        jnp.broadcast_to(after(dense_piece, rest_piece)[None], (chips,) + dense_piece.shape)
+    )
+
+    normed_grad = after(normed_grad, layer_out, rest_piece).astype(F32)
+    unit_first, inverse_first = norm_stats(mine(tokens).astype(F32))
+    input_mine = residual_grad + norm_back(unit_first, inverse_first, first_gain, normed_grad)
+    input_mine = input_mine.astype(BF)
+    up_grads, down_grads = [], []
+    for e in range(held):
+        row_weight = slot_weight[:, e].reshape(blocks * capacity, 1)
+        down_weight = after(row_weight, rest_half)
+        up_weight = after(row_weight, input_mine)
+        grads = cotan_slots[:, e].reshape(blocks * capacity, width)
+        rows = arrived[:, e].reshape(blocks * capacity, width)
+        down_grads.append(t_dot(hiddens[e], (grads.astype(F32) * down_weight).astype(BF)))
+        up_grads.append(t_dot(rows, (pre_grads[e].astype(F32) * up_weight).astype(BF)))
+    expert_up_grad = jnp.stack(up_grads)
+    expert_down_grad = jnp.stack(down_grads)
+    input_grad = lax.all_gather(input_mine, "tensor", axis=0, tiled=True)
+
+    in_rows = 3 * out_rows
     across = jnp.concatenate(
         [
-            project_out_piece.reshape(parts, head_columns // blocks, width),
-            jnp.broadcast_to(small_piece[None], (parts, 16, width)),
+            rest_piece[in_rows:-16].reshape(parts, out_rows, width),
+            jnp.broadcast_to(rest_piece[None, -16:], (parts, 16, width)),
         ],
         axis=1,
-    ).astype(BF)
-    across = jnp.sum(
-        lax.all_to_all(across, "tensor", 0, 0, tiled=True).astype(F32), axis=0
-    )
-    project_out_piece = across[: head_columns // blocks]
-    small_piece = across[head_columns // blocks :]
-    pieces = jnp.concatenate(
-        [project_in_piece, project_out_piece, small_piece, dense_piece], axis=0
-    ).astype(BF)
-    sizes = [
-        piece.shape[0] for piece in (project_in_piece, project_out_piece, small_piece)
-    ] + [dense_piece.shape[0] // 2] * 2
-    spread = exchange(jnp.broadcast_to(pieces[None], (blocks,) + pieces.shape))
-    project_in_grad, project_out_grad, small, dense_up_grad, dense_down_grad = [
-        piece.reshape(-1, width).astype(F32) for piece in unpack(spread, sizes)
-    ]
-    project_in_grad = jnp.transpose(project_in_grad.reshape(3, head_columns, width), (2, 0, 1))
-    small = small.reshape(blocks, 16, width)[:, :each].reshape(blocks * each, width)
+    )
+    across = after(scatter_tensor(across), input_mine)
+    across = sum(piece.astype(F32) for piece in across).astype(BF)
+    dense = after(dense, input_mine)
+    dense_other = from_pair(dense)
+    rest, rest_other = spread(jnp.concatenate([rest_piece[:in_rows], across], axis=0))
+    rest = both_sides(odd, rest, rest_other).reshape(blocks, -1, width)
+    dense = both_sides(odd, dense, dense_other).reshape(blocks, 2, -1, width)
+    dense_up_grad = dense[:, 0].astype(F32).reshape(width, width)
+    dense_down_grad = dense[:, 1].astype(F32).reshape(width, width)
+    project_in_grad = rest[:, :in_rows].astype(F32).reshape(3, head_columns, width)
+    project_in_grad = jnp.transpose(project_in_grad, (2, 0, 1))
+    project_out_grad = rest[:, in_rows:-16].astype(F32).reshape(head_columns, width)
+    small = rest[:, -16:][:, :each].astype(F32).reshape(blocks * each, width)
 
     return (
         layer_out,

time: 603 us -> 538 us (0.89)
  waiting for transfers between devices: 272 us -> 161 us
  Pallas kernels: 71 us -> 103 us
  matrix products: 97.5 us -> 79.5 us
  starting transfers between devices: 50.5 us -> 67.7 us
  local copies, waits for them, and re-layouts: 33.8 us -> 42.1 us
  other arithmetic: 54.8 us -> 61.1 us
    all_to_all x9 -> x6, waiting for transfers between devices: 165 us -> 42.7 us  [exchange(): return lax.all_to_all(buffer, 'expert', 0, 0, tiled=True)]
    reduce_scatter x3 -> x4, waiting for transfers between devices: 8.08 us -> 45.9 us  [the longest x1 25.1 us: local(): lax.psum_scatter(after(normed_low_part, layer_mine), 'tensor', scatter_di...]
    pallas_call x1 -> x6, Pallas kernels: 9.14 us -> 42.6 us  [the longest x3 21.9 us: combine(): pl.pallas_call(combine_kernel, grid=(rows // tile,), out_shape=jax.ShapeD...]
    all_gather x2, waiting for transfers between devices: 31.1 us -> 11.1 us  [the longest x1 11.1 us: local(): input_grad = lax.all_gather(input_mine, 'tensor', axis=0, tiled=True)]
    ppermute x1 -> x15, starting transfers between devices: 0.5 us -> 18.9 us  [the longest x9 16.8 us: shift_tensor(): lax.ppermute(pick(k), 'tensor', [(i, (i + k) % parts) for i in range(part...]
    ppermute x1 -> x15, waiting for transfers between devices: 3.09 us -> 21.1 us  [the longest x9 14.2 us: shift_tensor(): lax.ppermute(pick(k), 'tensor', [(i, (i + k) % parts) for i in range(part...]
    all_to_all x2 -> x5, waiting for transfers between devices: 37.8 us -> 20.5 us  [the longest x4 20.5 us: exchange_chips(): lax.all_to_all(buffer, 'expert', 0, 0, tiled=True, axis_index_groups=same...]
    all_to_all x9 -> x6, starting transfers between devices: 41.2 us -> 25.6 us  [exchange(): return lax.all_to_all(buffer, 'expert', 0, 0, tiled=True)]
  transfers between devices with their start and end apart: 18 -> 33, of which waited for: 15 -> 16; matrix products, arithmetic and copies ran while one was open for 27% -> 31% of each run, Pallas kernels for 9% -> 17%
where the time goes in v2:
time: 538 us; the launch traced here: 529 us
  waiting for transfers between devices  161 us (30%)
  Pallas kernels  103 us (19%)
  matrix products  79.5 us (15%)
  starting transfers between devices  67.7 us (13%)
  other arithmetic  61.1 us (11%)
  local copies, waits for them, and re-layouts  42.1 us (8%)
  between operations  15.3 us (3%)
    all_to_all x6, waiting for transfers between devices, exchange(): return lax.all_to_all(buffer, 'expert', 0, 0, tiled=True)  42.7 us
    dot_general x6, matrix products, dot(): return jnp.dot(a, b, preferred_element_type=F32)  30.5 us
    dot_general x8, matrix products, t_dot(): lax.dot_general(a, b, (((0,), (0,)), ((), ())), preferred_element_type=F32)  27.5 us
    all_to_all x6, starting transfers between devices, exchange(): return lax.all_to_all(buffer, 'expert', 0, 0, tiled=True)  25.6 us
    reduce_scatter x1, waiting for transfers between devices, local(): lax.psum_scatter(after(normed_low_part, layer_mine), 'tensor', scatter_di...  25.1 us
    pallas_call x3, Pallas kernels, combine(): pl.pallas_call(combine_kernel, grid=(rows // tile,), out_shape=jax.ShapeD...  21.9 us
    reduce_scatter x3, waiting for transfers between devices, sum_rows(): return lax.psum_scatter(rows, 'tensor', scatter_dimension=0, tiled=True)  20.7 us
    all_to_all x4, waiting for transfers between devices, exchange_chips(): lax.all_to_all(buffer, 'expert', 0, 0, tiled=True, axis_index_groups=same...  20.5 us
  transfers between devices with their start and end apart: 33, of which 16 were waited for; matrix products, arithmetic and copies ran while one was open for 31% of the time, Pallas kernels for 17%

profile of v2, /device:TPU:0, one launch (start us, length us, event | category | flops | bytes accessed | tf_op | source)
XLA Modules:
  0.0 529.4 jit_solution(1017410027544823524)
XLA Ops:
  9.2 6.3 %all-to-all-start = ((bf16[4,64,1024]{2,1,0:T(8,128)(2,1)}), bf16[4,64,1024]{2,1,0:T(8,128)(2,1)S(1)}, u32[]{:S(2)}, u32[]{:S(2)}) async-start(bf16[4,64,1024]{2,1,0:T(8,128)(2,1)} %broadcast_in_dim.55), calls=%async_computation | async-start | bytes 1048576 | tf_op jit(solution)/shard_map/all_to_all | solution.py:550
  21.8 9.8 %attend_forward.1 = (bf16[1024,256]{1,0:T(8,128)(2,1)}, f32[2,8,1024]{2,1,0:T(8,128)}) custom-call(bf16[3,1024,256]{2,1,0:T(8,128)(2,1)} %fusion.35.qkv_ref), custom_call_target="tpu_custom_call" | custom-call | flops 1073741824 | bytes 2097152 | tf_op jit(solution)/shard_map/attend_forward/pallas_call | solution.py:125
  33.2 7.6 %fusion.16 = bf16[2048,1024]{1,0:T(8,128)(2,1)} fusion(bf16[1024,1024]{1,0:T(8,128)(2,1)} %cotan_ref.1, s32[1024]{0:T(1024)S(1)} %get-tuple-element.70), kind=kOutput, calls=%fused_computation.41 | convolution fusion | flops 4299161600 | bytes 6295552 | tf_op jit(solution)/shard_map/dot_general | solution.py:48
  45.9 4.8 all-to-all-start.1
  59.0 19.8 %all-gather.4.cloned.1.call-done = bf16[4096,256]{1,0:T(8,128)(2,1)} async-done(((bf16[1024,256]{1,0:T(8,128)(2,1)}), bf16[4096,256]{1,0:T(8,128)(2,1)}) %all-gather.4.cloned.1.call-update) | async-done | bytes 2097168 | tf_op jit(solution)/shard_map/all_gather | solution.py:558
  78.8 7.4 %project_norm.1 = (f32[1024,1024]{1,0:T(8,128)}, bf16[1024,1024]{1,0:T(8,128)(2,1)}) custom-call(bf16[4,1024,256]{2,1,0:T(8,128)(2,1)} %bitcast.228, bf16[4,256,1024]{2,1,0:T(8,128)(2,1)} %bitcast.211, bf16[1024,1024]{1,0:T(8,128)(2,1)} %token_ref.3, f32[1,1024]{1,0:T(1,128)} %bitcast.241, f32[1,1024]{1,0:T(1,128)} %bitcast.253), custom_call_target="tpu_custom_call" | custom-call | flops 2147483648 | bytes 12582912 | tf_op jit(solution)/shard_map/project_norm/pallas_call | solution.py:177
  86.2 7.6 %fusion.17 = bf16[2048,1024]{1,0:T(8,128)(2,1)} fusion(bf16[1024,1024]{1,0:T(8,128)(2,1)} %get-tuple-element.75, s32[1024]{0:T(1024)S(1)} %get-tuple-element.70), kind=kOutput, calls=%fused_computation.42 | convolution fusion | flops 4299161600 | bytes 6295552 | tf_op jit(solution)/shard_map/dot_general | solution.py:48
  93.8 6.0 %all-to-all-done.1 = bf16[8,256,1024]{2,1,0:T(8,128)(2,1)} async-done(((bf16[8,256,1024]{2,1,0:T(8,128)(2,1)}), bf16[8,256,1024]{2,1,0:T(8,128)(2,1)}, u32[]{:S(2)}, u32[]{:S(2)}) %all-to-all-start.1) | async-done | bytes 4194336 | tf_op jit(solution)/shard_map/all_to_all | solution.py:578
  110.3 6.6 %fusion.93 = f32[1024,1024]{1,0:T(8,128)} fusion(bf16[1024,1024]{1,0:T(8,128)(2,1)} %get-tuple-element.75, bf16[1024,1024]{1,0:T(8,128)(2,1)} %param.28), kind=kOutput, calls=%fused_computation.206 | convolution fusion | flops 2147483648 | bytes 8388608 | tf_op jit(solution)/shard_map/dot_general | solution.py:48
  117.9 9.1 %expert_hidden_grad.1.hidden_grad_ref = bf16[2,1024,1024]{2,1,0:T(8,128)(2,1)} custom-call(bf16[8,2,128,1024]{3,2,1,0:T(8,128)(2,1)} %bitcast.17.grads_ref, bf16[2,1024,1024]{2,1,0:T(8,128)(2,1)} %weight_ref.3), custom_call_target="tpu_custom_call" | custom-call | flops 4294967296 | bytes 12582912 | tf_op jit(solution)/shard_map/expert_hidden_grad/pallas_call | solution.py:374
  127.0 6.9 %fusion.11 = bf16[1024,1024]{1,0:T(8,128)(2,1)S(1)} fusion(f32[1024,1024]{1,0:T(8,128)} %fusion.93, bf16[1024,1024]{1,0:T(8,128)(2,1)S(1)} %copy-done, bf16[1024,1024]{1,0:T(8,128)(2,1)} %cotan_ref.1, f32[1024]{0:T(1024)S(1)} %get-tuple-element.209), kind=kOutput, calls=%fused_computation.25 | convolution fusion | flops 2166358016 | bytes 10489856 | tf_op jit(solution)/shard_map/dot_general | solution.py:51
  153.6 14.7 %expert_back.1 = (bf16[2,1024,1024]{2,1,0:T(8,128)(2,1)}, bf16[2,1024,1024]{2,1,0:T(8,128)(2,1)}, bf16[8,2,128,512]{3,2,1,0:T(8,128)(2,1)}, f32[2,8,8,128]{3,2,1,0:T(8,128)}) custom-call(bf16[8,2,128,1024]{3,2,1,0:T(8,128)(2,1)} %bitcast.19.rows_ref, bf16[2,1024,1024]{2,1,0:T(8,128)(2,1)} %weight_ref.2, bf16[2,1024,1024]{2,1,0:T(8,128)(2,1)} %expert_hidden_grad.1.hidden_grad_ref), custom_call_target="tpu_custom_call" | custom-call | flops 6442450944 | bytes 27262976 | tf_op jit(solution)/shard_map/expert_back/pallas_call | solution.py:234
  172.1 6.6 %slot_tail_rows.1 = bf16[8,2,144,512]{3,2,1,0:T(8,128)(2,1)} custom-call(bf16[2,1024,1024]{2,1,0:T(8,128)(2,1)} %get-tuple-element.80.flat_ref, bf16[2,1024,1024]{2,1,0:T(8,128)(2,1)} %weight_ref.2, f32[2,8,8,128]{3,2,1,0:T(8,128)} %get-tuple-element.81.dot_ref), custom_call_target="tpu_custom_call" | custom-call | flops 2147483648 | bytes 12582912 | tf_op jit(solution)/shard_map/slot_tail_rows/pallas_call | solution.py:285
  178.7 9.1 %slot_rows.1 = bf16[8,2,128,1024]{3,2,1,0:T(8,128)(2,1)} custom-call(bf16[2,1024,1024]{2,1,0:T(8,128)(2,1)} %get-tuple-element.83.flat_ref, bf16[2,1024,1024]{2,1,0:T(8,128)(2,1)} %weight_ref.3), custom_call_target="tpu_custom_call" | custom-call | flops 4294967296 | bytes 16777216 | tf_op jit(solution)/shard_map/slot_rows/pallas_call | solution.py:313
  187.8 10.9 %all-to-all-done.5 = bf16[8,256,512]{2,1,0:T(8,128)(2,1)S(1)} async-done(((bf16[8,256,512]{2,1,0:T(8,128)(2,1)}), bf16[8,256,512]{2,1,0:T(8,128)(2,1)S(1)}, u32[]{:S(2)}, u32[]{:S(2)}) %all-to-all-start.5) | async-done | bytes 2097184 | tf_op jit(solution)/shard_map/all_to_all | solution.py:578
  205.5 6.3 %combine.3 = bf16[1024,512]{1,0:T(8,128)(2,1)} custom-call(s32[1024,1]{1,0:T(8,128)} %copy.99.place_ref, f32[1024,1]{1,0:T(8,128)} %get-tuple-element.187.weight_ref, bf16[2048,512]{1,0:T(8,128)(2,1)} %bitcast.214, f32[1024,1024]{1,0:T(8,128)} %fusion.94.base_ref), custom_call_target="tpu_custom_call" | custom-call | flops 2147483648 | bytes 5242880 | tf_op jit(solution)/shard_map/combine/pallas_call | solution.py:344
  211.7 22.1 %all-to-all-done.3 = bf16[8,288,512]{2,1,0:T(8,128)(2,1)} async-done(((bf16[8,288,512]{2,1,0:T(8,128)(2,1)}), bf16[8,288,512]{2,1,0:T(8,128)(2,1)}, u32[]{:S(2)}, u32[]{:S(2)}) %all-to-all-start.3) | async-done | bytes 2359328 | tf_op jit(solution)/shard_map/all_to_all | solution.py:578
  240.8 6.7 %combine.4 = bf16[1024,512]{1,0:T(8,128)(2,1)} custom-call(s32[1024,1]{1,0:T(8,128)} %copy.94.place_ref, f32[1024,1]{1,0:T(8,128)} %get-tuple-element.187.weight_ref, bf16[2304,512]{1,0:T(8,128)(2,1)} %bitcast.27.back_ref, f32[1024,1024]{1,0:T(8,128)} %fusion.94.base_ref), custom_call_target="tpu_custom_call" | custom-call | flops 2415919104 | bytes 5505024 | tf_op jit(solution)/shard_map/combine/pallas_call | solution.py:344
  261.5 20.7 %reduce-scatter.7.cloned.1.call-done.high_half_ref = bf16[256,512]{1,0:T(8,128)(2,1)} async-done(((bf16[1024,512]{1,0:T(8,128)(2,1)}), bf16[256,512]{1,0:T(8,128)(2,1)}) %reduce-scatter.7.cloned.1.call-update) | async-done | bytes 262160 | tf_op jit(solution)/shard_map/reduce_scatter | solution.py:637
  282.2 5.0 mid_back.1
  287.5 9.0 %combine.5 = bf16[1024,1024]{1,0:T(8,128)(2,1)} custom-call(s32[1024,1]{1,0:T(8,128)} %copy.99.place_ref, f32[1024,1]{1,0:T(8,128)} %get-tuple-element.187.weight_ref, bf16[2048,1024]{1,0:T(8,128)(2,1)} %bitcast.34.back_ref, f32[1024,1024]{1,0:T(8,128)} %get-tuple-element.198.base_ref), custom_call_target="tpu_custom_call" | custom-call | flops 4294967296 | bytes 10485760 | tf_op jit(solution)/shard_map/combine/pallas_call | solution.py:344
  311.6 13.3 %collective-permute-done.6 = bf16[256,256]{1,0:T(8,128)(2,1)S(1)} collective-permute-done((bf16[256,256]{1,0:T(8,128)(2,1)S(1)}, bf16[256,256]{1,0:T(8,128)(2,1)S(1)}, u32[]{:S(2)}, u32[]{:S(2)}) %collective-permute-start.6) | collective-permute-done | bytes 131104 | tf_op jit(solution)/shard_map/ppermute | solution.py:530
  331.5 12.2 %attend_backward.1.grad_ref = bf16[3,1024,256]{2,1,0:T(8,128)(2,1)} custom-call(bf16[3,1024,256]{2,1,0:T(8,128)(2,1)} %fusion.35.qkv_ref, f32[2,8,1024]{2,1,0:T(8,128)} %get-tuple-element.93.log_ref, bf16[1024,256]{1,0:T(8,128)(2,1)} %bitcast.227), custom_call_target="tpu_custom_call" | custom-call | flops 2684354560 | bytes 4194304 | tf_op jit(solution)/shard_map/attend_backward/pallas_call | solution.py:146
  343.7 7.0 %normed_back.1 = (bf16[1024,1024]{1,0:T(8,128)(2,1)}, f32[8,1024]{1,0:T(8,128)}) custom-call(bf16[3,1024,256]{2,1,0:T(8,128)(2,1)} %attend_backward.1.grad_ref, bf16[3,1024,256]{2,1,0:T(8,128)(2,1)} %bitcast.252, bf16[1024,1024]{1,0:T(8,128)(2,1)} %token_ref.3), custom_call_target="tpu_custom_call" | custom-call | flops 1610612736 | bytes 6291456 | tf_op jit(solution)/shard_map/normed_back/pallas_call | solution.py:410
  382.5 4.9 fusion.87
  391.4 14.9 %all-to-all-done.8 = bf16[4,240,1024]{2,1,0:T(8,128)(2,1)} async-done(((bf16[4,240,1024]{2,1,0:T(8,128)(2,1)}), bf16[4,240,1024]{2,1,0:T(8,128)(2,1)}, u32[]{:S(2)}, u32[]{:S(2)}) %all-to-all-start.8) | async-done | bytes 1966112 | tf_op jit(solution)/shard_map/all_to_all | solution.py:675
  414.4 6.7 %convolution_bitcast_fusion = f32[1,1024,1024]{2,1,0:T(8,128)} fusion(bf16[1024,1024]{1,0:T(8,128)(2,1)} %bitcast.220, bf16[2,1024,1024]{2,1,0:T(8,128)(2,1)} %get-tuple-element.83.flat_ref), kind=kOutput, calls=%fused_computation.45 | convolution fusion | flops 2147483648 | bytes 8388608 | tf_op jit(solution)/shard_map/dot_general | solution.py:40
  421.1 6.2 %collective-permute-start.12 = (bf16[48,1024]{1,0:T(8,128)(2,1)S(1)}, bf16[48,1024]{1,0:T(8,128)(2,1)S(1)}, u32[]{:S(2)}, u32[]{:S(2)}) collective-permute-start(bf16[48,1024]{1,0:T(8,128)(2,1)S(1)} %get-tuple-element.210), channel_id=1, source_target_pairs={{0,3},{1,0},{2,1},{3,2},{4,7},{5,4},{6,5},{7,6},{8,11},{9,8},{10,9... | collective-permute-start | bytes 294920 | tf_op jit(solution)/shard_map/ppermute | solution.py:530
  428.0 25.1 %reduce-scatter.11.cloned.1.call-done = bf16[256,1024]{1,0:T(8,128)(2,1)} async-done(((bf16[1024,1024]{1,0:T(8,128)(2,1)}), bf16[256,1024]{1,0:T(8,128)(2,1)}) %reduce-scatter.11.cloned.1.call-update) | async-done | bytes 524304 | tf_op jit(solution)/shard_map/reduce_scatter | solution.py:731
  471.2 5.6 %all-to-all-done.9 = bf16[4,144,1024]{2,1,0:T(8,128)(2,1)S(1)} async-done(((bf16[4,144,1024]{2,1,0:T(8,128)(2,1)}), bf16[4,144,1024]{2,1,0:T(8,128)(2,1)S(1)}, u32[]{:S(2)}, u32[]{:S(2)}) %all-to-all-start.9) | async-done | bytes 1179680 | tf_op jit(solution)/shard_map/all_to_all | solution.py:675
  476.8 5.0 convolution_bitcast_fusion.3
  506.8 11.1 %all-gather.8.cloned.1.call-done = bf16[1024,1024]{1,0:T(8,128)(2,1)} async-done(((bf16[256,1024]{1,0:T(8,128)(2,1)}), bf16[1024,1024]{1,0:T(8,128)(2,1)}) %all-gather.8.cloned.1.call-update) | async-done | bytes 2097168 | tf_op jit(solution)/shard_map/all_gather | solution.py:787
  (244 shorter events, 199.2 us)
Async XLA Ops:
  9.2 22.4 %all-to-all-start = ((bf16[4,64,1024]{2,1,0:T(8,128)(2,1)}), bf16[4,64,1024]{2,1,0:T(8,128)(2,1)S(1)}, u32[]{:S(2)}, u32[]{:S(2)}) async-start(bf16[4,64,1024]{2,1,0:T(8,128)(2,1)} %broadcast_in_dim.55), calls=%async_computation | async-start | bytes 1048576 | tf_op jit(solution)/shard_map/all_to_all | solution.py:550
  15.5 63.3 %all-gather.4.cloned.1.call-start = ((), (), s32[]{:S(2)}) async-start(), calls=%async_computation.15 | async-start | bytes 2621440 | tf_op jit(solution)/shard_map/all_gather | solution.py:558
  31.6 13.5 %collective-permute-start = (bf16[4,64,1024]{2,1,0:T(8,128)(2,1)S(1)}, bf16[4,64,1024]{2,1,0:T(8,128)(2,1)S(1)}, u32[]{:S(2)}, u32[]{:S(2)}) collective-permute-start(bf16[4,64,1024]{2,1,0:T(8,128)(2,1)S(1)} %all-to-all-done), channel_id=1, source_target_pairs={{0,8},{4,12},{8,0},{12,4},{16,24},{20,28},{24,16},{28,20},{1,9},{5... | collective-permute-start | bytes 1572872 | tf_op jit(solution)/shard_map/ppermute | solution.py:580
  45.9 54.0 %all-to-all-start.1 = ((bf16[8,256,1024]{2,1,0:T(8,128)(2,1)}), bf16[8,256,1024]{2,1,0:T(8,128)(2,1)}, u32[]{:S(2)}, u32[]{:S(2)}) async-start(bf16[8,256,1024]{2,1,0:T(8,128)(2,1)} %bitcast.218), calls=%async_computation.1 | async-start | bytes 8388608 | tf_op jit(solution)/shard_map/all_to_all | solution.py:578
  99.8 53.8 %all-to-all-start.2 = ((bf16[8,256,1024]{2,1,0:T(8,128)(2,1)}), bf16[8,256,1024]{2,1,0:T(8,128)(2,1)}, u32[]{:S(2)}, u32[]{:S(2)}) async-start(bf16[8,256,1024]{2,1,0:T(8,128)(2,1)} %bitcast.217), calls=%async_computation.2 | async-start | bytes 8388608 | tf_op jit(solution)/shard_map/all_to_all | solution.py:578
  168.3 30.3 %all-to-all-start.5 = ((bf16[8,256,512]{2,1,0:T(8,128)(2,1)}), bf16[8,256,512]{2,1,0:T(8,128)(2,1)S(1)}, u32[]{:S(2)}, u32[]{:S(2)}) async-start(bf16[8,256,512]{2,1,0:T(8,128)(2,1)} %bitcast.221), calls=%async_computation.5 | async-start | bytes 4194304 | tf_op jit(solution)/shard_map/all_to_all | solution.py:578
  200.0 33.8 %all-to-all-start.3 = ((bf16[8,288,512]{2,1,0:T(8,128)(2,1)}), bf16[8,288,512]{2,1,0:T(8,128)(2,1)}, u32[]{:S(2)}, u32[]{:S(2)}) async-start(bf16[8,288,512]{2,1,0:T(8,128)(2,1)} %bitcast.202), calls=%async_computation.3 | async-start | bytes 4718592 | tf_op jit(solution)/shard_map/all_to_all | solution.py:578
  204.4 57.1 %reduce-scatter.5.cloned.1.call-start = ((), (), s32[]{:S(2)}) async-start(), calls=%async_computation.16 | async-start | bytes 1310720 | tf_op jit(solution)/shard_map/reduce_scatter | solution.py:637
  233.8 53.7 %all-to-all-start.4 = ((bf16[8,256,1024]{2,1,0:T(8,128)(2,1)}), bf16[8,256,1024]{2,1,0:T(8,128)(2,1)}, u32[]{:S(2)}, u32[]{:S(2)}) async-start(bf16[8,256,1024]{2,1,0:T(8,128)(2,1)} %bitcast.216), calls=%async_computation.4 | async-start | bytes 8388608 | tf_op jit(solution)/shard_map/all_to_all | solution.py:578
  238.4 43.8 %reduce-scatter.7.cloned.1.call-start = ((), (), s32[]{:S(2)}) async-start(), calls=%async_computation.17 | async-start | bytes 1310720 | tf_op jit(solution)/shard_map/reduce_scatter | solution.py:637
  250.6 8.4 %collective-permute-start.2 = (f32[2,256]{1,0:T(2,128)S(1)}, f32[2,256]{1,0:T(2,128)S(1)}, u32[]{:S(2)}, u32[]{:S(2)}) collective-permute-start(f32[2,256]{1,0:T(2,128)S(1)} %bitcast.251), channel_id=1, source_target_pairs={{0,1},{1,2},{2,3},{3,0},{4,5},{5,6},{6,7},{7,4},{8,9},{9,10},{10,1... | collective-permute-start | bytes 6152 | tf_op jit(solution)/shard_map/ppermute | solution.py:530
  252.4 6.6 %collective-permute-start.3 = (f32[2,256]{1,0:T(2,128)S(1)}, f32[2,256]{1,0:T(2,128)S(1)}, u32[]{:S(2)}, u32[]{:S(2)}) collective-permute-start(f32[2,256]{1,0:T(2,128)S(1)} %bitcast.250), channel_id=1, source_target_pairs={{0,2},{1,3},{2,0},{3,1},{4,6},{5,7},{6,4},{7,5},{8,10},{9,11},{10,... | collective-permute-start | bytes 6152 | tf_op jit(solution)/shard_map/ppermute | solution.py:530
  254.8 4.3 collective-permute-start.4
  256.3 94.4 %reduce-scatter.9.cloned.1.call-start = ((), (), s32[]{:S(2)}) async-start(), calls=%async_computation.18 | async-start | bytes 2621440 | tf_op jit(solution)/shard_map/reduce_scatter | solution.py:637
  259.0 42.1 %collective-permute-start.8 = (bf16[4,256,1024]{2,1,0:T(8,128)(2,1)}, bf16[4,256,1024]{2,1,0:T(8,128)(2,1)}, u32[]{:S(2)}, u32[]{:S(2)}) collective-permute-start(bf16[4,256,1024]{2,1,0:T(8,128)(2,1)} %fusion.24), channel_id=1, source_target_pairs={{0,4},{4,0},{8,12},{12,8},{16,20},{20,16},{24,28},{28,24},{1,5},{5... | collective-permute-start | bytes 6291464 | tf_op jit(solution)/shard_map/ppermute | solution.py:564
  297.6 9.7 %collective-permute-start.5 = (bf16[256,256]{1,0:T(8,128)(2,1)S(1)}, bf16[256,256]{1,0:T(8,128)(2,1)S(1)}, u32[]{:S(2)}, u32[]{:S(2)}) collective-permute-start(bf16[256,256]{1,0:T(8,128)(2,1)S(1)} %get-tuple-element.208), channel_id=1, source_target_pairs={{0,3},{1,0},{2,1},{3,2},{4,7},{5,4},{6,5},{7,6},{8,11},{9,8},{10,9... | collective-permute-start | bytes 393224 | tf_op jit(solution)/shard_map/ppermute | solution.py:530
  305.7 19.9 %collective-permute-start.7 = (bf16[256,256]{1,0:T(8,128)(2,1)S(1)}, bf16[256,256]{1,0:T(8,128)(2,1)S(1)}, u32[]{:S(2)}, u32[]{:S(2)}) collective-permute-start(bf16[256,256]{1,0:T(8,128)(2,1)S(1)} %get-tuple-element.206), channel_id=1, source_target_pairs={{0,1},{1,2},{2,3},{3,0},{4,5},{5,6},{6,7},{7,4},{8,9},{9,10},{10,1... | collective-permute-start | bytes 393224 | tf_op jit(solution)/shard_map/ppermute | solution.py:530
  305.7 19.3 %collective-permute-start.6 = (bf16[256,256]{1,0:T(8,128)(2,1)S(1)}, bf16[256,256]{1,0:T(8,128)(2,1)S(1)}, u32[]{:S(2)}, u32[]{:S(2)}) collective-permute-start(bf16[256,256]{1,0:T(8,128)(2,1)S(1)} %get-tuple-element.207), channel_id=1, source_target_pairs={{0,2},{1,3},{2,0},{3,1},{4,6},{5,7},{6,4},{7,5},{8,10},{9,11},{10,... | collective-permute-start | bytes 393224 | tf_op jit(solution)/shard_map/ppermute | solution.py:530
  308.0 35.7 %all-to-all-start.6 = ((bf16[4,256,1024]{2,1,0:T(8,128)(2,1)}), bf16[4,256,1024]{2,1,0:T(8,128)(2,1)S(1)}, u32[]{:S(2)}, u32[]{:S(2)}) async-start(bf16[4,256,1024]{2,1,0:T(8,128)(2,1)} %fusion.12), calls=%async_computation.9 | async-start | bytes 4194304 | tf_op jit(solution)/shard_map/all_to_all | solution.py:675
  311.6 116.4 %all-gather.6.cloned.1.call-start = ((), (), s32[]{:S(2)}) async-start(), calls=%async_computation.19 | async-start | bytes 2621440 | tf_op jit(solution)/shard_map/all_gather | solution.py:730
  353.1 100.0 %reduce-scatter.11.cloned.1.call-start = ((), (), s32[]{:S(2)}) async-start(), calls=%async_computation.20 | async-start | bytes 2621440 | tf_op jit(solution)/shard_map/reduce_scatter | solution.py:731
  366.4 6.2 %collective-permute-start.9 = (bf16[4,240,1024]{2,1,0:T(8,128)(2,1)}, bf16[4,240,1024]{2,1,0:T(8,128)(2,1)}, u32[]{:S(2)}, u32[]{:S(2)}) collective-permute-start(bf16[4,240,1024]{2,1,0:T(8,128)(2,1)} %dynamic-slice_bitcast_fusion), channel_id=1, source_target_pairs={{0,4},{4,0},{8,12},{12,8},{16,20},{20,16},{24,28},{28,24},{1,5},{5... | collective-permute-start | bytes 5898248 | tf_op jit(solution)/shard_map/ppermute | solution.py:564
  369.3 8.1 %all-to-all-start.7 = ((f32[8,1,256]{2,1,0:T(1,128)}), f32[8,1,256]{2,1,0:T(1,128)S(1)}, u32[]{:S(2)}, u32[]{:S(2)}) async-start(f32[8,1,256]{2,1,0:T(1,128)} %all_to_all.43), calls=%async_computation.11 | async-start | bytes 16384 | tf_op jit(solution)/shard_map/all_to_all | solution.py:578
  377.3 29.0 %all-to-all-start.8 = ((bf16[4,240,1024]{2,1,0:T(8,128)(2,1)}), bf16[4,240,1024]{2,1,0:T(8,128)(2,1)}, u32[]{:S(2)}, u32[]{:S(2)}) async-start(bf16[4,240,1024]{2,1,0:T(8,128)(2,1)} %fusion.15), calls=%async_computation.12 | async-start | bytes 3932160 | tf_op jit(solution)/shard_map/all_to_all | solution.py:675
  409.9 47.3 %all-to-all-start.10 = ((bf16[4,256,1024]{2,1,0:T(8,128)(2,1)}), bf16[4,256,1024]{2,1,0:T(8,128)(2,1)}, u32[]{:S(2)}, u32[]{:S(2)}) async-start(bf16[4,256,1024]{2,1,0:T(8,128)(2,1)} %broadcast_in_dim.114), calls=%async_computation.14 | async-start | bytes 4194304 | tf_op jit(solution)/shard_map/all_to_all | solution.py:675
  421.1 36.0 %collective-permute-start.12 = (bf16[48,1024]{1,0:T(8,128)(2,1)S(1)}, bf16[48,1024]{1,0:T(8,128)(2,1)S(1)}, u32[]{:S(2)}, u32[]{:S(2)}) collective-permute-start(bf16[48,1024]{1,0:T(8,128)(2,1)S(1)} %get-tuple-element.210), channel_id=1, source_target_pairs={{0,3},{1,0},{2,1},{3,2},{4,7},{5,4},{6,5},{7,6},{8,11},{9,8},{10,9... | collective-permute-start | bytes 294920 | tf_op jit(solution)/shard_map/ppermute | solution.py:530
  427.3 29.8 %collective-permute-start.10 = (bf16[48,1024]{1,0:T(8,128)(2,1)S(1)}, bf16[48,1024]{1,0:T(8,128)(2,1)S(1)}, u32[]{:S(2)}, u32[]{:S(2)}) collective-permute-start(bf16[48,1024]{1,0:T(8,128)(2,1)S(1)} %get-tuple-element.212), channel_id=1, source_target_pairs={{0,1},{1,2},{2,3},{3,0},{4,5},{5,6},{6,7},{7,4},{8,9},{9,10},{10,1... | collective-permute-start | bytes 294920 | tf_op jit(solution)/shard_map/ppermute | solution.py:530
  427.3 29.8 %collective-permute-start.11 = (bf16[48,1024]{1,0:T(8,128)(2,1)S(1)}, bf16[48,1024]{1,0:T(8,128)(2,1)S(1)}, u32[]{:S(2)}, u32[]{:S(2)}) collective-permute-start(bf16[48,1024]{1,0:T(8,128)(2,1)S(1)} %get-tuple-element.213), channel_id=1, source_target_pairs={{0,2},{1,3},{2,0},{3,1},{4,6},{5,7},{6,4},{7,5},{8,10},{9,11},{10,... | collective-permute-start | bytes 294920 | tf_op jit(solution)/shard_map/ppermute | solution.py:530
  458.4 18.4 %all-to-all-start.9 = ((bf16[4,144,1024]{2,1,0:T(8,128)(2,1)}), bf16[4,144,1024]{2,1,0:T(8,128)(2,1)S(1)}, u32[]{:S(2)}, u32[]{:S(2)}) async-start(bf16[4,144,1024]{2,1,0:T(8,128)(2,1)} %broadcast_in_dim.113), calls=%async_computation.13 | async-start | bytes 2359296 | tf_op jit(solution)/shard_map/all_to_all | solution.py:675
  462.1 55.8 %all-gather.8.cloned.1.call-start = ((), (), s32[]{:S(2)}) async-start(), calls=%async_computation.21 | async-start | bytes 2621440 | tf_op jit(solution)/shard_map/all_gather | solution.py:787
  471.1 27.0 %collective-permute-start.14 = (bf16[4,256,1024]{2,1,0:T(8,128)(2,1)}, bf16[4,256,1024]{2,1,0:T(8,128)(2,1)}, u32[]{:S(2)}, u32[]{:S(2)}) collective-permute-start(bf16[4,256,1024]{2,1,0:T(8,128)(2,1)} %all-to-all-done.10), channel_id=1, source_target_pairs={{0,4},{4,0},{8,12},{12,8},{16,20},{20,16},{24,28},{28,24},{1,5},{5... | collective-permute-start | bytes 6291464 | tf_op jit(solution)/shard_map/ppermute | solution.py:564
  476.8 11.9 %collective-permute-start.13 = (bf16[4,144,1024]{2,1,0:T(8,128)(2,1)S(1)}, bf16[4,144,1024]{2,1,0:T(8,128)(2,1)S(1)}, u32[]{:S(2)}, u32[]{:S(2)}) collective-permute-start(bf16[4,144,1024]{2,1,0:T(8,128)(2,1)S(1)} %all-to-all-done.9), channel_id=1, source_target_pairs={{0,4},{4,0},{8,12},{12,8},{16,20},{20,16},{24,28},{28,24},{1,5},{5... | collective-permute-start | bytes 3538952 | tf_op jit(solution)/shard_map/ppermute | solution.py:564
  (32 other events, 306.2 us)
Sparse Core Ops, SparseCore 0:
  31.7 47.0 all-gather.3
  211.9 28.7 reduce-scatter.4
  256.4 25.7 reduce-scatter.6
  296.6 48.5 reduce-scatter.8
  353.2 48.2 all-gather.5
  404.3 48.7 reduce-scatter.10
  471.3 46.5 all-gather.7

commit v3 on v2

--- a/solution.py
+++ b/solution.py
@@ -10,6 +10,7 @@
 HEAD_DIM = 64
 EPS = 1e-05
 NEGATIVE = -1e30
+EXTRA = 8
 BF = jnp.bfloat16
 F32 = jnp.float32
 
@@ -198,7 +199,9 @@
     )(heads, weight, tokens, gain[None], shift[None])
 
 
-def gelu_back_kernel(rows_ref, up_ref, hidden_grad_ref, hidden_ref, pre_grad_ref, in_ref, dot_ref):
+def gelu_back_kernel(
+    rows_ref, up_ref, hidden_grad_ref, hidden_ref, pre_grad_ref, in_ref
+):
     shape = rows_ref.shape
     count = shape[0] * shape[2]
     rows = rows_ref[...].reshape(count, shape[3])
@@ -216,13 +219,18 @@
         for lane in range(0, step, 128):
             part = product[:, lane : lane + 128]
             dots = part if dots is None else dots + part
-    columns = in_ref.shape[3]
-    in_ref[...] = dot_t(pre_grad_ref[0], up_ref[0, :columns, :]).astype(BF).reshape(in_ref.shape)
+    in_rows = dot_t(pre_grad_ref[0], up_ref[0]).astype(BF)
     capacity = shape[2]
     for block in range(shape[0]):
-        here = jnp.transpose(dots[block * capacity : (block + 1) * capacity])
-        here = jnp.sum(here, axis=0, keepdims=True)
-        dot_ref[0, block] = jnp.broadcast_to(here, (8, capacity))
+        here = slice(block * capacity, (block + 1) * capacity)
+        in_ref[block, 0, :capacity, :] = in_rows[here]
+        total = jnp.sum(jnp.transpose(dots[here]), axis=0, keepdims=True)
+        total = jnp.broadcast_to(total, (EXTRA, capacity))
+        low = total - total.astype(BF).astype(F32)
+        line = lax.broadcasted_iota(jnp.int32, total.shape, 0)
+        both = jnp.where(line == 0, total, jnp.where(line == 1, low, 0.0))
+        in_ref[block, 0, capacity:, :] = jnp.zeros((EXTRA, shape[3]), BF)
+        in_ref[block, 0, capacity:, :capacity] = both.astype(BF)
 
 
 def expert_back(arrived, expert_up, hidden_grads, tile=512):
@@ -237,8 +245,7 @@
         out_shape=(
             jax.ShapeDtypeStruct((held, rows, units), BF),
             jax.ShapeDtypeStruct((held, rows, units), BF),
-            jax.ShapeDtypeStruct((blocks, held, capacity, width // 2), BF),
-            jax.ShapeDtypeStruct((held, blocks, 8, capacity), F32),
+            jax.ShapeDtypeStruct((blocks, held, capacity + EXTRA, width), BF),
         ),
         in_specs=[
             pl.BlockSpec((tile // capacity, 1, capacity, width), slots),
@@ -248,75 +255,32 @@
         out_specs=(
             flat,
             flat,
-            pl.BlockSpec((tile // capacity, 1, capacity, width // 2), slots),
-            pl.BlockSpec((1, tile // capacity, 8, capacity), lambda e, i: (e, i, 0, 0)),
+            pl.BlockSpec((tile // capacity, 1, capacity + EXTRA, width), slots),
         ),
         cost_estimate=pl.CostEstimate(
-            flops=3 * held * rows * units * width,
-            bytes_accessed=13 * held * rows * width,
+            flops=4 * held * rows * units * width,
+            bytes_accessed=14 * held * rows * width,
             transcendentals=held * rows * units,
         ),
         name="expert_back",
     )(arrived, expert_up, hidden_grads)
 
 
-EXTRA = 16
-
-
-def slot_tail_kernel(flat_ref, weight_ref, dot_ref, out_ref):
-    count, _, size, columns = out_ref.shape
-    capacity = size - EXTRA
-    rows = dot_t(flat_ref[0], weight_ref[0]).astype(BF)
-    for block in range(count):
-        out_ref[block, 0, :capacity, :] = rows[block * capacity : (block + 1) * capacity]
-        dots = dot_ref[0, block]
-        low = dots - dots.astype(BF).astype(F32)
-        line = lax.broadcasted_iota(jnp.int32, dots.shape, 0)
-        both = jnp.where(line == 0, dots, jnp.where(line == 1, low, 0.0))
-        out_ref[block, 0, capacity:, :] = jnp.zeros((EXTRA, columns), BF)
-        out_ref[block, 0, capacity:, :capacity] = jnp.concatenate(
-            [both, jnp.zeros_like(both)], axis=0
-        ).astype(BF)
-
-
-def slot_tail_rows(flat, weight, dots, columns, tile=512):
-    held, rows, depth = flat.shape
-    _, blocks, _, capacity = dots.shape
-    return pl.pallas_call(
-        slot_tail_kernel,
-        grid=(held, rows // tile),
-        out_shape=jax.ShapeDtypeStruct((blocks, held, capacity + EXTRA, columns), BF),
-        in_specs=[
-            pl.BlockSpec((1, tile, depth), lambda e, i: (e, i, 0)),
-            pl.BlockSpec((1, columns, depth), lambda e, i: (e, 1, 0)),
-            pl.BlockSpec((1, tile // capacity, 8, capacity), lambda e, i: (e, i, 0, 0)),
-        ],
-        out_specs=pl.BlockSpec(
-            (tile // capacity, 1, capacity + EXTRA, columns), lambda e, i: (i, e, 0, 0)
-        ),
-        cost_estimate=pl.CostEstimate(
-            flops=2 * held * rows * depth * columns,
-            bytes_accessed=4 * held * rows * (depth + columns),
-            transcendentals=0,
-        ),
-        name="slot_tail_rows",
-    )(flat, weight, dots)
-
-
 def slot_rows_kernel(flat_ref, weight_ref, out_ref):
     out_ref[...] = dot(flat_ref[0], weight_ref[0]).astype(BF).reshape(out_ref.shape)
 
 
-def slot_rows(flat, weight, part, columns, blocks, tile=512):
+def slot_rows(flat, weight, blocks, tile=512):
     held, rows, depth = flat.shape
     capacity = rows // blocks
+    columns = weight.shape[2]
     return pl.pallas_call(
         slot_rows_kernel,
         grid=(held, rows // tile),
         out_shape=jax.ShapeDtypeStruct((blocks, held, capacity, columns), BF),
         in_specs=[
             pl.BlockSpec((1, tile, depth), lambda e, i: (e, i, 0)),
-            pl.BlockSpec((1, depth, columns), lambda e, i: (e, 0, part)),
+            pl.BlockSpec((1, depth, columns), lambda e, i: (e, 0, 0)),
         ],
         out_specs=pl.BlockSpec(
             (tile // capacity, 1, capacity, columns), lambda e, i: (i, e, 0, 0)
@@ -337,7 +301,7 @@
     out_ref[...] = (base_ref[...] + weight_ref[...] * rows).astype(BF)
 
 
-def combine(place, weight, back, base, part, tile=256):
+def combine(place, weight, back, base, urgency=1, tile=256):
     slots, columns = back.shape
     rows = base.shape[0]
     own = pl.BlockSpec((tile, 1), lambda i: (i, 0))
@@ -349,11 +313,11 @@
             own,
             own,
             pl.BlockSpec((slots, columns), lambda i: (0, 0)),
-            pl.BlockSpec((tile, columns), lambda i: (i, part)),
+            pl.BlockSpec((tile, columns), lambda i: (i, 0)),
         ],
         out_specs=pl.BlockSpec((tile, columns), lambda i: (i, 0)),
         cost_estimate=pl.CostEstimate(
-            flops=2 * rows * slots * columns,
+            flops=2 * rows * slots * columns * urgency,
             bytes_accessed=2 * slots * columns + 6 * rows * columns,
             transcendentals=0,
         ),
@@ -433,11 +397,10 @@
 
 
 def mid_back_kernel(
-    place_ref, low_half_ref, high_half_ref, gates_ref, rest_ref, cotan_ref, gain_ref, weight_ref,
+    place_ref, grad_ref, gates_ref, rest_ref, cotan_ref, gain_ref, weight_ref,
     heads_ref, rest_grad_ref, low_ref, sums_ref,
 ):
-    grad = jnp.concatenate([low_half_ref[...], high_half_ref[...]], axis=1).astype(F32)
-    grad = grad + gates_ref[...]
+    grad = grad_ref[...].astype(F32) + gates_ref[...]
     unit, inverse = norm_stats(rest_ref[...])
     rest_grad = cotan_ref[...].astype(F32) + norm_back(unit, inverse, gain_ref[...], grad)
     rest_grad_ref[...] = rest_grad
@@ -449,9 +412,9 @@
     sums_ref[1:2, :] = jnp.sum(grad, axis=0, keepdims=True)
 
 
-def mid_back(place, mid_grads, gates, residual, cotangent, gain, weight):
+def mid_back(place, mid_grad, gates, residual, cotangent, gain, weight):
     parts, columns, width = weight.shape
-    rows = mid_grads[0].shape[0]
+    rows = mid_grad.shape[0]
     here = lambda i, place: (place[0], 0)
     whole = lambda i, place: (0, 0)
     cube = lambda i, place: (0, 0, 0)
@@ -461,8 +424,7 @@
             num_scalar_prefetch=1,
             grid=(1,),
             in_specs=[
-                pl.BlockSpec((rows, width // 2), whole),
-                pl.BlockSpec((rows, width // 2), whole),
+                pl.BlockSpec((rows, width), whole),
                 pl.BlockSpec((rows, width), whole),
                 pl.BlockSpec((rows, width), here),
                 pl.BlockSpec((rows, width), here),
@@ -488,7 +450,7 @@
             transcendentals=rows,
         ),
         name="mid_back",
-    )(place[None], *mid_grads, gates, residual, cotangent, gain[None], weight)
+    )(place[None], mid_grad, gates, residual, cotangent, gain[None], weight)
 
 
 def local(
@@ -616,14 +578,10 @@
     arrived, mid_dense_part, dense_dot, dense_up_grad, dense_down_grad = lax.optimization_barrier(
         (arrived, mid_dense_part, dense_dot, dense_up_grad, dense_down_grad)
     )
-    hiddens, pre_grads, low_slots, slot_dots = expert_back(arrived, expert_up, hidden_grads)
-    low_home = exchange(low_slots.reshape(blocks, held * capacity, width // 2))
-    high_slots = slot_tail_rows(after(pre_grads, low_slots), expert_up, slot_dots, width // 2)
-    out_slots = slot_rows(after(hiddens, high_slots), expert_down, 0, width, blocks)
-    high_home = exchange(
-        after(high_slots, out_slots).reshape(blocks, held * (capacity + EXTRA), width // 2)
-    )
-    high_home, out_slots = lax.optimization_barrier((high_home, out_slots))
+    hiddens, pre_grads, in_slots = expert_back(arrived, expert_up, hidden_grads)
+    in_home = exchange(in_slots.reshape(blocks, held * (capacity + EXTRA), width))
+    out_slots = slot_rows(after(hiddens, in_slots), expert_down, blocks)
+    in_home, out_slots = lax.optimization_barrier((in_home, out_slots))
     out_home = exchange(out_slots.reshape(blocks, held * capacity, width))
 
     out_base = dense_weight * dense_part
@@ -636,21 +594,25 @@
     def sum_rows(rows):
         return lax.psum_scatter(rows, "tensor", scatter_dimension=0, tiled=True)
 
-    mid_low_half = combine(
-        place_column, expert_weight, low_home.reshape(slot_total, -1), mid_dense_part, 0
-    )
-    mid_high_half = combine(
+    mid_part = combine(
         tail_column,
         expert_weight,
-        high_home.reshape(expert_count * (capacity + EXTRA), -1),
+        in_home.reshape(expert_count * (capacity + EXTRA), width),
         mid_dense_part,
-        1,
-    )
-    mid_grad_low = sum_rows(mid_low_half)
-    mid_grad_high = sum_rows(after(mid_high_half, mid_low_half))
-
-    slot_dot = after(high_home, mid_high_half).reshape(
-        blocks, held, capacity + EXTRA, width // 2
+    )
+    mid_grad = sum_rows(mid_part)
+    out_part = combine(
+        place_column,
+        expert_weight,
+        after(out_home, mid_part).reshape(slot_total, width),
+        out_base,
+        urgency=8,
+    )
+    out_sum = sum_rows(after(out_part, mid_part))
+    mid_grad = after(mid_grad, out_part)
+
+    slot_dot = after(in_home, mid_part).reshape(
+        blocks, held, capacity + EXTRA, width
     )[:, :, capacity : capacity + 2, :capacity]
     slot_dot = jnp.sum(slot_dot.astype(F32), axis=2).reshape(slot_total)
     expert_dot = jnp.sum(jnp.where(hit, slot_dot[:, None], 0.0), axis=0)
@@ -685,17 +647,28 @@
         return (kept.astype(F32) + from_pair(sent).astype(F32)).astype(BF)
 
     def spread(piece):
-        got = exchange_chips(jnp.broadcast_to(piece[None], (chips,) + piece.shape))
+        got = jnp.stack(
+            [piece]
+            + [
+                lax.ppermute(piece, "expert", [(i, i ^ (2 * k)) for i in range(blocks)])
+                for k in range(1, chips)
+            ]
+        )
+        bit = 1
+        while bit < chips:
+            sides = got.reshape(chips // (2 * bit), 2, bit, *piece.shape)
+            swap = place // 2 // bit % 2
+            got = jnp.where(swap == 0, sides, sides[:, ::-1]).reshape(chips, *piece.shape)
+            bit *= 2
         return got, from_pair(got)
 
     dense_half = pair_sum(
         jnp.concatenate([split(dense_up_grad.astype(BF)), split(dense_down_grad.astype(BF))], axis=2)
     )
-    dense_got = exchange_chips(after(dense_half, out_home))
 
     attended_grad, residual_grad, attn_grad_low, second_sums = mid_back(
         lax.axis_index("tensor"),
-        (mid_grad_low, mid_grad_high),
+        mid_grad,
         gates_mine,
         residual,
         cotangent,
@@ -703,16 +676,9 @@
         project_out_all,
     )
     attended_grad_sent = attended_grad
-    out_sum = sum_rows(
-        combine(
-            place_column,
-            expert_weight,
-            after(out_home, attended_grad_sent).reshape(slot_total, -1),
-            out_base,
-            0,
-        )
-    )
-    attended_grad = in_order(scatter_tensor(attended_grad)).reshape(row_count, head_columns)
+    pieces = scatter_tensor(attended_grad)
+    dense_got = exchange_chips(after(dense_half, pieces[1]))
+    attended_grad = in_order(pieces).reshape(row_count, head_columns)
     project_out_grad = jnp.einsum(
         "ztn,td->znd",
         mine(attended_all, 1),
@@ -721,12 +687,12 @@
     ).astype(BF)
     dense_piece = jnp.sum(after(dense_got, attended_grad_sent).astype(F32), axis=0).astype(BF)
     qkv_grad = attend_backward(qkv, log_total, attended_grad)
-    normed_low_part, first_sums = normed_back(after(qkv_grad, dense_got), project_in, tokens)
-    slot_weight = exchange(after(slot_weight, normed_low_part)).reshape(blocks, held, capacity)
     late_residual, late_sum = lax.optimization_barrier(
-        (residual, out_sum, normed_low_part)
+        (residual, out_sum, qkv_grad)
     )[:2]
     layer_mine = (mine(late_residual) + late_sum.astype(F32)).astype(BF)
+    normed_low_part, first_sums = normed_back(after(qkv_grad, dense_got, layer_mine), project_in, tokens)
+    slot_weight = exchange(after(slot_weight, normed_low_part)).reshape(blocks, held, capacity)
     layer_out = lax.all_gather(layer_mine, "tensor", axis=0, tiled=True)
     normed_grad = lax.psum_scatter(
         after(normed_low_part, layer_mine), "tensor", scatter_dimension=0, tiled=True
@@ -769,22 +735,36 @@
         jnp.broadcast_to(after(dense_piece, rest_piece)[None], (chips,) + dense_piece.shape)
     )
 
-    normed_grad = after(normed_grad, layer_out, rest_piece).astype(F32)
+    expert_rows = [
+        (
+            arrived[:, e].reshape(blocks * capacity, width),
+            cotan_slots[:, e].reshape(blocks * capacity, width).astype(F32),
+            slot_weight[:, e].reshape(blocks * capacity, 1),
+        )
+        for e in range(held)
+    ]
+    expert_down_grad = jnp.stack(
+        [
+            t_dot(hiddens[e], (grads * after(row_weight, rest_half)).astype(BF))
+            for e, (_, grads, row_weight) in enumerate(expert_rows)
+        ]
+    )
+    normed_grad, expert_down_grad = lax.optimization_barrier(
+        (normed_grad, expert_down_grad, layer_out, dense)
+    )[:2]
+    normed_grad = normed_grad.astype(F32)
     unit_first, inverse_first = norm_stats(mine(tokens).astype(F32))
     input_mine = residual_grad + norm_back(unit_first, inverse_first, first_gain, normed_grad)
     input_mine = input_mine.astype(BF)
-    up_grads, down_grads = [], []
-    for e in range(held):
-        row_weight = slot_weight[:, e].reshape(blocks * capacity, 1)
-        down_weight = after(row_weight, rest_half)
-        up_weight = after(row_weight, input_mine)
-        grads = cotan_slots[:, e].reshape(blocks * capacity, width)
-        rows = arrived[:, e].reshape(blocks * capacity, width)
-        down_grads.append(t_dot(hiddens[e], (grads.astype(F32) * down_weight).astype(BF)))
-        up_grads.append(t_dot(rows, (pre_grads[e].astype(F32) * up_weight).astype(BF)))
-    expert_up_grad = jnp.stack(up_grads)
-    expert_down_grad = jnp.stack(down_grads)
     input_grad = lax.all_gather(input_mine, "tensor", axis=0, tiled=True)
+    expert_up_grad = jnp.stack(
+        [
+            t_dot(
+                rows, (pre_grads[e].astype(F32) * after(row_weight, input_mine)).astype(BF)
+            )
+            for e, (rows, _, row_weight) in enumerate(expert_rows)
+        ]
+    )
 
     in_rows = 3 * out_rows
     across = jnp.concatenate(

time: 538 us -> 523 us (0.972)
  Pallas kernels: 103 us -> 93.7 us
  matrix products: 79.5 us -> 71 us
  waiting for transfers between devices: 161 us -> 169 us
  local copies, waits for them, and re-layouts: 42.1 us -> 35.6 us
    all_to_all x6 -> x5, waiting for transfers between devices: 42.7 us -> 78.2 us  [exchange(): return lax.all_to_all(buffer, 'expert', 0, 0, tiled=True)]
    reduce_scatter x3 -> x2, waiting for transfers between devices: 20.7 us -> 2.1 us  [sum_rows(): return lax.psum_scatter(rows, 'tensor', scatter_dimension=0, tiled=True)]
    reduce_scatter x1, waiting for transfers between devices: 25.1 us -> 12.5 us  [local(): lax.psum_scatter(after(normed_low_part, layer_mine), 'tensor', scatter_di...]
    ppermute x0 -> x3, waiting for transfers between devices: none -> 7.44 us  [spread(): lax.ppermute(piece, 'expert', [(i, i ^ 2 * k) for i in range(blocks)])]
    dot_general x8, matrix products: 27.5 us -> 20.7 us  [t_dot(): lax.dot_general(a, b, (((0,), (0,)), ((), ())), preferred_element_type=F32)]
    pallas_call x1 -> x0, Pallas kernels: 6.57 us -> none  [slot_tail_rows(): pl.pallas_call(slot_tail_kernel, grid=(held, rows // tile), out_shape=jax...]
    unnamed x74 -> x90, local copies, waits for them, and re-layouts: 18.2 us -> 14 us
    pallas_call x3 -> x2, Pallas kernels: 21.9 us -> 18.5 us  [combine(): pl.pallas_call(combine_kernel, grid=(rows // tile,), out_shape=jax.ShapeD...]
  transfers between devices with their start and end apart: 33 -> 33, of which waited for: 16 -> 16; matrix products, arithmetic and copies ran while one was open for 31% -> 30% of each run, Pallas kernels for 17% -> 15%
where the time goes in v3:
time: 523 us; the launch traced here: 515 us
  waiting for transfers between devices  169 us (32%)
  Pallas kernels  93.7 us (18%)
  matrix products  71 us (14%)
  starting transfers between devices  66.9 us (13%)
  other arithmetic  62.9 us (12%)
  local copies, waits for them, and re-layouts  35.6 us (7%)
  between operations  15.7 us (3%)
    all_to_all x5, waiting for transfers between devices, exchange(): return lax.all_to_all(buffer, 'expert', 0, 0, tiled=True)  78.2 us
    dot_general x6, matrix products, dot(): return jnp.dot(a, b, preferred_element_type=F32)  29 us
    all_to_all x5, starting transfers between devices, exchange(): return lax.all_to_all(buffer, 'expert', 0, 0, tiled=True)  23.3 us
    dot_general x8, matrix products, t_dot(): lax.dot_general(a, b, (((0,), (0,)), ((), ())), preferred_element_type=F32)  20.7 us
    all_gather x1, waiting for transfers between devices, local(): lax.all_gather(attended, 'tensor', axis=0, tiled=True)  19.9 us
    all_to_all x3, waiting for transfers between devices, exchange_chips(): lax.all_to_all(buffer, 'expert', 0, 0, tiled=True, axis_index_groups=same...  19.8 us
    pallas_call x2, Pallas kernels, combine(): pl.pallas_call(combine_kernel, grid=(rows // tile,), out_shape=jax.ShapeD...  18.5 us
    ppermute x9, starting transfers between devices, shift_tensor(): lax.ppermute(pick(k), 'tensor', [(i, (i + k) % parts) for i in range(part...  17.6 us
  transfers between devices with their start and end apart: 33, of which 16 were waited for; matrix products, arithmetic and copies ran while one was open for 30% of the time, Pallas kernels for 15%

profile of v3, /device:TPU:0, one launch (start us, length us, event | category | flops | bytes accessed | tf_op | source)
XLA Modules:
  0.0 514.7 jit_solution(9985029065815557188)
XLA Ops:
  9.2 6.3 %all-to-all-start = ((bf16[4,64,1024]{2,1,0:T(8,128)(2,1)}), bf16[4,64,1024]{2,1,0:T(8,128)(2,1)S(1)}, u32[]{:S(2)}, u32[]{:S(2)}) async-start(bf16[4,64,1024]{2,1,0:T(8,128)(2,1)} %broadcast_in_dim.53), calls=%async_computation | async-start | bytes 1048576 | tf_op jit(solution)/shard_map/all_to_all | solution.py:512
  22.4 9.8 %attend_forward.1 = (bf16[1024,256]{1,0:T(8,128)(2,1)}, f32[2,8,1024]{2,1,0:T(8,128)}) custom-call(bf16[3,1024,256]{2,1,0:T(8,128)(2,1)} %fusion.35.qkv_ref), custom_call_target="tpu_custom_call" | custom-call | flops 1073741824 | bytes 2097152 | tf_op jit(solution)/shard_map/attend_forward/pallas_call | solution.py:126
  33.8 7.6 %fusion.16 = bf16[2048,1024]{1,0:T(8,128)(2,1)} fusion(bf16[1024,1024]{1,0:T(8,128)(2,1)} %cotan_ref.1, s32[1024]{0:T(1024)S(1)} %get-tuple-element.69), kind=kOutput, calls=%fused_computation.41 | convolution fusion | flops 4299161600 | bytes 6295552 | tf_op jit(solution)/shard_map/dot_general | solution.py:49
  46.5 4.7 all-to-all-start.1
  59.5 19.9 %all-gather.4.cloned.1.call-done = bf16[4096,256]{1,0:T(8,128)(2,1)} async-done(((bf16[1024,256]{1,0:T(8,128)(2,1)}), bf16[4096,256]{1,0:T(8,128)(2,1)}) %all-gather.4.cloned.1.call-update) | async-done | bytes 2097168 | tf_op jit(solution)/shard_map/all_gather | solution.py:520
  79.4 7.4 %project_norm.1 = (f32[1024,1024]{1,0:T(8,128)}, bf16[1024,1024]{1,0:T(8,128)(2,1)}) custom-call(bf16[4,1024,256]{2,1,0:T(8,128)(2,1)} %bitcast.240, bf16[4,256,1024]{2,1,0:T(8,128)(2,1)} %bitcast.219, bf16[1024,1024]{1,0:T(8,128)(2,1)} %token_ref.3, f32[1,1024]{1,0:T(1,128)} %bitcast.253, f32[1,1024]{1,0:T(1,128)} %bitcast.265), custom_call_target="tpu_custom_call" | custom-call | flops 2147483648 | bytes 12582912 | tf_op jit(solution)/shard_map/project_norm/pallas_call | solution.py:178
  86.8 7.6 %fusion.17 = bf16[2048,1024]{1,0:T(8,128)(2,1)} fusion(bf16[1024,1024]{1,0:T(8,128)(2,1)} %get-tuple-element.74, s32[1024]{0:T(1024)S(1)} %get-tuple-element.69), kind=kOutput, calls=%fused_computation.42 | convolution fusion | flops 4299161600 | bytes 6295552 | tf_op jit(solution)/shard_map/dot_general | solution.py:49
  94.4 5.9 %all-to-all-done.1 = bf16[8,256,1024]{2,1,0:T(8,128)(2,1)} async-done(((bf16[8,256,1024]{2,1,0:T(8,128)(2,1)}), bf16[8,256,1024]{2,1,0:T(8,128)(2,1)}, u32[]{:S(2)}, u32[]{:S(2)}) %all-to-all-start.1) | async-done | bytes 4194336 | tf_op jit(solution)/shard_map/all_to_all | solution.py:540
  100.3 4.6 all-to-all-start.2
  104.9 6.7 %fusion.95 = f32[1024,1024]{1,0:T(8,128)} fusion(bf16[1024,1024]{1,0:T(8,128)(2,1)} %get-tuple-element.74, bf16[1024,1024]{1,0:T(8,128)(2,1)} %param.28), kind=kOutput, calls=%fused_computation.211 | convolution fusion | flops 2147483648 | bytes 8388608 | tf_op jit(solution)/shard_map/dot_general | solution.py:49
  116.8 9.1 %expert_hidden_grad.1.hidden_grad_ref = bf16[2,1024,1024]{2,1,0:T(8,128)(2,1)} custom-call(bf16[8,2,128,1024]{3,2,1,0:T(8,128)(2,1)} %bitcast.17.grads_ref, bf16[2,1024,1024]{2,1,0:T(8,128)(2,1)} %weight_ref.1), custom_call_target="tpu_custom_call" | custom-call | flops 4294967296 | bytes 12582912 | tf_op jit(solution)/shard_map/expert_hidden_grad/pallas_call | solution.py:338
  125.9 6.6 %fusion.11 = bf16[1024,1024]{1,0:T(8,128)(2,1)S(1)} fusion(f32[1024,1024]{1,0:T(8,128)} %fusion.95, bf16[1024,1024]{1,0:T(8,128)(2,1)S(1)} %copy-done, bf16[1024,1024]{1,0:T(8,128)(2,1)} %cotan_ref.1, f32[1024]{0:T(1024)S(1)} %get-tuple-element.207), kind=kOutput, calls=%fused_computation.25 | convolution fusion | flops 2166358016 | bytes 10489856 | tf_op jit(solution)/shard_map/dot_general | solution.py:52
  149.1 4.8 all-to-all-done.2
  153.9 16.6 %expert_back.1 = (bf16[2,1024,1024]{2,1,0:T(8,128)(2,1)}, bf16[2,1024,1024]{2,1,0:T(8,128)(2,1)}, bf16[8,2,136,1024]{3,2,1,0:T(8,128)(2,1)}) custom-call(bf16[8,2,128,1024]{3,2,1,0:T(8,128)(2,1)} %bitcast.19.rows_ref, bf16[2,1024,1024]{2,1,0:T(8,128)(2,1)} %up_ref.1, bf16[2,1024,1024]{2,1,0:T(8,128)(2,1)} %expert_hidden_grad.1.hidden_grad_ref), custom_call_target="tpu_custom_call" | custom-call | flops 8589934592 | bytes 29360128 | tf_op jit(solution)/shard_map/expert_back/pallas_call | solution.py:242
  170.5 4.6 all-to-all-start.3
  175.1 9.1 %slot_rows.1 = bf16[8,2,128,1024]{3,2,1,0:T(8,128)(2,1)} custom-call(bf16[2,1024,1024]{2,1,0:T(8,128)(2,1)} %get-tuple-element.79.flat_ref, bf16[2,1024,1024]{2,1,0:T(8,128)(2,1)} %weight_ref.1), custom_call_target="tpu_custom_call" | custom-call | flops 4294967296 | bytes 16777216 | tf_op jit(solution)/shard_map/slot_rows/pallas_call | solution.py:277
  184.2 42.8 %all-to-all-done.3 = bf16[8,272,1024]{2,1,0:T(8,128)(2,1)} async-done(((bf16[8,272,1024]{2,1,0:T(8,128)(2,1)}), bf16[8,272,1024]{2,1,0:T(8,128)(2,1)}, u32[]{:S(2)}, u32[]{:S(2)}) %all-to-all-start.3) | async-done | bytes 4456480 | tf_op jit(solution)/shard_map/all_to_all | solution.py:540
  227.0 5.0 all-to-all-start.4
  235.4 9.5 %combine.2 = bf16[1024,1024]{1,0:T(8,128)(2,1)} custom-call(s32[1024,1]{1,0:T(8,128)} %copy.90.place_ref, f32[1024,1]{1,0:T(8,128)} %get-tuple-element.185.weight_ref, bf16[2176,1024]{1,0:T(8,128)(2,1)} %bitcast.24.back_ref, f32[1024,1024]{1,0:T(8,128)} %fusion.96.base_ref), custom_call_target="tpu_custom_call" | custom-call | flops 4563402752 | bytes 10747904 | tf_op jit(solution)/shard_map/combine/pallas_call | solution.py:308
  256.7 24.4 %all-to-all-done.4 = bf16[8,256,1024]{2,1,0:T(8,128)(2,1)} async-done(((bf16[8,256,1024]{2,1,0:T(8,128)(2,1)}), bf16[8,256,1024]{2,1,0:T(8,128)(2,1)}, u32[]{:S(2)}, u32[]{:S(2)}) %all-to-all-start.4) | async-done | bytes 4194336 | tf_op jit(solution)/shard_map/all_to_all | solution.py:540
  281.1 9.1 %combine.3 = bf16[1024,1024]{1,0:T(8,128)(2,1)} custom-call(s32[1024,1]{1,0:T(8,128)} %copy.92.place_ref, f32[1024,1]{1,0:T(8,128)} %get-tuple-element.185.weight_ref, bf16[2048,1024]{1,0:T(8,128)(2,1)} %bitcast.25.back_ref, f32[1024,1024]{1,0:T(8,128)} %get-tuple-element.196.base_ref), custom_call_target="tpu_custom_call" | custom-call | flops 34359738368 | bytes 10485760 | tf_op jit(solution)/shard_map/combine/pallas_call | solution.py:308
  292.6 4.9 mid_back.1
  313.8 14.0 %collective-permute-done.6 = bf16[256,256]{1,0:T(8,128)(2,1)S(1)} collective-permute-done((bf16[256,256]{1,0:T(8,128)(2,1)S(1)}, bf16[256,256]{1,0:T(8,128)(2,1)S(1)}, u32[]{:S(2)}, u32[]{:S(2)}) %collective-permute-start.6) | collective-permute-done | bytes 131104 | tf_op jit(solution)/shard_map/ppermute | solution.py:492
  328.8 11.9 %attend_backward.1.grad_ref = bf16[3,1024,256]{2,1,0:T(8,128)(2,1)} custom-call(bf16[3,1024,256]{2,1,0:T(8,128)(2,1)} %fusion.35.qkv_ref, f32[2,8,1024]{2,1,0:T(8,128)} %get-tuple-element.85.log_ref, bf16[1024,256]{1,0:T(8,128)(2,1)} %bitcast.236), custom_call_target="tpu_custom_call" | custom-call | flops 2684354560 | bytes 4194304 | tf_op jit(solution)/shard_map/attend_backward/pallas_call | solution.py:147
  349.8 6.4 %normed_back.1 = (bf16[1024,1024]{1,0:T(8,128)(2,1)}, f32[8,1024]{1,0:T(8,128)}) custom-call(bf16[3,1024,256]{2,1,0:T(8,128)(2,1)} %attend_backward.1.grad_ref, bf16[3,1024,256]{2,1,0:T(8,128)(2,1)} %bitcast.264, bf16[1024,1024]{1,0:T(8,128)(2,1)} %token_ref.3), custom_call_target="tpu_custom_call" | custom-call | flops 1610612736 | bytes 6291456 | tf_op jit(solution)/shard_map/normed_back/pallas_call | solution.py:374
  376.4 4.6 all-to-all-start.7
  385.5 19.8 %all-to-all-done.7 = bf16[4,240,1024]{2,1,0:T(8,128)(2,1)} async-done(((bf16[4,240,1024]{2,1,0:T(8,128)(2,1)}), bf16[4,240,1024]{2,1,0:T(8,128)(2,1)}, u32[]{:S(2)}, u32[]{:S(2)}) %all-to-all-start.7) | async-done | bytes 1966112 | tf_op jit(solution)/shard_map/all_to_all | solution.py:637
  413.5 4.8 convolution_bitcast_fusion.3
  432.5 12.5 %reduce-scatter.8.cloned.1.call-done = bf16[256,1024]{1,0:T(8,128)(2,1)} async-done(((bf16[1024,1024]{1,0:T(8,128)(2,1)}), bf16[256,1024]{1,0:T(8,128)(2,1)}) %reduce-scatter.8.cloned.1.call-update) | async-done | bytes 524304 | tf_op jit(solution)/shard_map/reduce_scatter | solution.py:697
  452.7 4.8 fusion.89
  459.1 6.0 %collective-permute-done.14 = bf16[144,1024]{1,0:T(8,128)(2,1)S(1)} collective-permute-done((bf16[144,1024]{1,0:T(8,128)(2,1)S(1)}, bf16[144,1024]{1,0:T(8,128)(2,1)S(1)}, u32[]{:S(2)}, u32[]{:S(2)}) %collective-permute-start.14) | collective-permute-done | bytes 294944 | tf_op jit(solution)/shard_map/ppermute | solution.py:653
  496.5 6.3 %all-gather.8.cloned.1.call-done = bf16[1024,1024]{1,0:T(8,128)(2,1)} async-done(((bf16[256,1024]{1,0:T(8,128)(2,1)}), bf16[1024,1024]{1,0:T(8,128)(2,1)}) %all-gather.8.cloned.1.call-update) | async-done | bytes 2097168 | tf_op jit(solution)/shard_map/all_gather | solution.py:759
  (259 shorter events, 180.9 us)
Async XLA Ops:
  9.2 23.0 %all-to-all-start = ((bf16[4,64,1024]{2,1,0:T(8,128)(2,1)}), bf16[4,64,1024]{2,1,0:T(8,128)(2,1)S(1)}, u32[]{:S(2)}, u32[]{:S(2)}) async-start(bf16[4,64,1024]{2,1,0:T(8,128)(2,1)} %broadcast_in_dim.53), calls=%async_computation | async-start | bytes 1048576 | tf_op jit(solution)/shard_map/all_to_all | solution.py:512
  15.5 63.9 %all-gather.4.cloned.1.call-start = ((), (), s32[]{:S(2)}) async-start(), calls=%async_computation.12 | async-start | bytes 2621440 | tf_op jit(solution)/shard_map/all_gather | solution.py:520
  32.2 13.5 %collective-permute-start = (bf16[4,64,1024]{2,1,0:T(8,128)(2,1)S(1)}, bf16[4,64,1024]{2,1,0:T(8,128)(2,1)S(1)}, u32[]{:S(2)}, u32[]{:S(2)}) collective-permute-start(bf16[4,64,1024]{2,1,0:T(8,128)(2,1)S(1)} %all-to-all-done), channel_id=1, source_target_pairs={{0,8},{4,12},{8,0},{12,4},{16,24},{20,28},{24,16},{28,20},{1,9},{5... | collective-permute-start | bytes 1572872 | tf_op jit(solution)/shard_map/ppermute | solution.py:542
  46.5 53.8 %all-to-all-start.1 = ((bf16[8,256,1024]{2,1,0:T(8,128)(2,1)}), bf16[8,256,1024]{2,1,0:T(8,128)(2,1)}, u32[]{:S(2)}, u32[]{:S(2)}) async-start(bf16[8,256,1024]{2,1,0:T(8,128)(2,1)} %bitcast.228), calls=%async_computation.1 | async-start | bytes 8388608 | tf_op jit(solution)/shard_map/all_to_all | solution.py:540
  100.3 53.7 %all-to-all-start.2 = ((bf16[8,256,1024]{2,1,0:T(8,128)(2,1)}), bf16[8,256,1024]{2,1,0:T(8,128)(2,1)}, u32[]{:S(2)}, u32[]{:S(2)}) async-start(bf16[8,256,1024]{2,1,0:T(8,128)(2,1)} %bitcast.227), calls=%async_computation.2 | async-start | bytes 8388608 | tf_op jit(solution)/shard_map/all_to_all | solution.py:540
  170.5 56.5 %all-to-all-start.3 = ((bf16[8,272,1024]{2,1,0:T(8,128)(2,1)}), bf16[8,272,1024]{2,1,0:T(8,128)(2,1)}, u32[]{:S(2)}, u32[]{:S(2)}) async-start(bf16[8,272,1024]{2,1,0:T(8,128)(2,1)} %bitcast.225), calls=%async_computation.3 | async-start | bytes 8912896 | tf_op jit(solution)/shard_map/all_to_all | solution.py:540
  227.0 54.1 %all-to-all-start.4 = ((bf16[8,256,1024]{2,1,0:T(8,128)(2,1)}), bf16[8,256,1024]{2,1,0:T(8,128)(2,1)}, u32[]{:S(2)}, u32[]{:S(2)}) async-start(bf16[8,256,1024]{2,1,0:T(8,128)(2,1)} %bitcast.226), calls=%async_computation.4 | async-start | bytes 8388608 | tf_op jit(solution)/shard_map/all_to_all | solution.py:540
  232.0 60.6 %reduce-scatter.6.cloned.1.call-start = ((), (), s32[]{:S(2)}) async-start(), calls=%async_computation.14 | async-start | bytes 2621440 | tf_op jit(solution)/shard_map/reduce_scatter | solution.py:595
  244.9 97.9 %reduce-scatter.4.cloned.1.call-start = ((), (), s32[]{:S(2)}) async-start(), calls=%async_computation.13 | async-start | bytes 2621440 | tf_op jit(solution)/shard_map/reduce_scatter | solution.py:595
  248.3 8.4 %collective-permute-start.2 = (f32[2,256]{1,0:T(2,128)S(1)}, f32[2,256]{1,0:T(2,128)S(1)}, u32[]{:S(2)}, u32[]{:S(2)}) collective-permute-start(f32[2,256]{1,0:T(2,128)S(1)} %bitcast.261), channel_id=1, source_target_pairs={{0,1},{1,2},{2,3},{3,0},{4,5},{5,6},{6,7},{7,4},{8,9},{9,10},{10,1... | collective-permute-start | bytes 6152 | tf_op jit(solution)/shard_map/ppermute | solution.py:492
  250.0 6.7 %collective-permute-start.3 = (f32[2,256]{1,0:T(2,128)S(1)}, f32[2,256]{1,0:T(2,128)S(1)}, u32[]{:S(2)}, u32[]{:S(2)}) collective-permute-start(f32[2,256]{1,0:T(2,128)S(1)} %bitcast.262), channel_id=1, source_target_pairs={{0,2},{1,3},{2,0},{3,1},{4,6},{5,7},{6,4},{7,5},{8,10},{9,11},{10,... | collective-permute-start | bytes 6152 | tf_op jit(solution)/shard_map/ppermute | solution.py:492
  252.4 4.3 collective-permute-start.4
  256.7 45.9 %collective-permute-start.8 = (bf16[4,256,1024]{2,1,0:T(8,128)(2,1)}, bf16[4,256,1024]{2,1,0:T(8,128)(2,1)}, u32[]{:S(2)}, u32[]{:S(2)}) collective-permute-start(bf16[4,256,1024]{2,1,0:T(8,128)(2,1)} %fusion.24), channel_id=1, source_target_pairs={{0,4},{4,0},{8,12},{12,8},{16,20},{20,16},{24,28},{28,24},{1,5},{5... | collective-permute-start | bytes 6291464 | tf_op jit(solution)/shard_map/ppermute | solution.py:526
  298.7 10.4 %collective-permute-start.7 = (bf16[256,256]{1,0:T(8,128)(2,1)S(1)}, bf16[256,256]{1,0:T(8,128)(2,1)S(1)}, u32[]{:S(2)}, u32[]{:S(2)}) collective-permute-start(bf16[256,256]{1,0:T(8,128)(2,1)S(1)} %get-tuple-element.204), channel_id=1, source_target_pairs={{0,1},{1,2},{2,3},{3,0},{4,5},{5,6},{6,7},{7,4},{8,9},{9,10},{10,1... | collective-permute-start | bytes 393224 | tf_op jit(solution)/shard_map/ppermute | solution.py:492
  300.4 13.4 %collective-permute-start.5 = (bf16[256,256]{1,0:T(8,128)(2,1)S(1)}, bf16[256,256]{1,0:T(8,128)(2,1)S(1)}, u32[]{:S(2)}, u32[]{:S(2)}) collective-permute-start(bf16[256,256]{1,0:T(8,128)(2,1)S(1)} %get-tuple-element.206), channel_id=1, source_target_pairs={{0,3},{1,0},{2,1},{3,2},{4,7},{5,4},{6,5},{7,6},{8,11},{9,8},{10,9... | collective-permute-start | bytes 393224 | tf_op jit(solution)/shard_map/ppermute | solution.py:492
  306.8 21.0 %collective-permute-start.6 = (bf16[256,256]{1,0:T(8,128)(2,1)S(1)}, bf16[256,256]{1,0:T(8,128)(2,1)S(1)}, u32[]{:S(2)}, u32[]{:S(2)}) collective-permute-start(bf16[256,256]{1,0:T(8,128)(2,1)S(1)} %get-tuple-element.205), channel_id=1, source_target_pairs={{0,2},{1,3},{2,0},{3,1},{4,6},{5,7},{6,4},{7,5},{8,10},{9,11},{10,... | collective-permute-start | bytes 393224 | tf_op jit(solution)/shard_map/ppermute | solution.py:492
  309.1 40.7 %all-to-all-start.5 = ((bf16[4,256,1024]{2,1,0:T(8,128)(2,1)}), bf16[4,256,1024]{2,1,0:T(8,128)(2,1)}, u32[]{:S(2)}, u32[]{:S(2)}) async-start(bf16[4,256,1024]{2,1,0:T(8,128)(2,1)} %fusion.12), calls=%async_computation.7 | async-start | bytes 4194304 | tf_op jit(solution)/shard_map/all_to_all | solution.py:637
  313.6 118.9 %all-gather.6.cloned.1.call-start = ((), (), s32[]{:S(2)}) async-start(), calls=%async_computation.15 | async-start | bytes 2621440 | tf_op jit(solution)/shard_map/all_gather | solution.py:696
  345.2 99.8 %reduce-scatter.8.cloned.1.call-start = ((), (), s32[]{:S(2)}) async-start(), calls=%async_computation.16 | async-start | bytes 2621440 | tf_op jit(solution)/shard_map/reduce_scatter | solution.py:697
  364.5 7.1 %collective-permute-start.9 = (bf16[4,240,1024]{2,1,0:T(8,128)(2,1)}, bf16[4,240,1024]{2,1,0:T(8,128)(2,1)}, u32[]{:S(2)}, u32[]{:S(2)}) collective-permute-start(bf16[4,240,1024]{2,1,0:T(8,128)(2,1)} %dynamic-slice_bitcast_fusion), channel_id=1, source_target_pairs={{0,4},{4,0},{8,12},{12,8},{16,20},{20,16},{24,28},{28,24},{1,5},{5... | collective-permute-start | bytes 5898248 | tf_op jit(solution)/shard_map/ppermute | solution.py:526
  367.2 9.2 %all-to-all-start.6 = ((f32[8,1,256]{2,1,0:T(1,128)}), f32[8,1,256]{2,1,0:T(1,128)S(1)}, u32[]{:S(2)}, u32[]{:S(2)}) async-start(f32[8,1,256]{2,1,0:T(1,128)} %all_to_all.36), calls=%async_computation.9 | async-start | bytes 16384 | tf_op jit(solution)/shard_map/all_to_all | solution.py:540
  376.4 29.0 %all-to-all-start.7 = ((bf16[4,240,1024]{2,1,0:T(8,128)(2,1)}), bf16[4,240,1024]{2,1,0:T(8,128)(2,1)}, u32[]{:S(2)}, u32[]{:S(2)}) async-start(bf16[4,240,1024]{2,1,0:T(8,128)(2,1)} %fusion.15), calls=%async_computation.10 | async-start | bytes 3932160 | tf_op jit(solution)/shard_map/all_to_all | solution.py:637
  408.9 36.1 %all-to-all-start.8 = ((bf16[4,256,1024]{2,1,0:T(8,128)(2,1)}), bf16[4,256,1024]{2,1,0:T(8,128)(2,1)}, u32[]{:S(2)}, u32[]{:S(2)}) async-start(bf16[4,256,1024]{2,1,0:T(8,128)(2,1)} %broadcast_in_dim.106), calls=%async_computation.11 | async-start | bytes 4194304 | tf_op jit(solution)/shard_map/all_to_all | solution.py:637
  413.4 89.5 %all-gather.8.cloned.1.call-start = ((), (), s32[]{:S(2)}) async-start(), calls=%async_computation.17 | async-start | bytes 2621440 | tf_op jit(solution)/shard_map/all_gather | solution.py:759
  425.1 23.8 %collective-permute-start.10 = (bf16[48,1024]{1,0:T(8,128)(2,1)S(1)}, bf16[48,1024]{1,0:T(8,128)(2,1)S(1)}, u32[]{:S(2)}, u32[]{:S(2)}) collective-permute-start(bf16[48,1024]{1,0:T(8,128)(2,1)S(1)} %get-tuple-element.210), channel_id=1, source_target_pairs={{0,1},{1,2},{2,3},{3,0},{4,5},{5,6},{6,7},{7,4},{8,9},{9,10},{10,1... | collective-permute-start | bytes 294920 | tf_op jit(solution)/shard_map/ppermute | solution.py:492
  429.2 19.8 %collective-permute-start.11 = (bf16[48,1024]{1,0:T(8,128)(2,1)S(1)}, bf16[48,1024]{1,0:T(8,128)(2,1)S(1)}, u32[]{:S(2)}, u32[]{:S(2)}) collective-permute-start(bf16[48,1024]{1,0:T(8,128)(2,1)S(1)} %get-tuple-element.211), channel_id=1, source_target_pairs={{0,2},{1,3},{2,0},{3,1},{4,6},{5,7},{6,4},{7,5},{8,10},{9,11},{10,... | collective-permute-start | bytes 294920 | tf_op jit(solution)/shard_map/ppermute | solution.py:492
  429.4 19.6 %collective-permute-start.12 = (bf16[48,1024]{1,0:T(8,128)(2,1)S(1)}, bf16[48,1024]{1,0:T(8,128)(2,1)S(1)}, u32[]{:S(2)}, u32[]{:S(2)}) collective-permute-start(bf16[48,1024]{1,0:T(8,128)(2,1)S(1)} %get-tuple-element.208), channel_id=1, source_target_pairs={{0,3},{1,0},{2,1},{3,2},{4,7},{5,4},{6,5},{7,6},{8,11},{9,8},{10,9... | collective-permute-start | bytes 294920 | tf_op jit(solution)/shard_map/ppermute | solution.py:492
  449.1 9.9 %collective-permute-start.13 = (bf16[144,1024]{1,0:T(8,128)(2,1)S(1)}, bf16[144,1024]{1,0:T(8,128)(2,1)S(1)}, u32[]{:S(2)}, u32[]{:S(2)}) collective-permute-start(bf16[144,1024]{1,0:T(8,128)(2,1)S(1)} %get-tuple-element.213), channel_id=1, source_target_pairs={{0,8},{4,12},{8,0},{12,4},{16,24},{20,28},{24,16},{28,20},{1,9},{5... | collective-permute-start | bytes 884744 | tf_op jit(solution)/shard_map/ppermute | solution.py:653
  450.7 14.4 %collective-permute-start.14 = (bf16[144,1024]{1,0:T(8,128)(2,1)S(1)}, bf16[144,1024]{1,0:T(8,128)(2,1)S(1)}, u32[]{:S(2)}, u32[]{:S(2)}) collective-permute-start(bf16[144,1024]{1,0:T(8,128)(2,1)S(1)} %get-tuple-element.213), channel_id=1, source_target_pairs={{0,16},{4,20},{8,24},{12,28},{16,0},{20,4},{24,8},{28,12},{1,17},{... | collective-permute-start | bytes 884744 | tf_op jit(solution)/shard_map/ppermute | solution.py:653
  452.1 12.9 %collective-permute-start.15 = (bf16[144,1024]{1,0:T(8,128)(2,1)S(1)}, bf16[144,1024]{1,0:T(8,128)(2,1)S(1)}, u32[]{:S(2)}, u32[]{:S(2)}) collective-permute-start(bf16[144,1024]{1,0:T(8,128)(2,1)S(1)} %get-tuple-element.213), channel_id=1, source_target_pairs={{0,24},{4,28},{8,16},{12,20},{16,8},{20,12},{24,0},{28,4},{1,25},{... | collective-permute-start | bytes 884744 | tf_op jit(solution)/shard_map/ppermute | solution.py:653
  457.5 30.4 %collective-permute-start.17 = (bf16[4,256,1024]{2,1,0:T(8,128)(2,1)}, bf16[4,256,1024]{2,1,0:T(8,128)(2,1)}, u32[]{:S(2)}, u32[]{:S(2)}) collective-permute-start(bf16[4,256,1024]{2,1,0:T(8,128)(2,1)} %all-to-all-done.8), channel_id=1, source_target_pairs={{0,4},{4,0},{8,12},{12,8},{16,20},{20,16},{24,28},{28,24},{1,5},{5... | collective-permute-start | bytes 6291464 | tf_op jit(solution)/shard_map/ppermute | solution.py:526
  465.8 11.6 %collective-permute-start.16 = (bf16[4,144,1024]{2,1,0:T(8,128)(2,1)S(1)}, bf16[4,144,1024]{2,1,0:T(8,128)(2,1)S(1)}, u32[]{:S(2)}, u32[]{:S(2)}) collective-permute-start(bf16[4,144,1024]{2,1,0:T(8,128)(2,1)S(1)} %bitcast.223), channel_id=1, source_target_pairs={{0,4},{4,0},{8,12},{12,8},{16,20},{20,16},{24,28},{28,24},{1,5},{5... | collective-permute-start | bytes 3538952 | tf_op jit(solution)/shard_map/ppermute | solution.py:526
  (40 other events, 343.5 us)
Sparse Core Ops, SparseCore 0:
  32.3 47.0 all-gather.3
  245.0 45.0 reduce-scatter.5
  293.0 49.8 reduce-scatter.3
  345.3 48.1 all-gather.5
  396.2 48.7 reduce-scatter.7
  457.7 45.1 all-gather.7

commit v4 on v3

--- a/solution.py
+++ b/solution.py
@@ -743,20 +743,19 @@
         )
         for e in range(held)
     ]
-    expert_down_grad = jnp.stack(
-        [
-            t_dot(hiddens[e], (grads * after(row_weight, rest_half)).astype(BF))
-            for e, (_, grads, row_weight) in enumerate(expert_rows)
-        ]
-    )
-    normed_grad, expert_down_grad = lax.optimization_barrier(
-        (normed_grad, expert_down_grad, layer_out, dense)
+    down_grads = [
+        t_dot(hiddens[e], (grads * after(row_weight, rest_half)).astype(BF))
+        for e, (_, grads, row_weight) in enumerate(expert_rows)
+    ]
+    normed_grad, down_grads = lax.optimization_barrier(
+        (normed_grad, down_grads, layer_out, dense)
     )[:2]
     normed_grad = normed_grad.astype(F32)
     unit_first, inverse_first = norm_stats(mine(tokens).astype(F32))
     input_mine = residual_grad + norm_back(unit_first, inverse_first, first_gain, normed_grad)
     input_mine = input_mine.astype(BF)
     input_grad = lax.all_gather(input_mine, "tensor", axis=0, tiled=True)
+    expert_down_grad = jnp.stack(after(down_grads, input_mine))
     expert_up_grad = jnp.stack(
         [
             t_dot(

time: 523 us -> 518 us (level)
  waiting for transfers between devices: 169 us -> 158 us
    all_gather x1, waiting for transfers between devices: 6.31 us -> 0.07 us  [local(): input_grad = lax.all_gather(input_mine, 'tensor', axis=0, tiled=True)]
    unnamed x90 -> x92, local copies, waits for them, and re-layouts: 14 us -> 14.7 us
  transfers between devices with their start and end apart: 33 -> 33, of which waited for: 16 -> 16; matrix products, arithmetic and copies ran while one was open for 30% -> 32% of each run, Pallas kernels for 15% -> 15%
where the time goes in v4:
time: 518 us; the launch traced here: 510 us
  waiting for transfers between devices  158 us (31%)
  Pallas kernels  93.7 us (18%)
  matrix products  75.2 us (15%)
  starting transfers between devices  67.1 us (13%)
  other arithmetic  64.2 us (12%)
  local copies, waits for them, and re-layouts  36.3 us (7%)
  between operations  15.4 us (3%)
    all_to_all x5, waiting for transfers between devices, exchange(): return lax.all_to_all(buffer, 'expert', 0, 0, tiled=True)  78.1 us
    dot_general x6, matrix products, dot(): return jnp.dot(a, b, preferred_element_type=F32)  29 us
    dot_general x8, matrix products, t_dot(): lax.dot_general(a, b, (((0,), (0,)), ((), ())), preferred_element_type=F32)  24.6 us
    all_to_all x5, starting transfers between devices, exchange(): return lax.all_to_all(buffer, 'expert', 0, 0, tiled=True)  23.2 us
    all_gather x1, waiting for transfers between devices, local(): lax.all_gather(attended, 'tensor', axis=0, tiled=True)  19.8 us
    pallas_call x2, Pallas kernels, combine(): pl.pallas_call(combine_kernel, grid=(rows // tile,), out_shape=jax.ShapeD...  18.6 us
    all_to_all x3, waiting for transfers between devices, exchange_chips(): lax.all_to_all(buffer, 'expert', 0, 0, tiled=True, axis_index_groups=same...  18.4 us
    ppermute x9, starting transfers between devices, shift_tensor(): lax.ppermute(pick(k), 'tensor', [(i, (i + k) % parts) for i in range(part...  17.7 us
  transfers between devices with their start and end apart: 33, of which 16 were waited for; matrix products, arithmetic and copies ran while one was open for 32% of the time, Pallas kernels for 15%

profile of v4, /device:TPU:0, one launch (start us, length us, event | category | flops | bytes accessed | tf_op | source)
XLA Modules:
  0.0 509.9 jit_solution(3346180293214900378)
XLA Ops:
  9.2 6.3 %all-to-all-start = ((bf16[4,64,1024]{2,1,0:T(8,128)(2,1)}), bf16[4,64,1024]{2,1,0:T(8,128)(2,1)S(1)}, u32[]{:S(2)}, u32[]{:S(2)}) async-start(bf16[4,64,1024]{2,1,0:T(8,128)(2,1)} %broadcast_in_dim.53), calls=%async_computation | async-start | bytes 1048576 | tf_op jit(solution)/shard_map/all_to_all | solution.py:512
  22.4 9.8 %attend_forward.1 = (bf16[1024,256]{1,0:T(8,128)(2,1)}, f32[2,8,1024]{2,1,0:T(8,128)}) custom-call(bf16[3,1024,256]{2,1,0:T(8,128)(2,1)} %fusion.37.qkv_ref), custom_call_target="tpu_custom_call" | custom-call | flops 1073741824 | bytes 2097152 | tf_op jit(solution)/shard_map/attend_forward/pallas_call | solution.py:126
  33.8 7.6 %fusion.16 = bf16[2048,1024]{1,0:T(8,128)(2,1)} fusion(bf16[1024,1024]{1,0:T(8,128)(2,1)} %cotan_ref.1, s32[1024]{0:T(1024)S(1)} %get-tuple-element.72), kind=kOutput, calls=%fused_computation.41 | convolution fusion | flops 4299161600 | bytes 6295552 | tf_op jit(solution)/shard_map/dot_general | solution.py:49
  46.4 4.8 all-to-all-start.1
  59.6 19.8 %all-gather.4.cloned.1.call-done = bf16[4096,256]{1,0:T(8,128)(2,1)} async-done(((bf16[1024,256]{1,0:T(8,128)(2,1)}), bf16[4096,256]{1,0:T(8,128)(2,1)}) %all-gather.4.cloned.1.call-update) | async-done | bytes 2097168 | tf_op jit(solution)/shard_map/all_gather | solution.py:520
  79.4 7.4 %project_norm.1 = (f32[1024,1024]{1,0:T(8,128)}, bf16[1024,1024]{1,0:T(8,128)(2,1)}) custom-call(bf16[4,1024,256]{2,1,0:T(8,128)(2,1)} %bitcast.240, bf16[4,256,1024]{2,1,0:T(8,128)(2,1)} %bitcast.217, bf16[1024,1024]{1,0:T(8,128)(2,1)} %token_ref.3, f32[1,1024]{1,0:T(1,128)} %bitcast.253, f32[1,1024]{1,0:T(1,128)} %bitcast.265), custom_call_target="tpu_custom_call" | custom-call | flops 2147483648 | bytes 12582912 | tf_op jit(solution)/shard_map/project_norm/pallas_call | solution.py:178
  86.8 7.6 %fusion.17 = bf16[2048,1024]{1,0:T(8,128)(2,1)} fusion(bf16[1024,1024]{1,0:T(8,128)(2,1)} %get-tuple-element.77, s32[1024]{0:T(1024)S(1)} %get-tuple-element.72), kind=kOutput, calls=%fused_computation.42 | convolution fusion | flops 4299161600 | bytes 6295552 | tf_op jit(solution)/shard_map/dot_general | solution.py:49
  94.4 6.0 %all-to-all-done.1 = bf16[8,256,1024]{2,1,0:T(8,128)(2,1)} async-done(((bf16[8,256,1024]{2,1,0:T(8,128)(2,1)}), bf16[8,256,1024]{2,1,0:T(8,128)(2,1)}, u32[]{:S(2)}, u32[]{:S(2)}) %all-to-all-start.1) | async-done | bytes 4194336 | tf_op jit(solution)/shard_map/all_to_all | solution.py:540
  100.4 4.5 all-to-all-start.2
  105.0 6.7 %fusion.97 = f32[1024,1024]{1,0:T(8,128)} fusion(bf16[1024,1024]{1,0:T(8,128)(2,1)} %get-tuple-element.77, bf16[1024,1024]{1,0:T(8,128)(2,1)} %param.28), kind=kOutput, calls=%fused_computation.211 | convolution fusion | flops 2147483648 | bytes 8388608 | tf_op jit(solution)/shard_map/dot_general | solution.py:49
  116.9 9.1 %expert_hidden_grad.1.hidden_grad_ref = bf16[2,1024,1024]{2,1,0:T(8,128)(2,1)} custom-call(bf16[8,2,128,1024]{3,2,1,0:T(8,128)(2,1)} %bitcast.17.grads_ref, bf16[2,1024,1024]{2,1,0:T(8,128)(2,1)} %weight_ref.1), custom_call_target="tpu_custom_call" | custom-call | flops 4294967296 | bytes 12582912 | tf_op jit(solution)/shard_map/expert_hidden_grad/pallas_call | solution.py:338
  126.0 7.0 %fusion.11 = bf16[1024,1024]{1,0:T(8,128)(2,1)S(1)} fusion(f32[1024,1024]{1,0:T(8,128)} %fusion.97, bf16[1024,1024]{1,0:T(8,128)(2,1)S(1)} %copy-done, bf16[1024,1024]{1,0:T(8,128)(2,1)} %cotan_ref.1, f32[1024]{0:T(1024)S(1)} %get-tuple-element.213), kind=kOutput, calls=%fused_computation.25 | convolution fusion | flops 2166358016 | bytes 10489856 | tf_op jit(solution)/shard_map/dot_general | solution.py:52
  149.5 4.5 all-to-all-done.2
  154.0 16.6 %expert_back.1 = (bf16[2,1024,1024]{2,1,0:T(8,128)(2,1)}, bf16[2,1024,1024]{2,1,0:T(8,128)(2,1)}, bf16[8,2,136,1024]{3,2,1,0:T(8,128)(2,1)}) custom-call(bf16[8,2,128,1024]{3,2,1,0:T(8,128)(2,1)} %bitcast.19.rows_ref, bf16[2,1024,1024]{2,1,0:T(8,128)(2,1)} %up_ref.1, bf16[2,1024,1024]{2,1,0:T(8,128)(2,1)} %expert_hidden_grad.1.hidden_grad_ref), custom_call_target="tpu_custom_call" | custom-call | flops 8589934592 | bytes 29360128 | tf_op jit(solution)/shard_map/expert_back/pallas_call | solution.py:242
  170.6 4.6 all-to-all-start.3
  175.2 9.1 %slot_rows.1 = bf16[8,2,128,1024]{3,2,1,0:T(8,128)(2,1)} custom-call(bf16[2,1024,1024]{2,1,0:T(8,128)(2,1)} %get-tuple-element.82.flat_ref, bf16[2,1024,1024]{2,1,0:T(8,128)(2,1)} %weight_ref.1), custom_call_target="tpu_custom_call" | custom-call | flops 4294967296 | bytes 16777216 | tf_op jit(solution)/shard_map/slot_rows/pallas_call | solution.py:277
  184.3 42.8 %all-to-all-done.3 = bf16[8,272,1024]{2,1,0:T(8,128)(2,1)} async-done(((bf16[8,272,1024]{2,1,0:T(8,128)(2,1)}), bf16[8,272,1024]{2,1,0:T(8,128)(2,1)}, u32[]{:S(2)}, u32[]{:S(2)}) %all-to-all-start.3) | async-done | bytes 4456480 | tf_op jit(solution)/shard_map/all_to_all | solution.py:540
  227.1 4.7 all-to-all-start.4
  235.3 9.5 %combine.2 = bf16[1024,1024]{1,0:T(8,128)(2,1)} custom-call(s32[1024,1]{1,0:T(8,128)} %copy.90.place_ref, f32[1024,1]{1,0:T(8,128)} %get-tuple-element.191.weight_ref, bf16[2176,1024]{1,0:T(8,128)(2,1)} %bitcast.24.back_ref, f32[1024,1024]{1,0:T(8,128)} %fusion.98.base_ref), custom_call_target="tpu_custom_call" | custom-call | flops 4563402752 | bytes 10747904 | tf_op jit(solution)/shard_map/combine/pallas_call | solution.py:308
  256.6 24.4 %all-to-all-done.4 = bf16[8,256,1024]{2,1,0:T(8,128)(2,1)} async-done(((bf16[8,256,1024]{2,1,0:T(8,128)(2,1)}), bf16[8,256,1024]{2,1,0:T(8,128)(2,1)}, u32[]{:S(2)}, u32[]{:S(2)}) %all-to-all-start.4) | async-done | bytes 4194336 | tf_op jit(solution)/shard_map/all_to_all | solution.py:540
  281.0 9.1 %combine.3 = bf16[1024,1024]{1,0:T(8,128)(2,1)} custom-call(s32[1024,1]{1,0:T(8,128)} %copy.92.place_ref, f32[1024,1]{1,0:T(8,128)} %get-tuple-element.191.weight_ref, bf16[2048,1024]{1,0:T(8,128)(2,1)} %bitcast.25.back_ref, f32[1024,1024]{1,0:T(8,128)} %get-tuple-element.202.base_ref), custom_call_target="tpu_custom_call" | custom-call | flops 34359738368 | bytes 10485760 | tf_op jit(solution)/shard_map/combine/pallas_call | solution.py:308
  292.4 4.9 mid_back.1
  313.8 14.0 %collective-permute-done.6 = bf16[256,256]{1,0:T(8,128)(2,1)S(1)} collective-permute-done((bf16[256,256]{1,0:T(8,128)(2,1)S(1)}, bf16[256,256]{1,0:T(8,128)(2,1)S(1)}, u32[]{:S(2)}, u32[]{:S(2)}) %collective-permute-start.6) | collective-permute-done | bytes 131104 | tf_op jit(solution)/shard_map/ppermute | solution.py:492
  328.7 11.9 %attend_backward.1.grad_ref = bf16[3,1024,256]{2,1,0:T(8,128)(2,1)} custom-call(bf16[3,1024,256]{2,1,0:T(8,128)(2,1)} %fusion.37.qkv_ref, f32[2,8,1024]{2,1,0:T(8,128)} %get-tuple-element.88.log_ref, bf16[1024,256]{1,0:T(8,128)(2,1)} %bitcast.236), custom_call_target="tpu_custom_call" | custom-call | flops 2684354560 | bytes 4194304 | tf_op jit(solution)/shard_map/attend_backward/pallas_call | solution.py:147
  349.7 6.4 %normed_back.1 = (bf16[1024,1024]{1,0:T(8,128)(2,1)}, f32[8,1024]{1,0:T(8,128)}) custom-call(bf16[3,1024,256]{2,1,0:T(8,128)(2,1)} %attend_backward.1.grad_ref, bf16[3,1024,256]{2,1,0:T(8,128)(2,1)} %bitcast.264, bf16[1024,1024]{1,0:T(8,128)(2,1)} %token_ref.3), custom_call_target="tpu_custom_call" | custom-call | flops 1610612736 | bytes 6291456 | tf_op jit(solution)/shard_map/normed_back/pallas_call | solution.py:374
  376.3 4.7 all-to-all-start.7
  382.1 4.9 fusion.91
  386.9 18.4 %all-to-all-done.7 = bf16[4,240,1024]{2,1,0:T(8,128)(2,1)} async-done(((bf16[4,240,1024]{2,1,0:T(8,128)(2,1)}), bf16[4,240,1024]{2,1,0:T(8,128)(2,1)}, u32[]{:S(2)}, u32[]{:S(2)}) %all-to-all-start.7) | async-done | bytes 1966112 | tf_op jit(solution)/shard_map/all_to_all | solution.py:637
  434.0 10.6 %reduce-scatter.8.cloned.1.call-done = bf16[256,1024]{1,0:T(8,128)(2,1)} async-done(((bf16[1024,1024]{1,0:T(8,128)(2,1)}), bf16[256,1024]{1,0:T(8,128)(2,1)}) %reduce-scatter.8.cloned.1.call-update) | async-done | bytes 524304 | tf_op jit(solution)/shard_map/reduce_scatter | solution.py:697
  453.1 4.9 convolution_bitcast_fusion.1
  459.4 5.1 %collective-permute-done.14 = bf16[144,1024]{1,0:T(8,128)(2,1)S(1)} collective-permute-done((bf16[144,1024]{1,0:T(8,128)(2,1)S(1)}, bf16[144,1024]{1,0:T(8,128)(2,1)S(1)}, u32[]{:S(2)}, u32[]{:S(2)}) %collective-permute-start.14) | collective-permute-done | bytes 294944 | tf_op jit(solution)/shard_map/ppermute | solution.py:653
  466.9 4.8 pad_maximum_fusion.1
  (261 shorter events, 182.0 us)
Async XLA Ops:
  9.2 23.0 %all-to-all-start = ((bf16[4,64,1024]{2,1,0:T(8,128)(2,1)}), bf16[4,64,1024]{2,1,0:T(8,128)(2,1)S(1)}, u32[]{:S(2)}, u32[]{:S(2)}) async-start(bf16[4,64,1024]{2,1,0:T(8,128)(2,1)} %broadcast_in_dim.53), calls=%async_computation | async-start | bytes 1048576 | tf_op jit(solution)/shard_map/all_to_all | solution.py:512
  15.5 63.9 %all-gather.4.cloned.1.call-start = ((), (), s32[]{:S(2)}) async-start(), calls=%async_computation.12 | async-start | bytes 2621440 | tf_op jit(solution)/shard_map/all_gather | solution.py:520
  32.2 13.5 %collective-permute-start = (bf16[4,64,1024]{2,1,0:T(8,128)(2,1)S(1)}, bf16[4,64,1024]{2,1,0:T(8,128)(2,1)S(1)}, u32[]{:S(2)}, u32[]{:S(2)}) collective-permute-start(bf16[4,64,1024]{2,1,0:T(8,128)(2,1)S(1)} %all-to-all-done), channel_id=1, source_target_pairs={{0,8},{4,12},{8,0},{12,4},{16,24},{20,28},{24,16},{28,20},{1,9},{5... | collective-permute-start | bytes 1572872 | tf_op jit(solution)/shard_map/ppermute | solution.py:542
  46.4 54.0 %all-to-all-start.1 = ((bf16[8,256,1024]{2,1,0:T(8,128)(2,1)}), bf16[8,256,1024]{2,1,0:T(8,128)(2,1)}, u32[]{:S(2)}, u32[]{:S(2)}) async-start(bf16[8,256,1024]{2,1,0:T(8,128)(2,1)} %bitcast.226), calls=%async_computation.1 | async-start | bytes 8388608 | tf_op jit(solution)/shard_map/all_to_all | solution.py:540
  100.4 53.6 %all-to-all-start.2 = ((bf16[8,256,1024]{2,1,0:T(8,128)(2,1)}), bf16[8,256,1024]{2,1,0:T(8,128)(2,1)}, u32[]{:S(2)}, u32[]{:S(2)}) async-start(bf16[8,256,1024]{2,1,0:T(8,128)(2,1)} %bitcast.225), calls=%async_computation.2 | async-start | bytes 8388608 | tf_op jit(solution)/shard_map/all_to_all | solution.py:540
  170.6 56.5 %all-to-all-start.3 = ((bf16[8,272,1024]{2,1,0:T(8,128)(2,1)}), bf16[8,272,1024]{2,1,0:T(8,128)(2,1)}, u32[]{:S(2)}, u32[]{:S(2)}) async-start(bf16[8,272,1024]{2,1,0:T(8,128)(2,1)} %bitcast.223), calls=%async_computation.3 | async-start | bytes 8912896 | tf_op jit(solution)/shard_map/all_to_all | solution.py:540
  227.1 53.8 %all-to-all-start.4 = ((bf16[8,256,1024]{2,1,0:T(8,128)(2,1)}), bf16[8,256,1024]{2,1,0:T(8,128)(2,1)}, u32[]{:S(2)}, u32[]{:S(2)}) async-start(bf16[8,256,1024]{2,1,0:T(8,128)(2,1)} %bitcast.224), calls=%async_computation.4 | async-start | bytes 8388608 | tf_op jit(solution)/shard_map/all_to_all | solution.py:540
  231.9 60.6 %reduce-scatter.6.cloned.1.call-start = ((), (), s32[]{:S(2)}) async-start(), calls=%async_computation.14 | async-start | bytes 2621440 | tf_op jit(solution)/shard_map/reduce_scatter | solution.py:595
  244.8 97.9 %reduce-scatter.4.cloned.1.call-start = ((), (), s32[]{:S(2)}) async-start(), calls=%async_computation.13 | async-start | bytes 2621440 | tf_op jit(solution)/shard_map/reduce_scatter | solution.py:595
  248.2 8.4 %collective-permute-start.2 = (f32[2,256]{1,0:T(2,128)S(1)}, f32[2,256]{1,0:T(2,128)S(1)}, u32[]{:S(2)}, u32[]{:S(2)}) collective-permute-start(f32[2,256]{1,0:T(2,128)S(1)} %bitcast.261), channel_id=1, source_target_pairs={{0,1},{1,2},{2,3},{3,0},{4,5},{5,6},{6,7},{7,4},{8,9},{9,10},{10,1... | collective-permute-start | bytes 6152 | tf_op jit(solution)/shard_map/ppermute | solution.py:492
  249.9 6.7 %collective-permute-start.3 = (f32[2,256]{1,0:T(2,128)S(1)}, f32[2,256]{1,0:T(2,128)S(1)}, u32[]{:S(2)}, u32[]{:S(2)}) collective-permute-start(f32[2,256]{1,0:T(2,128)S(1)} %bitcast.262), channel_id=1, source_target_pairs={{0,2},{1,3},{2,0},{3,1},{4,6},{5,7},{6,4},{7,5},{8,10},{9,11},{10,... | collective-permute-start | bytes 6152 | tf_op jit(solution)/shard_map/ppermute | solution.py:492
  252.3 4.3 collective-permute-start.4
  256.6 45.9 %collective-permute-start.8 = (bf16[4,256,1024]{2,1,0:T(8,128)(2,1)}, bf16[4,256,1024]{2,1,0:T(8,128)(2,1)}, u32[]{:S(2)}, u32[]{:S(2)}) collective-permute-start(bf16[4,256,1024]{2,1,0:T(8,128)(2,1)} %fusion.24), channel_id=1, source_target_pairs={{0,4},{4,0},{8,12},{12,8},{16,20},{20,16},{24,28},{28,24},{1,5},{5... | collective-permute-start | bytes 6291464 | tf_op jit(solution)/shard_map/ppermute | solution.py:526
  298.6 10.4 %collective-permute-start.7 = (bf16[256,256]{1,0:T(8,128)(2,1)S(1)}, bf16[256,256]{1,0:T(8,128)(2,1)S(1)}, u32[]{:S(2)}, u32[]{:S(2)}) collective-permute-start(bf16[256,256]{1,0:T(8,128)(2,1)S(1)} %get-tuple-element.210), channel_id=1, source_target_pairs={{0,1},{1,2},{2,3},{3,0},{4,5},{5,6},{6,7},{7,4},{8,9},{9,10},{10,1... | collective-permute-start | bytes 393224 | tf_op jit(solution)/shard_map/ppermute | solution.py:492
  300.3 13.4 %collective-permute-start.5 = (bf16[256,256]{1,0:T(8,128)(2,1)S(1)}, bf16[256,256]{1,0:T(8,128)(2,1)S(1)}, u32[]{:S(2)}, u32[]{:S(2)}) collective-permute-start(bf16[256,256]{1,0:T(8,128)(2,1)S(1)} %get-tuple-element.212), channel_id=1, source_target_pairs={{0,3},{1,0},{2,1},{3,2},{4,7},{5,4},{6,5},{7,6},{8,11},{9,8},{10,9... | collective-permute-start | bytes 393224 | tf_op jit(solution)/shard_map/ppermute | solution.py:492
  306.7 21.1 %collective-permute-start.6 = (bf16[256,256]{1,0:T(8,128)(2,1)S(1)}, bf16[256,256]{1,0:T(8,128)(2,1)S(1)}, u32[]{:S(2)}, u32[]{:S(2)}) collective-permute-start(bf16[256,256]{1,0:T(8,128)(2,1)S(1)} %get-tuple-element.211), channel_id=1, source_target_pairs={{0,2},{1,3},{2,0},{3,1},{4,6},{5,7},{6,4},{7,5},{8,10},{9,11},{10,... | collective-permute-start | bytes 393224 | tf_op jit(solution)/shard_map/ppermute | solution.py:492
  309.0 40.7 %all-to-all-start.5 = ((bf16[4,256,1024]{2,1,0:T(8,128)(2,1)}), bf16[4,256,1024]{2,1,0:T(8,128)(2,1)}, u32[]{:S(2)}, u32[]{:S(2)}) async-start(bf16[4,256,1024]{2,1,0:T(8,128)(2,1)} %fusion.12), calls=%async_computation.7 | async-start | bytes 4194304 | tf_op jit(solution)/shard_map/all_to_all | solution.py:637
  313.5 112.2 %all-gather.6.cloned.1.call-start = ((), (), s32[]{:S(2)}) async-start(), calls=%async_computation.15 | async-start | bytes 2621440 | tf_op jit(solution)/shard_map/all_gather | solution.py:696
  345.0 99.6 %reduce-scatter.8.cloned.1.call-start = ((), (), s32[]{:S(2)}) async-start(), calls=%async_computation.16 | async-start | bytes 2621440 | tf_op jit(solution)/shard_map/reduce_scatter | solution.py:697
  364.4 7.2 %collective-permute-start.9 = (bf16[4,240,1024]{2,1,0:T(8,128)(2,1)}, bf16[4,240,1024]{2,1,0:T(8,128)(2,1)}, u32[]{:S(2)}, u32[]{:S(2)}) collective-permute-start(bf16[4,240,1024]{2,1,0:T(8,128)(2,1)} %dynamic-slice_bitcast_fusion), channel_id=1, source_target_pairs={{0,4},{4,0},{8,12},{12,8},{16,20},{20,16},{24,28},{28,24},{1,5},{5... | collective-permute-start | bytes 5898248 | tf_op jit(solution)/shard_map/ppermute | solution.py:526
  367.1 9.2 %all-to-all-start.6 = ((f32[8,1,256]{2,1,0:T(1,128)}), f32[8,1,256]{2,1,0:T(1,128)S(1)}, u32[]{:S(2)}, u32[]{:S(2)}) async-start(f32[8,1,256]{2,1,0:T(1,128)} %all_to_all.36), calls=%async_computation.9 | async-start | bytes 16384 | tf_op jit(solution)/shard_map/all_to_all | solution.py:540
  376.3 29.0 %all-to-all-start.7 = ((bf16[4,240,1024]{2,1,0:T(8,128)(2,1)}), bf16[4,240,1024]{2,1,0:T(8,128)(2,1)}, u32[]{:S(2)}, u32[]{:S(2)}) async-start(bf16[4,240,1024]{2,1,0:T(8,128)(2,1)} %fusion.15), calls=%async_computation.10 | async-start | bytes 3932160 | tf_op jit(solution)/shard_map/all_to_all | solution.py:637
  408.8 35.8 %all-to-all-start.8 = ((bf16[4,256,1024]{2,1,0:T(8,128)(2,1)}), bf16[4,256,1024]{2,1,0:T(8,128)(2,1)}, u32[]{:S(2)}, u32[]{:S(2)}) async-start(bf16[4,256,1024]{2,1,0:T(8,128)(2,1)} %broadcast_in_dim.106), calls=%async_computation.11 | async-start | bytes 4194304 | tf_op jit(solution)/shard_map/all_to_all | solution.py:637
  413.3 85.0 %all-gather.8.cloned.1.call-start = ((), (), s32[]{:S(2)}) async-start(), calls=%async_computation.17 | async-start | bytes 2621440 | tf_op jit(solution)/shard_map/all_gather | solution.py:757
  426.5 21.8 %collective-permute-start.10 = (bf16[48,1024]{1,0:T(8,128)(2,1)}, bf16[48,1024]{1,0:T(8,128)(2,1)}, u32[]{:S(2)}, u32[]{:S(2)}) collective-permute-start(bf16[48,1024]{1,0:T(8,128)(2,1)} %get-tuple-element.216), channel_id=1, source_target_pairs={{0,1},{1,2},{2,3},{3,0},{4,5},{5,6},{6,7},{7,4},{8,9},{9,10},{10,1... | collective-permute-start | bytes 294920 | tf_op jit(solution)/shard_map/ppermute | solution.py:492
  430.5 17.8 %collective-permute-start.11 = (bf16[48,1024]{1,0:T(8,128)(2,1)}, bf16[48,1024]{1,0:T(8,128)(2,1)}, u32[]{:S(2)}, u32[]{:S(2)}) collective-permute-start(bf16[48,1024]{1,0:T(8,128)(2,1)} %get-tuple-element.217), channel_id=1, source_target_pairs={{0,2},{1,3},{2,0},{3,1},{4,6},{5,7},{6,4},{7,5},{8,10},{9,11},{10,... | collective-permute-start | bytes 294920 | tf_op jit(solution)/shard_map/ppermute | solution.py:492
  430.6 17.7 %collective-permute-start.12 = (bf16[48,1024]{1,0:T(8,128)(2,1)S(1)}, bf16[48,1024]{1,0:T(8,128)(2,1)}, u32[]{:S(2)}, u32[]{:S(2)}) collective-permute-start(bf16[48,1024]{1,0:T(8,128)(2,1)S(1)} %get-tuple-element.214), channel_id=1, source_target_pairs={{0,3},{1,0},{2,1},{3,2},{4,7},{5,4},{6,5},{7,6},{8,11},{9,8},{10,9... | collective-permute-start | bytes 294920 | tf_op jit(solution)/shard_map/ppermute | solution.py:492
  449.5 9.9 %collective-permute-start.13 = (bf16[144,1024]{1,0:T(8,128)(2,1)S(1)}, bf16[144,1024]{1,0:T(8,128)(2,1)S(1)}, u32[]{:S(2)}, u32[]{:S(2)}) collective-permute-start(bf16[144,1024]{1,0:T(8,128)(2,1)S(1)} %get-tuple-element.219), channel_id=1, source_target_pairs={{0,8},{4,12},{8,0},{12,4},{16,24},{20,28},{24,16},{28,20},{1,9},{5... | collective-permute-start | bytes 884744 | tf_op jit(solution)/shard_map/ppermute | solution.py:653
  450.8 13.8 %collective-permute-start.14 = (bf16[144,1024]{1,0:T(8,128)(2,1)S(1)}, bf16[144,1024]{1,0:T(8,128)(2,1)S(1)}, u32[]{:S(2)}, u32[]{:S(2)}) collective-permute-start(bf16[144,1024]{1,0:T(8,128)(2,1)S(1)} %get-tuple-element.219), channel_id=1, source_target_pairs={{0,16},{4,20},{8,24},{12,28},{16,0},{20,4},{24,8},{28,12},{1,17},{... | collective-permute-start | bytes 884744 | tf_op jit(solution)/shard_map/ppermute | solution.py:653
  452.2 12.3 %collective-permute-start.15 = (bf16[144,1024]{1,0:T(8,128)(2,1)S(1)}, bf16[144,1024]{1,0:T(8,128)(2,1)S(1)}, u32[]{:S(2)}, u32[]{:S(2)}) collective-permute-start(bf16[144,1024]{1,0:T(8,128)(2,1)S(1)} %get-tuple-element.219), channel_id=1, source_target_pairs={{0,24},{4,28},{8,16},{12,20},{16,8},{20,12},{24,0},{28,4},{1,25},{... | collective-permute-start | bytes 884744 | tf_op jit(solution)/shard_map/ppermute | solution.py:653
  453.0 36.6 %collective-permute-start.17 = (bf16[4,256,1024]{2,1,0:T(8,128)(2,1)}, bf16[4,256,1024]{2,1,0:T(8,128)(2,1)}, u32[]{:S(2)}, u32[]{:S(2)}) collective-permute-start(bf16[4,256,1024]{2,1,0:T(8,128)(2,1)} %all-to-all-done.8), channel_id=1, source_target_pairs={{0,4},{4,0},{8,12},{12,8},{16,20},{20,16},{24,28},{28,24},{1,5},{5... | collective-permute-start | bytes 6291464 | tf_op jit(solution)/shard_map/ppermute | solution.py:526
  465.3 13.7 %collective-permute-start.16 = (bf16[4,144,1024]{2,1,0:T(8,128)(2,1)S(1)}, bf16[4,144,1024]{2,1,0:T(8,128)(2,1)S(1)}, u32[]{:S(2)}, u32[]{:S(2)}) collective-permute-start(bf16[4,144,1024]{2,1,0:T(8,128)(2,1)S(1)} %bitcast.221), channel_id=1, source_target_pairs={{0,4},{4,0},{8,12},{12,8},{16,20},{20,16},{24,28},{28,24},{1,5},{5... | collective-permute-start | bytes 3538952 | tf_op jit(solution)/shard_map/ppermute | solution.py:526
  (41 other events, 374.7 us)
Sparse Core Ops, SparseCore 0:
  32.3 47.0 all-gather.3
  244.9 45.0 reduce-scatter.5
  292.9 49.7 reduce-scatter.3
  345.2 48.1 all-gather.5
  396.1 48.4 reduce-scatter.7
  453.2 45.0 all-gather.7
